TPU v7x, 32 devices: a whole 2x2x4 slice. The times are simulated.
32 devices in a mesh: region: 2 (over x), grid: 16 (over z, y, core).
Axes of the slice: x: 2, y: 2, z: 4, core: 2. Of those that a mesh axis runs over, the one named last changes fastest.
Arguments:
- radar_subimages: bfloat16 [768, 4, 2, 128, 128], P(('region', 'grid')), parts along dimension 0, may hold values from -25 to 25, as said below
- owning_sector: int32 [768, 1], P(('region', 'grid')), parts along dimension 0, may hold values from 0 to 15; in each aligned block of 24 rows (0 to 23, 24 to 47, ...) at most 2 rows name the same one
- sector_down_start: int32 [768], P(('region', 'grid')), parts along dimension 0, may hold values from 0 to 3
- sector_across_start: int32 [768], P(('region', 'grid')), parts along dimension 0, may hold values from 0 to 7
Outputs:
- coherence: float32 [3, 4096, 256], P(None, ('region', 'grid')), parts along dimension 1
There are 2 independent parts, one for each index of `region`. A program takes and returns all parts, laid end to end along the dimension named above; each array names one. Nothing has to cross between parts.
Inputs may be any that keep to these rules, and one draw needn't show every extreme that they name: `owning_sector`: the blocks of one device name any one tile at most 2 times, and some device's blocks name a tile exactly 2 times. `radar_subimages`: speckled complex samples whose dates are partly correlated with one another.
All inputs are finite; a program needn't handle non-finite values.
Results may differ from a plain program's by a relative error of at most 0.0003.
Values may be sent and summed in bfloat16 or wider, within the bound.
No kernel may reach another device: no remote copies, remote signals or barrier semaphores. Data moves between devices by JAX's collectives and lax.ppermute only.
A program may use at most 128 MiB of HBM per device.

v0:
```python
import functools

import jax
import jax.numpy as jnp
from jax import lax
from jax.experimental import pallas as pl
from jax.experimental.pallas import tpu as pltpu
from jax.sharding import PartitionSpec as P


TILE_TALL_PARTS = 4
TILE_WIDE_PARTS = 8
EPSILON = 1e-06
LANES = 128
CHUNKS = (2, 1, 1)


def spans(dates):
    out = []
    for size in CHUNKS:
        out.append((sum(s for _, s in out), size))
    if sum(CHUNKS) != dates:
        out = [(d, 1) for d in range(dates)]
    return out


def strip_of(device, group):
    if group % 4:
        return device
    column, side, core = device // 4, (device // 2) % 2, device % 2
    return side * (group // 2) + 2 * (column + side * (group // 4 - 1 - 2 * column)) + core


def device_at(group):
    places = [strip_of(d, group) for d in range(group)]
    return [places.index(s) for s in range(group)]


def cut_kernel(strip_ref, cells_ref, *refs, tagged):
    tag_ref, outs = (refs[0], refs[1:]) if tagged else (None, refs)
    for m, out in enumerate(outs):
        held, span, planes, _, rows, side = cells_ref.shape
        count = held * span * planes
        out[:count] = cells_ref[:, :, :, strip_ref[m]].reshape(count, rows, side)
        if tagged:
            out[count] = tag_ref[...]


def cut(strips, cells, tag, begin, span):
    held, _, planes, group, rows, side = cells.shape
    tagged = tag is not None
    piece = (held * span * planes + tagged, rows, side)
    cells_spec = pl.BlockSpec(
        (held, pl.Element(span), planes, group, rows, side), lambda i, strips: (0, begin, 0, 0, 0, 0)
    )
    if begin % span == 0:
        cells_spec = pl.BlockSpec(
            (held, span, planes, group, rows, side), lambda i, strips: (0, begin // span, 0, 0, 0, 0)
        )
    return pl.pallas_call(
        functools.partial(cut_kernel, tagged=tagged),
        out_shape=[jax.ShapeDtypeStruct(piece, cells.dtype)] * group,
        grid_spec=pltpu.PrefetchScalarGridSpec(
            num_scalar_prefetch=1,
            grid=(1,),
            in_specs=[cells_spec] + [pl.BlockSpec((rows, side), lambda i, strips: (0, 0))] * tagged,
            out_specs=[pl.BlockSpec(piece, lambda i, strips: (0, 0, 0))] * group,
        ),
        name="cut",
    )(strips, cells, *([tag] if tagged else []))


def step_kernel(strip_ref, place_ref, share_ref, *refs, group, held, span, first, last):
    pieces, window_ref, refs = refs[:group], refs[group], refs[group + 1 :]
    if not first:
        before_ref, refs = refs[0], refs[1:]
    kept = [] if last else [refs[0]]
    refs = refs if last else refs[1:]
    own_ref, up_ref, down_ref, sums_ref = refs[:4]
    refs = refs[4:]
    fresh = span if last else span - 1
    comps = list(refs[:fresh]) + kept
    if not first:
        old_ref, sem = refs[fresh:]
        fetch = pltpu.make_async_copy(before_ref, old_ref, sem)
        fetch.start()
    slots, planes, rows, side = comps[0].shape
    wide = window_ref.shape[0] // side
    lines = slots // wide
    strip = strip_ref[0]
    for comp in comps:
        comp[...] = jnp.zeros(comp.shape, jnp.float32)
    for m, piece in enumerate(pieces):

        def add(k, carry, m=m, piece=piece):
            place = place_ref[m * held + k]
            share = share_ref[m * held + k]
            for d, comp in enumerate(comps):
                for q in range(planes):
                    comp[place, q] += piece[(k * span + d) * planes + q].astype(jnp.float32) * share
            return carry

        lax.fori_loop(0, held, add, 0, unroll=4)
    if not first:
        fetch.wait()
        comps = [old_ref] + comps
    step = min(lines, 16)
    window = window_ref[...]

    def row_of(comp, q, at):
        parts = [comp[pl.ds(c * lines + at, step), q].reshape(step * rows, side) for c in range(wide)]
        return jnp.concatenate(parts, axis=1)

    def emit(index, field, at):
        high = field.astype(jnp.bfloat16)
        low = (field - high.astype(jnp.float32)).astype(jnp.bfloat16)
        total = jnp.dot(high, window, preferred_element_type=jnp.float32)
        total += jnp.dot(low, window, preferred_element_type=jnp.float32)
        for half in range(sums_ref.shape[1]):
            sums_ref[index, half, pl.ds(at * rows, step * rows), :] = total[:, half * LANES : (half + 1) * LANES]

    for number in range(lines // step):
        at = number * step
        index = 0
        re_old = im_old = None
        for d, comp in enumerate(comps):
            re, im = row_of(comp, 0, at), row_of(comp, 1, at)
            if first or d:
                emit(index, re * re + im * im, at)
                index += 1
            if d:
                emit(index, re_old * re + im_old * im, at)
                emit(index + 1, im_old * re - re_old * im, at)
                index += 2
            re_old, im_old = re, im
    for f in range(sums_ref.shape[0]):
        level = [
            jnp.concatenate(
                [sums_ref[f, half, pl.ds(y, lines, stride=rows), :] for half in range(sums_ref.shape[1])], axis=1
            )
            for y in range(rows)
        ]
        for i in range(rows // 4):
            begin, end = max(0, 4 * i - 1), min(rows, 4 * i + 6)
            own_ref[f, i] = sum(level[begin + 1 : end], level[begin])
        up, down = level[0] + level[1], level[rows - 1]
        line = lax.broadcasted_iota(jnp.int32, up.shape, 0)
        up_next = jnp.where(line == lines - 1, 0.0, pltpu.roll(up, lines - 1, 0))
        down_next = jnp.where(line == 0, 0.0, pltpu.roll(down, 1, 0))
        up_ref[f] = jnp.where(strip == 0, up_next, up)
        down_ref[f] = jnp.where(strip == group - 1, down_next, down)


def chunk_step(strips, places, shares, pieces, window, before, span, last):
    group = len(pieces)
    held = places.shape[0] // group
    _, rows, side = pieces[0].shape
    lines = group * TILE_TALL_PARTS
    out_cols = window.shape[1]
    first = before is None
    fields = 3 * span - 2 * first
    comp = jax.ShapeDtypeStruct((lines * TILE_WIDE_PARTS, 2, rows, side), jnp.float32)
    outs = [] if last else [comp]
    outs += [
        jax.ShapeDtypeStruct((fields, rows // 4, lines, out_cols), jnp.float32),
        jax.ShapeDtypeStruct((fields, lines, out_cols), jnp.float32),
        jax.ShapeDtypeStruct((fields, lines, out_cols), jnp.float32),
    ]
    scratch = [pltpu.VMEM((fields, out_cols // LANES, lines * rows, LANES), jnp.float32)]
    scratch += [pltpu.VMEM(comp.shape, comp.dtype)] * (span if last else span - 1)
    if not first:
        scratch += [pltpu.VMEM(comp.shape, comp.dtype), pltpu.SemaphoreType.DMA(())]
    vmem = pl.BlockSpec(memory_space=pltpu.VMEM)
    result = pl.pallas_call(
        functools.partial(step_kernel, group=group, held=held, span=span, first=first, last=last),
        out_shape=outs,
        grid_spec=pltpu.PrefetchScalarGridSpec(
            num_scalar_prefetch=3,
            grid=(),
            in_specs=[vmem] * (group + 1) + ([] if first else [pl.BlockSpec(memory_space=pl.ANY)]),
            out_specs=[vmem] * len(outs),
            scratch_shapes=scratch,
        ),
        name="chunk_step",
    )(strips, places, shares, *pieces, window, *([] if first else [before]))
    return (None, *result) if last else tuple(result)


def local(radar_subimages, owning_sector, sector_down_start, sector_across_start):
    group = lax.axis_size("grid")
    held, dates, planes, side, _ = radar_subimages.shape
    rows = side // group
    lines = group * TILE_TALL_PARTS
    cols = TILE_WIDE_PARTS * side
    me = lax.axis_index("grid").astype(jnp.int32)
    strips = strip_of(me ^ jnp.arange(group, dtype=jnp.int32), group)
    at = device_at(group)
    line = owning_sector[:, 0] * TILE_TALL_PARTS + sector_down_start
    tag = jnp.zeros((rows, side), radar_subimages.dtype)
    tag = tag.at[0, :held].set(line.astype(tag.dtype)).at[1, :held].set(sector_across_start.astype(tag.dtype))
    col = jnp.arange(cols)[:, None]
    out_col = jnp.arange(cols // 4)[None, :]
    window = ((col >= 4 * out_col - 12) & (col <= 4 * out_col + 15)).astype(jnp.bfloat16)

    cells = radar_subimages.reshape(held, dates, planes, group, rows, side)
    chunks = spans(dates)
    order = sorted(range(1, group), reverse=True)
    arrived = []
    for number, (begin, span) in enumerate(chunks):
        sends = cut(strips, cells, None if number else tag, begin, span)
        pieces = [sends[0]] + [None] * (group - 1)
        for m in order:
            pieces[m] = lax.ppermute(sends[m], "grid", [(i, i ^ m) for i in range(group)])
        arrived.append(pieces)

    tags = jnp.stack([piece[-1, :2, :held] for piece in arrived[0]]).astype(jnp.int32)
    places = (tags[:, 1] * lines + tags[:, 0]).reshape(group * held)
    counts = jnp.sum((places[:, None] == places[None, :]).astype(jnp.int32), axis=1)
    shares = 1.0 / jnp.maximum(counts, 1).astype(jnp.float32)

    comp = None
    power, cross = [], []
    for number, (begin, span) in enumerate(chunks):
        comp, own, up, down = chunk_step(
            strips, places, shares, arrived[number], window, comp, span, number == len(chunks) - 1
        )
        below = lax.ppermute(up, "grid", [(at[s], at[s - 1]) for s in range(group)])
        above = lax.ppermute(down, "grid", [(at[s - 1], at[s]) for s in range(group)])
        own = own.at[:, 0].add(above)
        own = own.at[:, -1].add(below)
        index = 0
        for d in range(begin, begin + span):
            power.append(own[index])
            index += 1
            if d:
                cross.append((own[index], own[index + 1]))
                index += 2
    ready = jnp.stack(
        [
            jnp.sqrt(re**2 + im**2) / jnp.sqrt(power[k] * power[k + 1] + EPSILON)
            for k, (re, im) in enumerate(cross)
        ]
    )
    ready = ready.reshape(dates - 1, -1, group, TILE_TALL_PARTS, cols // 4).transpose(2, 0, 1, 3, 4)
    mine = lax.all_to_all(ready, "grid", split_axis=0, concat_axis=0, tiled=True)
    if group % 4 == 0:
        mine = mine.reshape(group // 4, 2, 2, *mine.shape[1:])
        mine = jnp.concatenate([mine[:, 0], mine[::-1, 1]]).reshape(group, *mine.shape[3:])
    return mine.transpose(1, 3, 0, 2, 4).reshape(dates - 1, TILE_TALL_PARTS * side // 4, cols // 4)


def solution(mesh):
    in_specs = (
        P(("region", "grid"), None, None, None, None),
        P(("region", "grid"), None),
        P(("region", "grid")),
        P(("region", "grid")),
    )
    out_specs = P(None, ("region", "grid"), None)

    return jax.shard_map(local, mesh=mesh, in_specs=in_specs, out_specs=out_specs, check_vma=False)
```

profile of v0, /device:TPU:13, one launch (start us, length us, event | category | flops | bytes accessed | tf_op | source)
XLA Modules:
  0.0 222.3 jit_solution(14094775507155890951)
XLA Ops:
  2.6 4.9 %cut.3 = (bf16[97,8,128]{2,1,0:T(8,128)(2,1)}, bf16[97,8,128]{2,1,0:T(8,128)(2,1)}, bf16[97,8,128]{2,1,0:T(8,128)(2,1)}, bf16[97,8,128]{2,1,0:T(8,128)(2,1)}, bf...) custom-call(s32[16]{0:T(128)} %fusion.24.strip_ref, ...), custom_call_target="tpu_custom_call" | custom-call | tf_op jit(solution)/shard_map/cut/pallas_call | solution.py:60
  11.7 3.6 %cut.4 = (bf16[48,8,128]{2,1,0:T(8,128)(2,1)}, bf16[48,8,128]{2,1,0:T(8,128)(2,1)}, bf16[48,8,128]{2,1,0:T(8,128)(2,1)}, bf16[48,8,128]{2,1,0:T(8,128)(2,1)}, bf...) custom-call(s32[16]{0:T(128)} %fusion.24.strip_ref, ...), custom_call_target="tpu_custom_call" | custom-call | tf_op jit(solution)/shard_map/cut/pallas_call | solution.py:60
  15.4 3.8 %cut.5 = (bf16[48,8,128]{2,1,0:T(8,128)(2,1)}, bf16[48,8,128]{2,1,0:T(8,128)(2,1)}, bf16[48,8,128]{2,1,0:T(8,128)(2,1)}, bf16[48,8,128]{2,1,0:T(8,128)(2,1)}, bf...) custom-call(s32[16]{0:T(128)} %fusion.24.strip_ref, ...), custom_call_target="tpu_custom_call" | custom-call | tf_op jit(solution)/shard_map/cut/pallas_call | solution.py:60
  21.1 2.6 %collective-permute-start.6 = (bf16[97,8,128]{2,1,0:T(8,128)(2,1)S(1)}, bf16[97,8,128]{2,1,0:T(8,128)(2,1)S(1)}, u32[]{:S(2)}, u32[]{:S(2)}) collective-permute-start(bf16[97,8,128]{2,1,0:T(8,128)(2,1)S(1)} %copy-done.34), channel_id=1, source_target_pairs={{0,7},{1,6},{2,5},{3,4},{4,3},{5,2},{6,1},{7,0},{8,15},{9,14},{10,... | collective-permute-start | bytes 595976 | tf_op jit(solution)/shard_map/ppermute | solution.py:213
  23.8 2.4 %collective-permute-start.7 = (bf16[97,8,128]{2,1,0:T(8,128)(2,1)S(1)}, bf16[97,8,128]{2,1,0:T(8,128)(2,1)S(1)}, u32[]{:S(2)}, u32[]{:S(2)}) collective-permute-start(bf16[97,8,128]{2,1,0:T(8,128)(2,1)S(1)} %copy-done.33), channel_id=1, source_target_pairs={{0,8},{1,9},{2,10},{3,11},{4,12},{5,13},{6,14},{7,15},{8,0},{9,1},... | collective-permute-start | bytes 595976 | tf_op jit(solution)/shard_map/ppermute | solution.py:213
  26.6 2.3 %collective-permute-start.9 = (bf16[97,8,128]{2,1,0:T(8,128)(2,1)S(1)}, bf16[97,8,128]{2,1,0:T(8,128)(2,1)S(1)}, u32[]{:S(2)}, u32[]{:S(2)}) collective-permute-start(bf16[97,8,128]{2,1,0:T(8,128)(2,1)S(1)} %copy-done.31), channel_id=1, source_target_pairs={{0,10},{1,11},{2,8},{3,9},{4,14},{5,15},{6,12},{7,13},{8,2},{9,3},... | collective-permute-start | bytes 595976 | tf_op jit(solution)/shard_map/ppermute | solution.py:213
  29.0 7.6 %collective-permute-start.10 = (bf16[97,8,128]{2,1,0:T(8,128)(2,1)}, bf16[97,8,128]{2,1,0:T(8,128)(2,1)S(1)}, u32[]{:S(2)}, u32[]{:S(2)}) collective-permute-start(bf16[97,8,128]{2,1,0:T(8,128)(2,1)} %get-tuple-element.171), channel_id=1, source_target_pairs={{0,11},{1,10},{2,9},{3,8},{4,15},{5,14},{6,13},{7,12},{8,3},{9,2},... | collective-permute-start | bytes 595976 | tf_op jit(solution)/shard_map/ppermute | solution.py:213
  39.1 18.9 %collective-permute-done.8.refs_9_ = bf16[97,8,128]{2,1,0:T(8,128)(2,1)S(1)} collective-permute-done((bf16[97,8,128]{2,1,0:T(8,128)(2,1)S(1)}, bf16[97,8,128]{2,1,0:T(8,128)(2,1)S(1)}, u32[]{:S(2)}, u32[]{:S(2)}) %collective-permute-start.8) | collective-permute-done | bytes 198688 | tf_op jit(solution)/shard_map/ppermute | solution.py:213
  58.0 6.4 %collective-permute-done.9.refs_10_ = bf16[97,8,128]{2,1,0:T(8,128)(2,1)S(1)} collective-permute-done((bf16[97,8,128]{2,1,0:T(8,128)(2,1)S(1)}, bf16[97,8,128]{2,1,0:T(8,128)(2,1)S(1)}, u32[]{:S(2)}, u32[]{:S(2)}) %collective-permute-start.9) | collective-permute-done | bytes 198688 | tf_op jit(solution)/shard_map/ppermute | solution.py:213
  64.8 12.4 %collective-permute-done.10.refs_11_ = bf16[97,8,128]{2,1,0:T(8,128)(2,1)S(1)} collective-permute-done((bf16[97,8,128]{2,1,0:T(8,128)(2,1)}, bf16[97,8,128]{2,1,0:T(8,128)(2,1)S(1)}, u32[]{:S(2)}, u32[]{:S(2)}) %collective-permute-start.10) | collective-permute-done | bytes 198688 | tf_op jit(solution)/shard_map/ppermute | solution.py:213
  78.9 2.6 %collective-permute-done.11.refs_12_ = bf16[97,8,128]{2,1,0:T(8,128)(2,1)S(1)} collective-permute-done((bf16[97,8,128]{2,1,0:T(8,128)(2,1)}, bf16[97,8,128]{2,1,0:T(8,128)(2,1)S(1)}, u32[]{:S(2)}, u32[]{:S(2)}) %collective-permute-start.11) | collective-permute-done | bytes 198688 | tf_op jit(solution)/shard_map/ppermute | solution.py:213
  81.8 4.9 %collective-permute-done.12.refs_13_ = bf16[97,8,128]{2,1,0:T(8,128)(2,1)S(1)} collective-permute-done((bf16[97,8,128]{2,1,0:T(8,128)(2,1)S(1)}, bf16[97,8,128]{2,1,0:T(8,128)(2,1)S(1)}, u32[]{:S(2)}, u32[]{:S(2)}) %collective-permute-start.12) | collective-permute-done | bytes 198688 | tf_op jit(solution)/shard_map/ppermute | solution.py:213
  90.0 7.8 %collective-permute-start.22 = (bf16[48,8,128]{2,1,0:T(8,128)(2,1)}, bf16[48,8,128]{2,1,0:T(8,128)(2,1)S(1)}, u32[]{:S(2)}, u32[]{:S(2)}) collective-permute-start(bf16[48,8,128]{2,1,0:T(8,128)(2,1)} %get-tuple-element.185), channel_id=1, source_target_pairs={{0,6},{1,7},{2,4},{3,5},{4,2},{5,3},{6,0},{7,1},{8,14},{9,15},{10,... | collective-permute-start | bytes 294920 | tf_op jit(solution)/shard_map/ppermute | solution.py:213
  99.4 2.1 collective-permute-start.24
  102.6 2.1 collective-permute-start.26
  104.7 2.5 %collective-permute-start.27 = (bf16[48,8,128]{2,1,0:T(8,128)(2,1)}, bf16[48,8,128]{2,1,0:T(8,128)(2,1)}, u32[]{:S(2)}, u32[]{:S(2)}) collective-permute-start(bf16[48,8,128]{2,1,0:T(8,128)(2,1)} %get-tuple-element.190), channel_id=1, source_target_pairs={{0,11},{1,10},{2,9},{3,8},{4,15},{5,14},{6,13},{7,12},{8,3},{9,2},... | collective-permute-start | bytes 294920 | tf_op jit(solution)/shard_map/ppermute | solution.py:213
  109.0 7.8 %collective-permute-done.25.refs_9_ = bf16[48,8,128]{2,1,0:T(8,128)(2,1)} collective-permute-done((bf16[48,8,128]{2,1,0:T(8,128)(2,1)}, bf16[48,8,128]{2,1,0:T(8,128)(2,1)}, u32[]{:S(2)}, u32[]{:S(2)}) %collective-permute-start.25) | collective-permute-done | bytes 98336 | tf_op jit(solution)/shard_map/ppermute | solution.py:213
  118.9 3.6 %collective-permute-start.31 = (bf16[48,8,128]{2,1,0:T(8,128)(2,1)}, bf16[48,8,128]{2,1,0:T(8,128)(2,1)}, u32[]{:S(2)}, u32[]{:S(2)}) collective-permute-start(bf16[48,8,128]{2,1,0:T(8,128)(2,1)} %get-tuple-element.194), channel_id=1, source_target_pairs={{0,15},{1,14},{2,13},{3,12},{4,11},{5,10},{6,9},{7,8},{8,7},{9,6},... | collective-permute-start | bytes 294920 | tf_op jit(solution)/shard_map/ppermute | solution.py:213
  122.5 4.8 %collective-permute-start.34 = (bf16[48,8,128]{2,1,0:T(8,128)(2,1)}, bf16[48,8,128]{2,1,0:T(8,128)(2,1)}, u32[]{:S(2)}, u32[]{:S(2)}) collective-permute-start(bf16[48,8,128]{2,1,0:T(8,128)(2,1)} %get-tuple-element.200), channel_id=1, source_target_pairs={{0,1},{1,0},{2,3},{3,2},{4,5},{5,4},{6,7},{7,6},{8,9},{9,8},{10,11... | collective-permute-start | bytes 294920 | tf_op jit(solution)/shard_map/ppermute | solution.py:213
  127.5 3.4 %collective-permute-start.35 = (bf16[48,8,128]{2,1,0:T(8,128)(2,1)}, bf16[48,8,128]{2,1,0:T(8,128)(2,1)}, u32[]{:S(2)}, u32[]{:S(2)}) collective-permute-start(bf16[48,8,128]{2,1,0:T(8,128)(2,1)} %get-tuple-element.201), channel_id=1, source_target_pairs={{0,2},{1,3},{2,0},{3,1},{4,6},{5,7},{6,4},{7,5},{8,10},{9,11},{10,... | collective-permute-start | bytes 294920 | tf_op jit(solution)/shard_map/ppermute | solution.py:213
  130.9 2.6 %collective-permute-done.29.refs_13_ = bf16[48,8,128]{2,1,0:T(8,128)(2,1)} collective-permute-done((bf16[48,8,128]{2,1,0:T(8,128)(2,1)}, bf16[48,8,128]{2,1,0:T(8,128)(2,1)}, u32[]{:S(2)}, u32[]{:S(2)}) %collective-permute-start.29) | collective-permute-done | bytes 98336 | tf_op jit(solution)/shard_map/ppermute | solution.py:213
  134.9 2.1 collective-permute-done.31.refs_15_
  143.4 1.9 collective-permute-start.43
  145.3 2.3 %collective-permute-start.44 = (bf16[48,8,128]{2,1,0:T(8,128)(2,1)}, bf16[48,8,128]{2,1,0:T(8,128)(2,1)}, u32[]{:S(2)}, u32[]{:S(2)}) collective-permute-start(bf16[48,8,128]{2,1,0:T(8,128)(2,1)} %get-tuple-element.210), channel_id=1, source_target_pairs={{0,11},{1,10},{2,9},{3,8},{4,15},{5,14},{6,13},{7,12},{8,3},{9,2},... | collective-permute-start | bytes 294920 | tf_op jit(solution)/shard_map/ppermute | solution.py:213
  148.3 9.3 %chunk_step.3 = (f32[512,2,8,128]{3,2,1,0:T(8,128)}, f32[4,2,64,256]{3,2,1,0:T(8,128)}, f32[4,64,256]{2,1,0:T(8,128)}, f32[4,64,256]{2,1,0:T(8,128)}) custom-call(s32[16]{0:T(128)} %fusion.24.strip_ref, s32[384]{0:T(512)} %copy-done.26, f32[384]{0:T(512)} %convert_divide_fusion.share_ref, bf16[97,8,128]{2,1,0:T(8,128)(2,1)} %get-tuple-element.160.refs_0_, ...), custom_call_target="tpu_custom_call" | custom-call | tf_op jit(solution)/shard_map/chunk_step/pallas_call | solution.py:174
  157.7 7.9 %chunk_step.4 = (f32[512,2,8,128]{3,2,1,0:T(8,128)}, f32[3,2,64,256]{3,2,1,0:T(8,128)}, f32[3,64,256]{2,1,0:T(8,128)}, f32[3,64,256]{2,1,0:T(8,128)}) custom-call(s32[16]{0:T(128)} %fusion.24.strip_ref, s32[384]{0:T(512)} %copy-done.26, f32[384]{0:T(512)} %convert_divide_fusion.share_ref, bf16[48,8,128]{2,1,0:T(8,128)(2,1)} %get-tuple-element.179.refs_0_, ...), custom_call_target="tpu_custom_call" | custom-call | tf_op jit(solution)/shard_map/chunk_step/pallas_call | solution.py:174
  171.5 9.7 %collective-permute-done.45.refs_12_ = bf16[48,8,128]{2,1,0:T(8,128)(2,1)S(1)} collective-permute-done((bf16[48,8,128]{2,1,0:T(8,128)(2,1)S(1)}, bf16[48,8,128]{2,1,0:T(8,128)(2,1)S(1)}, u32[]{:S(2)}, u32[]{:S(2)}) %collective-permute-start.45) | collective-permute-done | bytes 98336 | tf_op jit(solution)/shard_map/ppermute | solution.py:213
  182.1 2.0 collective-permute-start.16
  186.7 7.8 %chunk_step.5 = (f32[3,2,64,256]{3,2,1,0:T(8,128)}, f32[3,64,256]{2,1,0:T(8,128)}, f32[3,64,256]{2,1,0:T(8,128)}) custom-call(s32[16]{0:T(128)} %fusion.24.strip_ref, s32[384]{0:T(512)} %copy-done.26, f32[384]{0:T(512)} %convert_divide_fusion.share_ref, bf16[48,8,128]{2,1,0:T(8,128)(2,1)} %get-tuple-element.199.refs_0_, ...), custom_call_target="tpu_custom_call" | custom-call | tf_op jit(solution)/shard_map/chunk_step/pallas_call | solution.py:174
  196.3 2.1 collective-permute-start.50
  199.6 2.3 %collective-permute-done.50 = f32[3,64,256]{2,1,0:T(8,128)S(1)} collective-permute-done((f32[3,64,256]{2,1,0:T(8,128)}, f32[3,64,256]{2,1,0:T(8,128)S(1)}, u32[]{:S(2)}, u32[]{:S(2)}) %collective-permute-start.50) | collective-permute-done | bytes 196640 | tf_op jit(solution)/shard_map/ppermute | solution.py:227
  202.6 18.4 %all_to_all.5 = f32[16,3,2,4,256]{4,3,2,1,0:T(4,128)S(1)} all-to-all(f32[16,3,2,4,256]{4,3,2,1,0:T(4,128)S(1)} %copy_bitcast_fusion), channel_id=1, replica_groups=mesh['region'=2,'grid'=16] {'grid'}, dimensions={0} | all-to-all | bytes 786432 | tf_op jit(solution)/shard_map/all_to_all | solution.py:245
  (206 shorter events, 46.5 us)
Async XLA Ops:
  8.5 15.3 %collective-permute-start.2 = (bf16[97,8,128]{2,1,0:T(8,128)(2,1)}, bf16[97,8,128]{2,1,0:T(8,128)(2,1)S(1)}, u32[]{:S(2)}, u32[]{:S(2)}) collective-permute-start(bf16[97,8,128]{2,1,0:T(8,128)(2,1)} %get-tuple-element.163), channel_id=1, source_target_pairs={{0,3},{1,2},{2,1},{3,0},{4,7},{5,6},{6,5},{7,4},{8,11},{9,10},{10,... | collective-permute-start | bytes 595976 | tf_op jit(solution)/shard_map/ppermute | solution.py:213
  9.9 16.2 %collective-permute-start.3 = (bf16[97,8,128]{2,1,0:T(8,128)(2,1)}, bf16[97,8,128]{2,1,0:T(8,128)(2,1)S(1)}, u32[]{:S(2)}, u32[]{:S(2)}) collective-permute-start(bf16[97,8,128]{2,1,0:T(8,128)(2,1)} %get-tuple-element.164), channel_id=1, source_target_pairs={{0,4},{1,5},{2,6},{3,7},{4,0},{5,1},{6,2},{7,3},{8,12},{9,13},{10,... | collective-permute-start | bytes 595976 | tf_op jit(solution)/shard_map/ppermute | solution.py:213
  10.1 16.5 %collective-permute-start.4 = (bf16[97,8,128]{2,1,0:T(8,128)(2,1)}, bf16[97,8,128]{2,1,0:T(8,128)(2,1)S(1)}, u32[]{:S(2)}, u32[]{:S(2)}) collective-permute-start(bf16[97,8,128]{2,1,0:T(8,128)(2,1)} %get-tuple-element.165), channel_id=1, source_target_pairs={{0,5},{1,4},{2,7},{3,6},{4,1},{5,0},{6,3},{7,2},{8,13},{9,12},{10,... | collective-permute-start | bytes 595976 | tf_op jit(solution)/shard_map/ppermute | solution.py:213
  21.1 15.5 %collective-permute-start.6 = (bf16[97,8,128]{2,1,0:T(8,128)(2,1)S(1)}, bf16[97,8,128]{2,1,0:T(8,128)(2,1)S(1)}, u32[]{:S(2)}, u32[]{:S(2)}) collective-permute-start(bf16[97,8,128]{2,1,0:T(8,128)(2,1)S(1)} %copy-done.34), channel_id=1, source_target_pairs={{0,7},{1,6},{2,5},{3,4},{4,3},{5,2},{6,1},{7,0},{8,15},{9,14},{10,... | collective-permute-start | bytes 595976 | tf_op jit(solution)/shard_map/ppermute | solution.py:213
  23.8 14.1 %collective-permute-start.7 = (bf16[97,8,128]{2,1,0:T(8,128)(2,1)S(1)}, bf16[97,8,128]{2,1,0:T(8,128)(2,1)S(1)}, u32[]{:S(2)}, u32[]{:S(2)}) collective-permute-start(bf16[97,8,128]{2,1,0:T(8,128)(2,1)S(1)} %copy-done.33), channel_id=1, source_target_pairs={{0,8},{1,9},{2,10},{3,11},{4,12},{5,13},{6,14},{7,15},{8,0},{9,1},... | collective-permute-start | bytes 595976 | tf_op jit(solution)/shard_map/ppermute | solution.py:213
  26.2 31.8 %collective-permute-start.8 = (bf16[97,8,128]{2,1,0:T(8,128)(2,1)S(1)}, bf16[97,8,128]{2,1,0:T(8,128)(2,1)S(1)}, u32[]{:S(2)}, u32[]{:S(2)}) collective-permute-start(bf16[97,8,128]{2,1,0:T(8,128)(2,1)S(1)} %copy-done.32), channel_id=1, source_target_pairs={{0,9},{1,8},{2,11},{3,10},{4,13},{5,12},{6,15},{7,14},{8,1},{9,0},... | collective-permute-start | bytes 595976 | tf_op jit(solution)/shard_map/ppermute | solution.py:213
  26.6 37.8 %collective-permute-start.9 = (bf16[97,8,128]{2,1,0:T(8,128)(2,1)S(1)}, bf16[97,8,128]{2,1,0:T(8,128)(2,1)S(1)}, u32[]{:S(2)}, u32[]{:S(2)}) collective-permute-start(bf16[97,8,128]{2,1,0:T(8,128)(2,1)S(1)} %copy-done.31), channel_id=1, source_target_pairs={{0,10},{1,11},{2,8},{3,9},{4,14},{5,15},{6,12},{7,13},{8,2},{9,3},... | collective-permute-start | bytes 595976 | tf_op jit(solution)/shard_map/ppermute | solution.py:213
  29.0 48.3 %collective-permute-start.10 = (bf16[97,8,128]{2,1,0:T(8,128)(2,1)}, bf16[97,8,128]{2,1,0:T(8,128)(2,1)S(1)}, u32[]{:S(2)}, u32[]{:S(2)}) collective-permute-start(bf16[97,8,128]{2,1,0:T(8,128)(2,1)} %get-tuple-element.171), channel_id=1, source_target_pairs={{0,11},{1,10},{2,9},{3,8},{4,15},{5,14},{6,13},{7,12},{8,3},{9,2},... | collective-permute-start | bytes 595976 | tf_op jit(solution)/shard_map/ppermute | solution.py:213
  36.6 44.9 %collective-permute-start.11 = (bf16[97,8,128]{2,1,0:T(8,128)(2,1)}, bf16[97,8,128]{2,1,0:T(8,128)(2,1)S(1)}, u32[]{:S(2)}, u32[]{:S(2)}) collective-permute-start(bf16[97,8,128]{2,1,0:T(8,128)(2,1)} %get-tuple-element.172), channel_id=1, source_target_pairs={{0,12},{1,13},{2,14},{3,15},{4,8},{5,9},{6,10},{7,11},{8,4},{9,5},... | collective-permute-start | bytes 595976 | tf_op jit(solution)/shard_map/ppermute | solution.py:213
  37.9 48.8 %collective-permute-start.12 = (bf16[97,8,128]{2,1,0:T(8,128)(2,1)S(1)}, bf16[97,8,128]{2,1,0:T(8,128)(2,1)S(1)}, u32[]{:S(2)}, u32[]{:S(2)}) collective-permute-start(bf16[97,8,128]{2,1,0:T(8,128)(2,1)S(1)} %copy-done.30), channel_id=1, source_target_pairs={{0,13},{1,12},{2,15},{3,14},{4,9},{5,8},{6,11},{7,10},{8,5},{9,4},... | collective-permute-start | bytes 595976 | tf_op jit(solution)/shard_map/ppermute | solution.py:213
  58.0 32.0 %collective-permute-start.13 = (bf16[97,8,128]{2,1,0:T(8,128)(2,1)}, bf16[97,8,128]{2,1,0:T(8,128)(2,1)S(1)}, u32[]{:S(2)}, u32[]{:S(2)}) collective-permute-start(bf16[97,8,128]{2,1,0:T(8,128)(2,1)} %get-tuple-element.174), channel_id=1, source_target_pairs={{0,14},{1,15},{2,12},{3,13},{4,10},{5,11},{6,8},{7,9},{8,6},{9,7},... | collective-permute-start | bytes 595976 | tf_op jit(solution)/shard_map/ppermute | solution.py:213
  64.4 40.3 %collective-permute-start.14 = (bf16[97,8,128]{2,1,0:T(8,128)(2,1)}, bf16[97,8,128]{2,1,0:T(8,128)(2,1)S(1)}, u32[]{:S(2)}, u32[]{:S(2)}) collective-permute-start(bf16[97,8,128]{2,1,0:T(8,128)(2,1)} %get-tuple-element.175), channel_id=1, source_target_pairs={{0,15},{1,14},{2,13},{3,12},{4,11},{5,10},{6,9},{7,8},{8,7},{9,6},... | collective-permute-start | bytes 595976 | tf_op jit(solution)/shard_map/ppermute | solution.py:213
  101.4 15.3 %collective-permute-start.25 = (bf16[48,8,128]{2,1,0:T(8,128)(2,1)}, bf16[48,8,128]{2,1,0:T(8,128)(2,1)}, u32[]{:S(2)}, u32[]{:S(2)}) collective-permute-start(bf16[48,8,128]{2,1,0:T(8,128)(2,1)} %get-tuple-element.188), channel_id=1, source_target_pairs={{0,9},{1,8},{2,11},{3,10},{4,13},{5,12},{6,15},{7,14},{8,1},{9,0},... | collective-permute-start | bytes 294920 | tf_op jit(solution)/shard_map/ppermute | solution.py:213
  102.6 16.3 %collective-permute-start.26 = (bf16[48,8,128]{2,1,0:T(8,128)(2,1)}, bf16[48,8,128]{2,1,0:T(8,128)(2,1)}, u32[]{:S(2)}, u32[]{:S(2)}) collective-permute-start(bf16[48,8,128]{2,1,0:T(8,128)(2,1)} %get-tuple-element.189), channel_id=1, source_target_pairs={{0,10},{1,11},{2,8},{3,9},{4,14},{5,15},{6,12},{7,13},{8,2},{9,3},... | collective-permute-start | bytes 294920 | tf_op jit(solution)/shard_map/ppermute | solution.py:213
  104.7 17.8 %collective-permute-start.27 = (bf16[48,8,128]{2,1,0:T(8,128)(2,1)}, bf16[48,8,128]{2,1,0:T(8,128)(2,1)}, u32[]{:S(2)}, u32[]{:S(2)}) collective-permute-start(bf16[48,8,128]{2,1,0:T(8,128)(2,1)} %get-tuple-element.190), channel_id=1, source_target_pairs={{0,11},{1,10},{2,9},{3,8},{4,15},{5,14},{6,13},{7,12},{8,3},{9,2},... | collective-permute-start | bytes 294920 | tf_op jit(solution)/shard_map/ppermute | solution.py:213
  107.2 20.3 %collective-permute-start.28 = (bf16[48,8,128]{2,1,0:T(8,128)(2,1)}, bf16[48,8,128]{2,1,0:T(8,128)(2,1)}, u32[]{:S(2)}, u32[]{:S(2)}) collective-permute-start(bf16[48,8,128]{2,1,0:T(8,128)(2,1)} %get-tuple-element.191), channel_id=1, source_target_pairs={{0,12},{1,13},{2,14},{3,15},{4,8},{5,9},{6,10},{7,11},{8,4},{9,5},... | collective-permute-start | bytes 294920 | tf_op jit(solution)/shard_map/ppermute | solution.py:213
  109.0 24.5 %collective-permute-start.29 = (bf16[48,8,128]{2,1,0:T(8,128)(2,1)}, bf16[48,8,128]{2,1,0:T(8,128)(2,1)}, u32[]{:S(2)}, u32[]{:S(2)}) collective-permute-start(bf16[48,8,128]{2,1,0:T(8,128)(2,1)} %get-tuple-element.192), channel_id=1, source_target_pairs={{0,13},{1,12},{2,15},{3,14},{4,9},{5,8},{6,11},{7,10},{8,5},{9,4},... | collective-permute-start | bytes 294920 | tf_op jit(solution)/shard_map/ppermute | solution.py:213
  116.8 18.1 %collective-permute-start.30 = (bf16[48,8,128]{2,1,0:T(8,128)(2,1)}, bf16[48,8,128]{2,1,0:T(8,128)(2,1)}, u32[]{:S(2)}, u32[]{:S(2)}) collective-permute-start(bf16[48,8,128]{2,1,0:T(8,128)(2,1)} %get-tuple-element.193), channel_id=1, source_target_pairs={{0,14},{1,15},{2,12},{3,13},{4,10},{5,11},{6,8},{7,9},{8,6},{9,7},... | collective-permute-start | bytes 294920 | tf_op jit(solution)/shard_map/ppermute | solution.py:213
  118.9 18.1 %collective-permute-start.31 = (bf16[48,8,128]{2,1,0:T(8,128)(2,1)}, bf16[48,8,128]{2,1,0:T(8,128)(2,1)}, u32[]{:S(2)}, u32[]{:S(2)}) collective-permute-start(bf16[48,8,128]{2,1,0:T(8,128)(2,1)} %get-tuple-element.194), channel_id=1, source_target_pairs={{0,15},{1,14},{2,13},{3,12},{4,11},{5,10},{6,9},{7,8},{8,7},{9,6},... | collective-permute-start | bytes 294920 | tf_op jit(solution)/shard_map/ppermute | solution.py:213
  122.5 14.5 %collective-permute-start.34 = (bf16[48,8,128]{2,1,0:T(8,128)(2,1)}, bf16[48,8,128]{2,1,0:T(8,128)(2,1)}, u32[]{:S(2)}, u32[]{:S(2)}) collective-permute-start(bf16[48,8,128]{2,1,0:T(8,128)(2,1)} %get-tuple-element.200), channel_id=1, source_target_pairs={{0,1},{1,0},{2,3},{3,2},{4,5},{5,4},{6,7},{7,6},{8,9},{9,8},{10,11... | collective-permute-start | bytes 294920 | tf_op jit(solution)/shard_map/ppermute | solution.py:213
  138.7 26.9 %collective-permute-start.40 = (bf16[48,8,128]{2,1,0:T(8,128)(2,1)}, bf16[48,8,128]{2,1,0:T(8,128)(2,1)}, u32[]{:S(2)}, u32[]{:S(2)}) collective-permute-start(bf16[48,8,128]{2,1,0:T(8,128)(2,1)} %get-tuple-element.206), channel_id=1, source_target_pairs={{0,7},{1,6},{2,5},{3,4},{4,3},{5,2},{6,1},{7,0},{8,15},{9,14},{10,... | collective-permute-start | bytes 294920 | tf_op jit(solution)/shard_map/ppermute | solution.py:213
  140.9 25.2 %collective-permute-start.41 = (bf16[48,8,128]{2,1,0:T(8,128)(2,1)}, bf16[48,8,128]{2,1,0:T(8,128)(2,1)}, u32[]{:S(2)}, u32[]{:S(2)}) collective-permute-start(bf16[48,8,128]{2,1,0:T(8,128)(2,1)} %get-tuple-element.207), channel_id=1, source_target_pairs={{0,8},{1,9},{2,10},{3,11},{4,12},{5,13},{6,14},{7,15},{8,0},{9,1},... | collective-permute-start | bytes 294920 | tf_op jit(solution)/shard_map/ppermute | solution.py:213
  142.7 24.0 %collective-permute-start.42 = (bf16[48,8,128]{2,1,0:T(8,128)(2,1)}, bf16[48,8,128]{2,1,0:T(8,128)(2,1)}, u32[]{:S(2)}, u32[]{:S(2)}) collective-permute-start(bf16[48,8,128]{2,1,0:T(8,128)(2,1)} %get-tuple-element.208), channel_id=1, source_target_pairs={{0,9},{1,8},{2,11},{3,10},{4,13},{5,12},{6,15},{7,14},{8,1},{9,0},... | collective-permute-start | bytes 294920 | tf_op jit(solution)/shard_map/ppermute | solution.py:213
  143.4 24.5 %collective-permute-start.43 = (bf16[48,8,128]{2,1,0:T(8,128)(2,1)}, bf16[48,8,128]{2,1,0:T(8,128)(2,1)}, u32[]{:S(2)}, u32[]{:S(2)}) collective-permute-start(bf16[48,8,128]{2,1,0:T(8,128)(2,1)} %get-tuple-element.209), channel_id=1, source_target_pairs={{0,10},{1,11},{2,8},{3,9},{4,14},{5,15},{6,12},{7,13},{8,2},{9,3},... | collective-permute-start | bytes 294920 | tf_op jit(solution)/shard_map/ppermute | solution.py:213
  145.3 24.5 %collective-permute-start.44 = (bf16[48,8,128]{2,1,0:T(8,128)(2,1)}, bf16[48,8,128]{2,1,0:T(8,128)(2,1)}, u32[]{:S(2)}, u32[]{:S(2)}) collective-permute-start(bf16[48,8,128]{2,1,0:T(8,128)(2,1)} %get-tuple-element.210), channel_id=1, source_target_pairs={{0,11},{1,10},{2,9},{3,8},{4,15},{5,14},{6,13},{7,12},{8,3},{9,2},... | collective-permute-start | bytes 294920 | tf_op jit(solution)/shard_map/ppermute | solution.py:213
  165.7 30.6 %collective-permute-start.32 = (f32[3,64,256]{2,1,0:T(8,128)}, f32[3,64,256]{2,1,0:T(8,128)S(1)}, u32[]{:S(2)}, u32[]{:S(2)}) collective-permute-start(f32[3,64,256]{2,1,0:T(8,128)} %get-tuple-element.197), channel_id=1, source_target_pairs={{3,0},{0,1},{1,4},{4,5},{5,8},{8,9},{9,12},{12,13},{13,14},{14,15}... | collective-permute-start | bytes 589832 | tf_op jit(solution)/shard_map/ppermute | solution.py:228
  166.1 15.2 %collective-permute-start.45 = (bf16[48,8,128]{2,1,0:T(8,128)(2,1)S(1)}, bf16[48,8,128]{2,1,0:T(8,128)(2,1)S(1)}, u32[]{:S(2)}, u32[]{:S(2)}) collective-permute-start(bf16[48,8,128]{2,1,0:T(8,128)(2,1)S(1)} %copy-done.39), channel_id=1, source_target_pairs={{0,12},{1,13},{2,14},{3,15},{4,8},{5,9},{6,10},{7,11},{8,4},{9,5},... | collective-permute-start | bytes 294920 | tf_op jit(solution)/shard_map/ppermute | solution.py:213
  166.7 15.4 %collective-permute-start.46 = (bf16[48,8,128]{2,1,0:T(8,128)(2,1)S(1)}, bf16[48,8,128]{2,1,0:T(8,128)(2,1)S(1)}, u32[]{:S(2)}, u32[]{:S(2)}) collective-permute-start(bf16[48,8,128]{2,1,0:T(8,128)(2,1)S(1)} %copy-done.38), channel_id=1, source_target_pairs={{0,13},{1,12},{2,15},{3,14},{4,9},{5,8},{6,11},{7,10},{8,5},{9,4},... | collective-permute-start | bytes 294920 | tf_op jit(solution)/shard_map/ppermute | solution.py:213
  167.9 17.1 %collective-permute-start.47 = (bf16[48,8,128]{2,1,0:T(8,128)(2,1)S(1)}, bf16[48,8,128]{2,1,0:T(8,128)(2,1)S(1)}, u32[]{:S(2)}, u32[]{:S(2)}) collective-permute-start(bf16[48,8,128]{2,1,0:T(8,128)(2,1)S(1)} %copy-done.37), channel_id=1, source_target_pairs={{0,14},{1,15},{2,12},{3,13},{4,10},{5,11},{6,8},{7,9},{8,6},{9,7},... | collective-permute-start | bytes 294920 | tf_op jit(solution)/shard_map/ppermute | solution.py:213
  169.8 16.3 %collective-permute-start.48 = (bf16[48,8,128]{2,1,0:T(8,128)(2,1)S(1)}, bf16[48,8,128]{2,1,0:T(8,128)(2,1)S(1)}, u32[]{:S(2)}, u32[]{:S(2)}) collective-permute-start(bf16[48,8,128]{2,1,0:T(8,128)(2,1)S(1)} %copy-done.36), channel_id=1, source_target_pairs={{0,15},{1,14},{2,13},{3,12},{4,11},{5,10},{6,9},{7,8},{8,7},{9,6},... | collective-permute-start | bytes 294920 | tf_op jit(solution)/shard_map/ppermute | solution.py:213
  181.3 20.7 %collective-permute-start.15 = (f32[4,64,256]{2,1,0:T(8,128)S(1)}, f32[4,64,256]{2,1,0:T(8,128)S(1)}, u32[]{:S(2)}, u32[]{:S(2)}) collective-permute-start(f32[4,64,256]{2,1,0:T(8,128)S(1)} %copy-done.29), channel_id=1, source_target_pairs={{3,0},{0,1},{1,4},{4,5},{5,8},{8,9},{9,12},{12,13},{13,14},{14,15}... | collective-permute-start | bytes 786440 | tf_op jit(solution)/shard_map/ppermute | solution.py:228
  182.1 20.0 %collective-permute-start.16 = (f32[4,64,256]{2,1,0:T(8,128)S(1)}, f32[4,64,256]{2,1,0:T(8,128)S(1)}, u32[]{:S(2)}, u32[]{:S(2)}) collective-permute-start(f32[4,64,256]{2,1,0:T(8,128)S(1)} %copy-done.28), channel_id=1, source_target_pairs={{0,3},{1,0},{4,1},{5,4},{8,5},{9,8},{12,9},{13,12},{14,13},{15,14}... | collective-permute-start | bytes 786440 | tf_op jit(solution)/shard_map/ppermute | solution.py:227
  (60 other events, 2201.9 us)
where the time goes:
time: 225 us; the launch traced here: 222 us
  starting transfers between devices  78.7 us (35%)
  waiting for transfers between devices  76.9 us (34%)
  Pallas kernels  37.4 us (17%)
  blocking collectives  18.4 us (8%)
  local copies, waits for them, and re-layouts  5.85 us (3%)
  other arithmetic  4.43 us (2%)
    ppermute x45, waiting for transfers between devices, local(): lax.ppermute(sends[m], 'grid', [(i, i ^ m) for i in range(group)])  73.6 us
    ppermute x45, starting transfers between devices, local(): lax.ppermute(sends[m], 'grid', [(i, i ^ m) for i in range(group)])  73.4 us
    pallas_call x3, Pallas kernels, chunk_step(): pl.pallas_call(functools.partial(step_kernel, group=group, held=held, spa...  25 us
    all_to_all x1, blocking collectives, local(): lax.all_to_all(ready, 'grid', split_axis=0, concat_axis=0, tiled=True)  18.4 us
    pallas_call x3, Pallas kernels, cut(): pl.pallas_call(functools.partial(cut_kernel, tagged=tagged), out_shape=[j...  12.4 us
  transfers between devices with their start and end apart: 51, of which 18 were waited for; matrix products, arithmetic and copies ran while one was open for 2% of the time, Pallas kernels for 15%

commit v1 on v0

--- a/solution.py
+++ b/solution.py
@@ -37,10 +37,14 @@
 
 
 def cut_kernel(strip_ref, cells_ref, *refs, tagged):
-    tag_ref, outs = (refs[0], refs[1:]) if tagged else (None, refs)
+    held, span, planes, group, rows, side = cells_ref.shape
+    count = held * span * planes
+    if tagged:
+        tag_ref, out = refs
+        outs = [out.at[m] for m in range(group)]
+    else:
+        outs = refs
     for m, out in enumerate(outs):
-        held, span, planes, _, rows, side = cells_ref.shape
-        count = held * span * planes
         out[:count] = cells_ref[:, :, :, strip_ref[m]].reshape(count, rows, side)
         if tagged:
             out[count] = tag_ref[...]
@@ -57,21 +61,28 @@
         cells_spec = pl.BlockSpec(
             (held, span, planes, group, rows, side), lambda i, strips: (0, begin // span, 0, 0, 0, 0)
         )
+    if tagged:
+        pieces, specs = [(group, *piece)], [pl.BlockSpec((group, *piece), lambda i, strips: (0, 0, 0, 0))]
+    else:
+        pieces, specs = [piece] * group, [pl.BlockSpec(piece, lambda i, strips: (0, 0, 0))] * group
     return pl.pallas_call(
         functools.partial(cut_kernel, tagged=tagged),
-        out_shape=[jax.ShapeDtypeStruct(piece, cells.dtype)] * group,
+        out_shape=[jax.ShapeDtypeStruct(p, cells.dtype) for p in pieces],
         grid_spec=pltpu.PrefetchScalarGridSpec(
             num_scalar_prefetch=1,
             grid=(1,),
             in_specs=[cells_spec] + [pl.BlockSpec((rows, side), lambda i, strips: (0, 0))] * tagged,
-            out_specs=[pl.BlockSpec(piece, lambda i, strips: (0, 0, 0))] * group,
+            out_specs=specs,
         ),
         name="cut",
     )(strips, cells, *([tag] if tagged else []))
 
 
 def step_kernel(strip_ref, place_ref, share_ref, *refs, group, held, span, first, last):
-    pieces, window_ref, refs = refs[:group], refs[group], refs[group + 1 :]
+    if first:
+        pieces, window_ref, refs = [refs[0].at[m] for m in range(group)], refs[1], refs[2:]
+    else:
+        pieces, window_ref, refs = refs[:group], refs[group], refs[group + 1 :]
     if not first:
         before_ref, refs = refs[0], refs[1:]
     kept = [] if last else [refs[0]]
@@ -152,9 +163,8 @@
 
 
 def chunk_step(strips, places, shares, pieces, window, before, span, last):
-    group = len(pieces)
-    held = places.shape[0] // group
-    _, rows, side = pieces[0].shape
+    group, held = strips.shape[0], places.shape[0] // strips.shape[0]
+    rows, side = pieces[0].shape[-2:]
     lines = group * TILE_TALL_PARTS
     out_cols = window.shape[1]
     first = before is None
@@ -177,7 +187,7 @@
         grid_spec=pltpu.PrefetchScalarGridSpec(
             num_scalar_prefetch=3,
             grid=(),
-            in_specs=[vmem] * (group + 1) + ([] if first else [pl.BlockSpec(memory_space=pl.ANY)]),
+            in_specs=[vmem] * (len(pieces) + 1) + ([] if first else [pl.BlockSpec(memory_space=pl.ANY)]),
             out_specs=[vmem] * len(outs),
             scratch_shapes=scratch,
         ),
@@ -193,7 +203,8 @@
     lines = group * TILE_TALL_PARTS
     cols = TILE_WIDE_PARTS * side
     me = lax.axis_index("grid").astype(jnp.int32)
-    strips = strip_of(me ^ jnp.arange(group, dtype=jnp.int32), group)
+    devices = jnp.arange(group, dtype=jnp.int32)
+    strips = strip_of(me ^ devices, group)
     at = device_at(group)
     line = owning_sector[:, 0] * TILE_TALL_PARTS + sector_down_start
     tag = jnp.zeros((rows, side), radar_subimages.dtype)
@@ -207,22 +218,28 @@
     order = sorted(range(1, group), reverse=True)
     arrived = []
     for number, (begin, span) in enumerate(chunks):
-        sends = cut(strips, cells, None if number else tag, begin, span)
+        if number == 0:
+            (sends,) = cut(strip_of(devices, group), cells, tag, begin, span)
+            arrived.append([lax.all_to_all(sends, "grid", split_axis=0, concat_axis=0, tiled=True)])
+            continue
+        sends = cut(strips, cells, None, begin, span)
         pieces = [sends[0]] + [None] * (group - 1)
         for m in order:
             pieces[m] = lax.ppermute(sends[m], "grid", [(i, i ^ m) for i in range(group)])
         arrived.append(pieces)
 
-    tags = jnp.stack([piece[-1, :2, :held] for piece in arrived[0]]).astype(jnp.int32)
-    places = (tags[:, 1] * lines + tags[:, 0]).reshape(group * held)
+    tags = arrived[0][0][:, -1, :2, :held].astype(jnp.int32)
+    places = tags[:, 1] * lines + tags[:, 0]
+    places = places.reshape(group * held)
     counts = jnp.sum((places[:, None] == places[None, :]).astype(jnp.int32), axis=1)
     shares = 1.0 / jnp.maximum(counts, 1).astype(jnp.float32)
+    tables = [(places, shares), tuple(t.reshape(group, held)[me ^ devices].reshape(group * held) for t in (places, shares))]
 
     comp = None
     power, cross = [], []
     for number, (begin, span) in enumerate(chunks):
         comp, own, up, down = chunk_step(
-            strips, places, shares, arrived[number], window, comp, span, number == len(chunks) - 1
+            strips, *tables[number > 0], arrived[number], window, comp, span, number == len(chunks) - 1
         )
         below = lax.ppermute(up, "grid", [(at[s], at[s - 1]) for s in range(group)])
         above = lax.ppermute(down, "grid", [(at[s - 1], at[s]) for s in range(group)])

time: 225 us -> 209 us (0.929)
  starting transfers between devices: 78.7 us -> 48.6 us
  waiting for transfers between devices: 76.9 us -> 89.5 us
    all_to_all x0 -> x1, waiting for transfers between devices: none -> 46.7 us  [local(): lax.all_to_all(sends, 'grid', split_axis=0, concat_axis=0, tiled=True)]
    ppermute x45 -> x30, starting transfers between devices: 73.4 us -> 37 us  [local(): lax.ppermute(sends[m], 'grid', [(i, i ^ m) for i in range(group)])]
    ppermute x45 -> x30, waiting for transfers between devices: 73.6 us -> 37.9 us  [local(): lax.ppermute(sends[m], 'grid', [(i, i ^ m) for i in range(group)])]
    all_to_all x0 -> x1, starting transfers between devices: none -> 6.52 us  [local(): lax.all_to_all(sends, 'grid', split_axis=0, concat_axis=0, tiled=True)]
  transfers between devices with their start and end apart: 51 -> 37, of which waited for: 18 -> 15; matrix products, arithmetic and copies ran while one was open for 2% -> 4% of each run, Pallas kernels for 15% -> 16%
where the time goes in v1:
time: 209 us; the launch traced here: 206 us
  waiting for transfers between devices  89.5 us (43%)
  starting transfers between devices  48.6 us (23%)
  Pallas kernels  37.2 us (18%)
  blocking collectives  16.8 us (8%)
  local copies, waits for them, and re-layouts  8.05 us (4%)
  other arithmetic  5.14 us (2%)
    all_to_all x1, waiting for transfers between devices, local(): lax.all_to_all(sends, 'grid', split_axis=0, concat_axis=0, tiled=True)  46.7 us
    ppermute x30, waiting for transfers between devices, local(): lax.ppermute(sends[m], 'grid', [(i, i ^ m) for i in range(group)])  37.9 us
    ppermute x30, starting transfers between devices, local(): lax.ppermute(sends[m], 'grid', [(i, i ^ m) for i in range(group)])  37 us
    pallas_call x3, Pallas kernels, chunk_step(): pl.pallas_call(functools.partial(step_kernel, group=group, held=held, spa...  24.9 us
    all_to_all x1, blocking collectives, local(): lax.all_to_all(ready, 'grid', split_axis=0, concat_axis=0, tiled=True)  16.8 us
    pallas_call x3, Pallas kernels, cut(): pl.pallas_call(functools.partial(cut_kernel, tagged=tagged), out_shape=[j...  12.3 us
    all_to_all x1, starting transfers between devices, local(): lax.all_to_all(sends, 'grid', split_axis=0, concat_axis=0, tiled=True)  6.52 us
  transfers between devices with their start and end apart: 37, of which 15 were waited for; matrix products, arithmetic and copies ran while one was open for 4% of the time, Pallas kernels for 16%

profile of v1, /device:TPU:13, one launch (start us, length us, event | category | flops | bytes accessed | tf_op | source)
XLA Modules:
  0.0 205.7 jit_solution(238738358376557043)
XLA Ops:
  2.6 5.0 %cut.3 = bf16[16,97,8,128]{3,2,1,0:T(8,128)(2,1)} custom-call(s32[16]{0:T(128)} %fusion.24.strip_ref, bf16[24,4,2,16,8,128]{5,4,3,2,1,0:T(8,128)(2,1)} %bitcast.56, bf16[8,128]{1,0:T(8,128)(2,1)} %copy-done.11), custom_call_target="tpu_custom_call" | custom-call | tf_op jit(solution)/shard_map/cut/pallas_call | solution.py:68
  7.7 6.5 %all-to-all-start = ((bf16[16,97,8,128]{3,2,1,0:T(8,128)(2,1)}), bf16[16,97,8,128]{3,2,1,0:T(8,128)(2,1)S(1)}, u32[]{:S(2)}, u32[]{:S(2)}) async-start(bf16[16,97,8,128]{3,2,1,0:T(8,128)(2,1)} %cut.3), calls=%async_computation | async-start | bytes 6356992 | tf_op jit(solution)/shard_map/all_to_all | solution.py:223
  14.8 3.6 %cut.4 = (bf16[48,8,128]{2,1,0:T(8,128)(2,1)}, bf16[48,8,128]{2,1,0:T(8,128)(2,1)}, bf16[48,8,128]{2,1,0:T(8,128)(2,1)}, bf16[48,8,128]{2,1,0:T(8,128)(2,1)}, bf...) custom-call(s32[16]{0:T(128)} %fusion.25.strip_ref, ...), custom_call_target="tpu_custom_call" | custom-call | tf_op jit(solution)/shard_map/cut/pallas_call | solution.py:68
  19.0 1.5 collective-permute-start.4
  20.8 1.5 collective-permute-start.6
  22.3 3.7 %cut.5 = (bf16[48,8,128]{2,1,0:T(8,128)(2,1)}, bf16[48,8,128]{2,1,0:T(8,128)(2,1)}, bf16[48,8,128]{2,1,0:T(8,128)(2,1)}, bf16[48,8,128]{2,1,0:T(8,128)(2,1)}, bf...) custom-call(s32[16]{0:T(128)} %fusion.25.strip_ref, ...), custom_call_target="tpu_custom_call" | custom-call | tf_op jit(solution)/shard_map/cut/pallas_call | solution.py:68
  27.1 3.2 %collective-permute-done.3.refs_2_ = bf16[48,8,128]{2,1,0:T(8,128)(2,1)S(1)} collective-permute-done((bf16[48,8,128]{2,1,0:T(8,128)(2,1)}, bf16[48,8,128]{2,1,0:T(8,128)(2,1)S(1)}, u32[]{:S(2)}, u32[]{:S(2)}) %collective-permute-start.3) | collective-permute-done | bytes 98336 | tf_op jit(solution)/shard_map/ppermute | solution.py:228
  30.3 7.8 %collective-permute-start.8 = (bf16[48,8,128]{2,1,0:T(8,128)(2,1)}, bf16[48,8,128]{2,1,0:T(8,128)(2,1)}, u32[]{:S(2)}, u32[]{:S(2)}) collective-permute-start(bf16[48,8,128]{2,1,0:T(8,128)(2,1)} %get-tuple-element.154), channel_id=1, source_target_pairs={{0,7},{1,6},{2,5},{3,4},{4,3},{5,2},{6,1},{7,0},{8,15},{9,14},{10,... | collective-permute-start | bytes 294920 | tf_op jit(solution)/shard_map/ppermute | solution.py:228
  38.1 46.7 %all-to-all-done.refs_0_ = bf16[16,97,8,128]{3,2,1,0:T(8,128)(2,1)S(1)} async-done(((bf16[16,97,8,128]{3,2,1,0:T(8,128)(2,1)}), bf16[16,97,8,128]{3,2,1,0:T(8,128)(2,1)S(1)}, u32[]{:S(2)}, u32[]{:S(2)}) %all-to-all-start) | async-done | bytes 3178528 | tf_op jit(solution)/shard_map/all_to_all | solution.py:223
  84.8 3.1 %collective-permute-start.9 = (bf16[48,8,128]{2,1,0:T(8,128)(2,1)}, bf16[48,8,128]{2,1,0:T(8,128)(2,1)}, u32[]{:S(2)}, u32[]{:S(2)}) collective-permute-start(bf16[48,8,128]{2,1,0:T(8,128)(2,1)} %get-tuple-element.155), channel_id=1, source_target_pairs={{0,8},{1,9},{2,10},{3,11},{4,12},{5,13},{6,14},{7,15},{8,0},{9,1},... | collective-permute-start | bytes 294920 | tf_op jit(solution)/shard_map/ppermute | solution.py:228
  88.0 3.8 %collective-permute-start.12 = (bf16[48,8,128]{2,1,0:T(8,128)(2,1)}, bf16[48,8,128]{2,1,0:T(8,128)(2,1)}, u32[]{:S(2)}, u32[]{:S(2)}) collective-permute-start(bf16[48,8,128]{2,1,0:T(8,128)(2,1)} %get-tuple-element.158), channel_id=1, source_target_pairs={{0,11},{1,10},{2,9},{3,8},{4,15},{5,14},{6,13},{7,12},{8,3},{9,2},... | collective-permute-start | bytes 294920 | tf_op jit(solution)/shard_map/ppermute | solution.py:228
  93.1 2.9 %collective-permute-done.9.refs_8_ = bf16[48,8,128]{2,1,0:T(8,128)(2,1)} collective-permute-done((bf16[48,8,128]{2,1,0:T(8,128)(2,1)}, bf16[48,8,128]{2,1,0:T(8,128)(2,1)}, u32[]{:S(2)}, u32[]{:S(2)}) %collective-permute-start.9) | collective-permute-done | bytes 98336 | tf_op jit(solution)/shard_map/ppermute | solution.py:228
  96.0 4.3 %collective-permute-done.10.refs_9_ = bf16[48,8,128]{2,1,0:T(8,128)(2,1)} collective-permute-done((bf16[48,8,128]{2,1,0:T(8,128)(2,1)}, bf16[48,8,128]{2,1,0:T(8,128)(2,1)}, u32[]{:S(2)}, u32[]{:S(2)}) %collective-permute-start.10) | collective-permute-done | bytes 98336 | tf_op jit(solution)/shard_map/ppermute | solution.py:228
  100.5 2.0 collective-permute-done.11.refs_10_
  102.5 3.2 %collective-permute-start.16 = (bf16[48,8,128]{2,1,0:T(8,128)(2,1)}, bf16[48,8,128]{2,1,0:T(8,128)(2,1)}, u32[]{:S(2)}, u32[]{:S(2)}) collective-permute-start(bf16[48,8,128]{2,1,0:T(8,128)(2,1)} %get-tuple-element.162), channel_id=1, source_target_pairs={{0,15},{1,14},{2,13},{3,12},{4,11},{5,10},{6,9},{7,8},{8,7},{9,6},... | collective-permute-start | bytes 294920 | tf_op jit(solution)/shard_map/ppermute | solution.py:228
  105.7 3.1 %collective-permute-done.12.refs_11_ = bf16[48,8,128]{2,1,0:T(8,128)(2,1)} collective-permute-done((bf16[48,8,128]{2,1,0:T(8,128)(2,1)}, bf16[48,8,128]{2,1,0:T(8,128)(2,1)}, u32[]{:S(2)}, u32[]{:S(2)}) %collective-permute-start.12) | collective-permute-done | bytes 98336 | tf_op jit(solution)/shard_map/ppermute | solution.py:228
  109.3 4.7 %collective-permute-done.13.refs_12_ = bf16[48,8,128]{2,1,0:T(8,128)(2,1)} collective-permute-done((bf16[48,8,128]{2,1,0:T(8,128)(2,1)}, bf16[48,8,128]{2,1,0:T(8,128)(2,1)}, u32[]{:S(2)}, u32[]{:S(2)}) %collective-permute-start.13) | collective-permute-done | bytes 98336 | tf_op jit(solution)/shard_map/ppermute | solution.py:228
  116.6 1.5 collective-permute-done.15.refs_14_
  118.1 2.7 %collective-permute-done.16.refs_15_ = bf16[48,8,128]{2,1,0:T(8,128)(2,1)} collective-permute-done((bf16[48,8,128]{2,1,0:T(8,128)(2,1)}, bf16[48,8,128]{2,1,0:T(8,128)(2,1)}, u32[]{:S(2)}, u32[]{:S(2)}) %collective-permute-start.16) | collective-permute-done | bytes 98336 | tf_op jit(solution)/shard_map/ppermute | solution.py:228
  124.9 2.5 %collective-permute-start.26 = (bf16[48,8,128]{2,1,0:T(8,128)(2,1)}, bf16[48,8,128]{2,1,0:T(8,128)(2,1)}, u32[]{:S(2)}, u32[]{:S(2)}) collective-permute-start(bf16[48,8,128]{2,1,0:T(8,128)(2,1)} %get-tuple-element.175), channel_id=1, source_target_pairs={{0,8},{1,9},{2,10},{3,11},{4,12},{5,13},{6,14},{7,15},{8,0},{9,1},... | collective-permute-start | bytes 294920 | tf_op jit(solution)/shard_map/ppermute | solution.py:228
  128.5 2.1 %collective-permute-start.28 = (bf16[48,8,128]{2,1,0:T(8,128)(2,1)}, bf16[48,8,128]{2,1,0:T(8,128)(2,1)}, u32[]{:S(2)}, u32[]{:S(2)}) collective-permute-start(bf16[48,8,128]{2,1,0:T(8,128)(2,1)} %get-tuple-element.177), channel_id=1, source_target_pairs={{0,10},{1,11},{2,8},{3,9},{4,14},{5,15},{6,12},{7,13},{8,2},{9,3},... | collective-permute-start | bytes 294920 | tf_op jit(solution)/shard_map/ppermute | solution.py:228
  132.7 9.2 %chunk_step.3 = (f32[512,2,8,128]{3,2,1,0:T(8,128)}, f32[4,2,64,256]{3,2,1,0:T(8,128)}, f32[4,64,256]{2,1,0:T(8,128)}, f32[4,64,256]{2,1,0:T(8,128)}) custom-call(s32[16]{0:T(128)} %fusion.25.strip_ref, s32[384]{0:T(512)} %copy-done.9, f32[384]{0:T(512)} %copy-done.10, bf16[16,97,8,128]{3,2,1,0:T(8,128)(2,1)} %copy-done, ...), custom_call_target="tpu_custom_call" | custom-call | tf_op jit(solution)/shard_map/chunk_step/pallas_call | solution.py:184
  141.9 7.9 %chunk_step.4 = (f32[512,2,8,128]{3,2,1,0:T(8,128)}, f32[3,2,64,256]{3,2,1,0:T(8,128)}, f32[3,64,256]{2,1,0:T(8,128)}, f32[3,64,256]{2,1,0:T(8,128)}) custom-call(s32[16]{0:T(128)} %fusion.25.strip_ref, s32[384]{0:T(512)} %reshape.359.place_ref, f32[384]{0:T(512)} %reshape.360.share_ref, bf16[48,8,128]{2,1,0:T(8,128)(2,1)} %get-tuple-element.147.refs_0_, ...), custom_call_target="tpu_custom_call" | custom-call | tf_op jit(solution)/shard_map/chunk_step/pallas_call | solution.py:184
  150.8 1.3 collective-permute-start.30
  153.7 1.5 collective-permute-start.33
  156.3 11.5 %collective-permute-done.30.refs_12_ = bf16[48,8,128]{2,1,0:T(8,128)(2,1)S(1)} collective-permute-done((bf16[48,8,128]{2,1,0:T(8,128)(2,1)S(1)}, bf16[48,8,128]{2,1,0:T(8,128)(2,1)S(1)}, u32[]{:S(2)}, u32[]{:S(2)}) %collective-permute-start.30) | collective-permute-done | bytes 98336 | tf_op jit(solution)/shard_map/ppermute | solution.py:228
  167.9 2.5 %collective-permute-start.1 = (f32[4,64,256]{2,1,0:T(8,128)S(1)}, f32[4,64,256]{2,1,0:T(8,128)S(1)}, u32[]{:S(2)}, u32[]{:S(2)}) collective-permute-start(f32[4,64,256]{2,1,0:T(8,128)S(1)} %copy-done.12), channel_id=1, source_target_pairs={{0,3},{1,0},{4,1},{5,4},{8,5},{9,8},{12,9},{13,12},{14,13},{15,14}... | collective-permute-start | bytes 786440 | tf_op jit(solution)/shard_map/ppermute | solution.py:244
  171.5 7.8 %chunk_step.5 = (f32[3,2,64,256]{3,2,1,0:T(8,128)}, f32[3,64,256]{2,1,0:T(8,128)}, f32[3,64,256]{2,1,0:T(8,128)}) custom-call(s32[16]{0:T(128)} %fusion.25.strip_ref, s32[384]{0:T(512)} %reshape.359.place_ref, f32[384]{0:T(512)} %reshape.360.share_ref, bf16[48,8,128]{2,1,0:T(8,128)(2,1)} %get-tuple-element.167.refs_0_, ...), custom_call_target="tpu_custom_call" | custom-call | tf_op jit(solution)/shard_map/chunk_step/pallas_call | solution.py:184
  180.3 1.3 collective-permute-start.34
  181.9 2.6 %collective-permute-done.34 = f32[3,64,256]{2,1,0:T(8,128)S(1)} collective-permute-done((f32[3,64,256]{2,1,0:T(8,128)}, f32[3,64,256]{2,1,0:T(8,128)S(1)}, u32[]{:S(2)}, u32[]{:S(2)}) %collective-permute-start.34) | collective-permute-done | bytes 196640 | tf_op jit(solution)/shard_map/ppermute | solution.py:245
  184.6 2.3 %collective-permute-done.35 = f32[3,64,256]{2,1,0:T(8,128)S(1)} collective-permute-done((f32[3,64,256]{2,1,0:T(8,128)}, f32[3,64,256]{2,1,0:T(8,128)S(1)}, u32[]{:S(2)}, u32[]{:S(2)}) %collective-permute-start.35) | collective-permute-done | bytes 196640 | tf_op jit(solution)/shard_map/ppermute | solution.py:244
  187.5 16.8 %all_to_all.10 = f32[16,3,2,4,256]{4,3,2,1,0:T(4,128)S(1)} all-to-all(f32[16,3,2,4,256]{4,3,2,1,0:T(4,128)S(1)} %copy_bitcast_fusion), channel_id=1, replica_groups=mesh['region'=2,'grid'=16] {'grid'}, dimensions={0} | all-to-all | bytes 786432 | tf_op jit(solution)/shard_map/all_to_all | solution.py:262
  (125 shorter events, 25.2 us)
Async XLA Ops:
  7.7 77.1 %all-to-all-start = ((bf16[16,97,8,128]{3,2,1,0:T(8,128)(2,1)}), bf16[16,97,8,128]{3,2,1,0:T(8,128)(2,1)S(1)}, u32[]{:S(2)}, u32[]{:S(2)}) async-start(bf16[16,97,8,128]{3,2,1,0:T(8,128)(2,1)} %cut.3), calls=%async_computation | async-start | bytes 6356992 | tf_op jit(solution)/shard_map/all_to_all | solution.py:223
  18.8 11.6 %collective-permute-start.3 = (bf16[48,8,128]{2,1,0:T(8,128)(2,1)}, bf16[48,8,128]{2,1,0:T(8,128)(2,1)S(1)}, u32[]{:S(2)}, u32[]{:S(2)}) collective-permute-start(bf16[48,8,128]{2,1,0:T(8,128)(2,1)} %get-tuple-element.149), channel_id=1, source_target_pairs={{0,2},{1,3},{2,0},{3,1},{4,6},{5,7},{6,4},{7,5},{8,10},{9,11},{10,... | collective-permute-start | bytes 294920 | tf_op jit(solution)/shard_map/ppermute | solution.py:228
  19.0 65.7 %collective-permute-start.4 = (bf16[48,8,128]{2,1,0:T(8,128)(2,1)}, bf16[48,8,128]{2,1,0:T(8,128)(2,1)S(1)}, u32[]{:S(2)}, u32[]{:S(2)}) collective-permute-start(bf16[48,8,128]{2,1,0:T(8,128)(2,1)} %get-tuple-element.150), channel_id=1, source_target_pairs={{0,3},{1,2},{2,1},{3,0},{4,7},{5,6},{6,5},{7,4},{8,11},{9,10},{10,... | collective-permute-start | bytes 294920 | tf_op jit(solution)/shard_map/ppermute | solution.py:228
  20.5 67.4 %collective-permute-start.5 = (bf16[48,8,128]{2,1,0:T(8,128)(2,1)}, bf16[48,8,128]{2,1,0:T(8,128)(2,1)}, u32[]{:S(2)}, u32[]{:S(2)}) collective-permute-start(bf16[48,8,128]{2,1,0:T(8,128)(2,1)} %get-tuple-element.151), channel_id=1, source_target_pairs={{0,4},{1,5},{2,6},{3,7},{4,0},{5,1},{6,2},{7,3},{8,12},{9,13},{10,... | collective-permute-start | bytes 294920 | tf_op jit(solution)/shard_map/ppermute | solution.py:228
  20.8 67.2 %collective-permute-start.6 = (bf16[48,8,128]{2,1,0:T(8,128)(2,1)}, bf16[48,8,128]{2,1,0:T(8,128)(2,1)}, u32[]{:S(2)}, u32[]{:S(2)}) collective-permute-start(bf16[48,8,128]{2,1,0:T(8,128)(2,1)} %get-tuple-element.152), channel_id=1, source_target_pairs={{0,5},{1,4},{2,7},{3,6},{4,1},{5,0},{6,3},{7,2},{8,13},{9,12},{10,... | collective-permute-start | bytes 294920 | tf_op jit(solution)/shard_map/ppermute | solution.py:228
  27.0 60.9 %collective-permute-start.7 = (bf16[48,8,128]{2,1,0:T(8,128)(2,1)}, bf16[48,8,128]{2,1,0:T(8,128)(2,1)}, u32[]{:S(2)}, u32[]{:S(2)}) collective-permute-start(bf16[48,8,128]{2,1,0:T(8,128)(2,1)} %get-tuple-element.153), channel_id=1, source_target_pairs={{0,6},{1,7},{2,4},{3,5},{4,2},{5,3},{6,0},{7,1},{8,14},{9,15},{10,... | collective-permute-start | bytes 294920 | tf_op jit(solution)/shard_map/ppermute | solution.py:228
  30.3 61.5 %collective-permute-start.8 = (bf16[48,8,128]{2,1,0:T(8,128)(2,1)}, bf16[48,8,128]{2,1,0:T(8,128)(2,1)}, u32[]{:S(2)}, u32[]{:S(2)}) collective-permute-start(bf16[48,8,128]{2,1,0:T(8,128)(2,1)} %get-tuple-element.154), channel_id=1, source_target_pairs={{0,7},{1,6},{2,5},{3,4},{4,3},{5,2},{6,1},{7,0},{8,15},{9,14},{10,... | collective-permute-start | bytes 294920 | tf_op jit(solution)/shard_map/ppermute | solution.py:228
  84.8 11.2 %collective-permute-start.9 = (bf16[48,8,128]{2,1,0:T(8,128)(2,1)}, bf16[48,8,128]{2,1,0:T(8,128)(2,1)}, u32[]{:S(2)}, u32[]{:S(2)}) collective-permute-start(bf16[48,8,128]{2,1,0:T(8,128)(2,1)} %get-tuple-element.155), channel_id=1, source_target_pairs={{0,8},{1,9},{2,10},{3,11},{4,12},{5,13},{6,14},{7,15},{8,0},{9,1},... | collective-permute-start | bytes 294920 | tf_op jit(solution)/shard_map/ppermute | solution.py:228
  87.9 12.5 %collective-permute-start.10 = (bf16[48,8,128]{2,1,0:T(8,128)(2,1)}, bf16[48,8,128]{2,1,0:T(8,128)(2,1)}, u32[]{:S(2)}, u32[]{:S(2)}) collective-permute-start(bf16[48,8,128]{2,1,0:T(8,128)(2,1)} %get-tuple-element.156), channel_id=1, source_target_pairs={{0,9},{1,8},{2,11},{3,10},{4,13},{5,12},{6,15},{7,14},{8,1},{9,0},... | collective-permute-start | bytes 294920 | tf_op jit(solution)/shard_map/ppermute | solution.py:228
  88.0 14.5 %collective-permute-start.11 = (bf16[48,8,128]{2,1,0:T(8,128)(2,1)}, bf16[48,8,128]{2,1,0:T(8,128)(2,1)}, u32[]{:S(2)}, u32[]{:S(2)}) collective-permute-start(bf16[48,8,128]{2,1,0:T(8,128)(2,1)} %get-tuple-element.157), channel_id=1, source_target_pairs={{0,10},{1,11},{2,8},{3,9},{4,14},{5,15},{6,12},{7,13},{8,2},{9,3},... | collective-permute-start | bytes 294920 | tf_op jit(solution)/shard_map/ppermute | solution.py:228
  88.0 20.8 %collective-permute-start.12 = (bf16[48,8,128]{2,1,0:T(8,128)(2,1)}, bf16[48,8,128]{2,1,0:T(8,128)(2,1)}, u32[]{:S(2)}, u32[]{:S(2)}) collective-permute-start(bf16[48,8,128]{2,1,0:T(8,128)(2,1)} %get-tuple-element.158), channel_id=1, source_target_pairs={{0,11},{1,10},{2,9},{3,8},{4,15},{5,14},{6,13},{7,12},{8,3},{9,2},... | collective-permute-start | bytes 294920 | tf_op jit(solution)/shard_map/ppermute | solution.py:228
  91.8 22.2 %collective-permute-start.13 = (bf16[48,8,128]{2,1,0:T(8,128)(2,1)}, bf16[48,8,128]{2,1,0:T(8,128)(2,1)}, u32[]{:S(2)}, u32[]{:S(2)}) collective-permute-start(bf16[48,8,128]{2,1,0:T(8,128)(2,1)} %get-tuple-element.159), channel_id=1, source_target_pairs={{0,12},{1,13},{2,14},{3,15},{4,8},{5,9},{6,10},{7,11},{8,4},{9,5},... | collective-permute-start | bytes 294920 | tf_op jit(solution)/shard_map/ppermute | solution.py:228
  96.0 19.3 %collective-permute-start.14 = (bf16[48,8,128]{2,1,0:T(8,128)(2,1)}, bf16[48,8,128]{2,1,0:T(8,128)(2,1)}, u32[]{:S(2)}, u32[]{:S(2)}) collective-permute-start(bf16[48,8,128]{2,1,0:T(8,128)(2,1)} %get-tuple-element.160), channel_id=1, source_target_pairs={{0,13},{1,12},{2,15},{3,14},{4,9},{5,8},{6,11},{7,10},{8,5},{9,4},... | collective-permute-start | bytes 294920 | tf_op jit(solution)/shard_map/ppermute | solution.py:228
  100.4 17.7 %collective-permute-start.15 = (bf16[48,8,128]{2,1,0:T(8,128)(2,1)}, bf16[48,8,128]{2,1,0:T(8,128)(2,1)}, u32[]{:S(2)}, u32[]{:S(2)}) collective-permute-start(bf16[48,8,128]{2,1,0:T(8,128)(2,1)} %get-tuple-element.161), channel_id=1, source_target_pairs={{0,14},{1,15},{2,12},{3,13},{4,10},{5,11},{6,8},{7,9},{8,6},{9,7},... | collective-permute-start | bytes 294920 | tf_op jit(solution)/shard_map/ppermute | solution.py:228
  102.5 18.4 %collective-permute-start.16 = (bf16[48,8,128]{2,1,0:T(8,128)(2,1)}, bf16[48,8,128]{2,1,0:T(8,128)(2,1)}, u32[]{:S(2)}, u32[]{:S(2)}) collective-permute-start(bf16[48,8,128]{2,1,0:T(8,128)(2,1)} %get-tuple-element.162), channel_id=1, source_target_pairs={{0,15},{1,14},{2,13},{3,12},{4,11},{5,10},{6,9},{7,8},{8,7},{9,6},... | collective-permute-start | bytes 294920 | tf_op jit(solution)/shard_map/ppermute | solution.py:228
  108.8 13.1 %collective-permute-start.19 = (bf16[48,8,128]{2,1,0:T(8,128)(2,1)}, bf16[48,8,128]{2,1,0:T(8,128)(2,1)}, u32[]{:S(2)}, u32[]{:S(2)}) collective-permute-start(bf16[48,8,128]{2,1,0:T(8,128)(2,1)} %get-tuple-element.168), channel_id=1, source_target_pairs={{0,1},{1,0},{2,3},{3,2},{4,5},{5,4},{6,7},{7,6},{8,9},{9,8},{10,11... | collective-permute-start | bytes 294920 | tf_op jit(solution)/shard_map/ppermute | solution.py:228
  114.0 8.8 %collective-permute-start.20 = (bf16[48,8,128]{2,1,0:T(8,128)(2,1)}, bf16[48,8,128]{2,1,0:T(8,128)(2,1)}, u32[]{:S(2)}, u32[]{:S(2)}) collective-permute-start(bf16[48,8,128]{2,1,0:T(8,128)(2,1)} %get-tuple-element.169), channel_id=1, source_target_pairs={{0,2},{1,3},{2,0},{3,1},{4,6},{5,7},{6,4},{7,5},{8,10},{9,11},{10,... | collective-permute-start | bytes 294920 | tf_op jit(solution)/shard_map/ppermute | solution.py:228
  115.3 9.7 %collective-permute-start.21 = (bf16[48,8,128]{2,1,0:T(8,128)(2,1)}, bf16[48,8,128]{2,1,0:T(8,128)(2,1)}, u32[]{:S(2)}, u32[]{:S(2)}) collective-permute-start(bf16[48,8,128]{2,1,0:T(8,128)(2,1)} %get-tuple-element.170), channel_id=1, source_target_pairs={{0,3},{1,2},{2,1},{3,0},{4,7},{5,6},{6,5},{7,4},{8,11},{9,10},{10,... | collective-permute-start | bytes 294920 | tf_op jit(solution)/shard_map/ppermute | solution.py:228
  118.1 9.3 %collective-permute-start.22 = (bf16[48,8,128]{2,1,0:T(8,128)(2,1)}, bf16[48,8,128]{2,1,0:T(8,128)(2,1)}, u32[]{:S(2)}, u32[]{:S(2)}) collective-permute-start(bf16[48,8,128]{2,1,0:T(8,128)(2,1)} %get-tuple-element.171), channel_id=1, source_target_pairs={{0,4},{1,5},{2,6},{3,7},{4,0},{5,1},{6,2},{7,3},{8,12},{9,13},{10,... | collective-permute-start | bytes 294920 | tf_op jit(solution)/shard_map/ppermute | solution.py:228
  122.8 27.1 %collective-permute-start.25 = (bf16[48,8,128]{2,1,0:T(8,128)(2,1)}, bf16[48,8,128]{2,1,0:T(8,128)(2,1)}, u32[]{:S(2)}, u32[]{:S(2)}) collective-permute-start(bf16[48,8,128]{2,1,0:T(8,128)(2,1)} %get-tuple-element.174), channel_id=1, source_target_pairs={{0,7},{1,6},{2,5},{3,4},{4,3},{5,2},{6,1},{7,0},{8,15},{9,14},{10,... | collective-permute-start | bytes 294920 | tf_op jit(solution)/shard_map/ppermute | solution.py:228
  124.9 25.9 %collective-permute-start.26 = (bf16[48,8,128]{2,1,0:T(8,128)(2,1)}, bf16[48,8,128]{2,1,0:T(8,128)(2,1)}, u32[]{:S(2)}, u32[]{:S(2)}) collective-permute-start(bf16[48,8,128]{2,1,0:T(8,128)(2,1)} %get-tuple-element.175), channel_id=1, source_target_pairs={{0,8},{1,9},{2,10},{3,11},{4,12},{5,13},{6,14},{7,15},{8,0},{9,1},... | collective-permute-start | bytes 294920 | tf_op jit(solution)/shard_map/ppermute | solution.py:228
  127.4 24.7 %collective-permute-start.27 = (bf16[48,8,128]{2,1,0:T(8,128)(2,1)}, bf16[48,8,128]{2,1,0:T(8,128)(2,1)}, u32[]{:S(2)}, u32[]{:S(2)}) collective-permute-start(bf16[48,8,128]{2,1,0:T(8,128)(2,1)} %get-tuple-element.176), channel_id=1, source_target_pairs={{0,9},{1,8},{2,11},{3,10},{4,13},{5,12},{6,15},{7,14},{8,1},{9,0},... | collective-permute-start | bytes 294920 | tf_op jit(solution)/shard_map/ppermute | solution.py:228
  128.5 24.0 %collective-permute-start.28 = (bf16[48,8,128]{2,1,0:T(8,128)(2,1)}, bf16[48,8,128]{2,1,0:T(8,128)(2,1)}, u32[]{:S(2)}, u32[]{:S(2)}) collective-permute-start(bf16[48,8,128]{2,1,0:T(8,128)(2,1)} %get-tuple-element.177), channel_id=1, source_target_pairs={{0,10},{1,11},{2,8},{3,9},{4,14},{5,15},{6,12},{7,13},{8,2},{9,3},... | collective-permute-start | bytes 294920 | tf_op jit(solution)/shard_map/ppermute | solution.py:228
  130.6 23.1 %collective-permute-start.29 = (bf16[48,8,128]{2,1,0:T(8,128)(2,1)}, bf16[48,8,128]{2,1,0:T(8,128)(2,1)}, u32[]{:S(2)}, u32[]{:S(2)}) collective-permute-start(bf16[48,8,128]{2,1,0:T(8,128)(2,1)} %get-tuple-element.178), channel_id=1, source_target_pairs={{0,11},{1,10},{2,9},{3,8},{4,15},{5,14},{6,13},{7,12},{8,3},{9,2},... | collective-permute-start | bytes 294920 | tf_op jit(solution)/shard_map/ppermute | solution.py:228
  149.9 31.7 %collective-permute-start.17 = (f32[3,64,256]{2,1,0:T(8,128)}, f32[3,64,256]{2,1,0:T(8,128)S(1)}, u32[]{:S(2)}, u32[]{:S(2)}) collective-permute-start(f32[3,64,256]{2,1,0:T(8,128)} %get-tuple-element.165), channel_id=1, source_target_pairs={{3,0},{0,1},{1,4},{4,5},{5,8},{8,9},{9,12},{12,13},{13,14},{14,15}... | collective-permute-start | bytes 589832 | tf_op jit(solution)/shard_map/ppermute | solution.py:245
  150.8 17.0 %collective-permute-start.30 = (bf16[48,8,128]{2,1,0:T(8,128)(2,1)S(1)}, bf16[48,8,128]{2,1,0:T(8,128)(2,1)S(1)}, u32[]{:S(2)}, u32[]{:S(2)}) collective-permute-start(bf16[48,8,128]{2,1,0:T(8,128)(2,1)S(1)} %copy-done.17), channel_id=1, source_target_pairs={{0,12},{1,13},{2,14},{3,15},{4,8},{5,9},{6,10},{7,11},{8,4},{9,5},... | collective-permute-start | bytes 294920 | tf_op jit(solution)/shard_map/ppermute | solution.py:228
  152.1 15.7 %collective-permute-start.31 = (bf16[48,8,128]{2,1,0:T(8,128)(2,1)S(1)}, bf16[48,8,128]{2,1,0:T(8,128)(2,1)S(1)}, u32[]{:S(2)}, u32[]{:S(2)}) collective-permute-start(bf16[48,8,128]{2,1,0:T(8,128)(2,1)S(1)} %copy-done.16), channel_id=1, source_target_pairs={{0,13},{1,12},{2,15},{3,14},{4,9},{5,8},{6,11},{7,10},{8,5},{9,4},... | collective-permute-start | bytes 294920 | tf_op jit(solution)/shard_map/ppermute | solution.py:228
  152.5 17.9 %collective-permute-start.32 = (bf16[48,8,128]{2,1,0:T(8,128)(2,1)S(1)}, bf16[48,8,128]{2,1,0:T(8,128)(2,1)S(1)}, u32[]{:S(2)}, u32[]{:S(2)}) collective-permute-start(bf16[48,8,128]{2,1,0:T(8,128)(2,1)S(1)} %copy-done.15), channel_id=1, source_target_pairs={{0,14},{1,15},{2,12},{3,13},{4,10},{5,11},{6,8},{7,9},{8,6},{9,7},... | collective-permute-start | bytes 294920 | tf_op jit(solution)/shard_map/ppermute | solution.py:228
  153.7 17.1 %collective-permute-start.33 = (bf16[48,8,128]{2,1,0:T(8,128)(2,1)S(1)}, bf16[48,8,128]{2,1,0:T(8,128)(2,1)S(1)}, u32[]{:S(2)}, u32[]{:S(2)}) collective-permute-start(bf16[48,8,128]{2,1,0:T(8,128)(2,1)S(1)} %copy-done.14), channel_id=1, source_target_pairs={{0,15},{1,14},{2,13},{3,12},{4,11},{5,10},{6,9},{7,8},{8,7},{9,6},... | collective-permute-start | bytes 294920 | tf_op jit(solution)/shard_map/ppermute | solution.py:228
  167.8 19.1 %collective-permute-start = (f32[4,64,256]{2,1,0:T(8,128)S(1)}, f32[4,64,256]{2,1,0:T(8,128)S(1)}, u32[]{:S(2)}, u32[]{:S(2)}) collective-permute-start(f32[4,64,256]{2,1,0:T(8,128)S(1)} %copy-done.13), channel_id=1, source_target_pairs={{3,0},{0,1},{1,4},{4,5},{5,8},{8,9},{9,12},{12,13},{13,14},{14,15}... | collective-permute-start | bytes 786440 | tf_op jit(solution)/shard_map/ppermute | solution.py:245
  167.9 19.2 %collective-permute-start.1 = (f32[4,64,256]{2,1,0:T(8,128)S(1)}, f32[4,64,256]{2,1,0:T(8,128)S(1)}, u32[]{:S(2)}, u32[]{:S(2)}) collective-permute-start(f32[4,64,256]{2,1,0:T(8,128)S(1)} %copy-done.12), channel_id=1, source_target_pairs={{0,3},{1,0},{4,1},{5,4},{8,5},{9,8},{12,9},{13,12},{14,13},{15,14}... | collective-permute-start | bytes 786440 | tf_op jit(solution)/shard_map/ppermute | solution.py:244
  170.3 11.5 %collective-permute-start.18 = (f32[3,64,256]{2,1,0:T(8,128)}, f32[3,64,256]{2,1,0:T(8,128)S(1)}, u32[]{:S(2)}, u32[]{:S(2)}) collective-permute-start(f32[3,64,256]{2,1,0:T(8,128)} %get-tuple-element.166), channel_id=1, source_target_pairs={{0,3},{1,0},{4,1},{5,4},{8,5},{9,8},{12,9},{13,12},{14,13},{15,14}... | collective-permute-start | bytes 589832 | tf_op jit(solution)/shard_map/ppermute | solution.py:244
  (23 other events, 529.6 us)

commit v2 on v0

v2 whole, which is shorter than its diff:
```python
import functools

import jax
import jax.numpy as jnp
from jax import lax
from jax.experimental import pallas as pl
from jax.experimental.pallas import tpu as pltpu
from jax.sharding import PartitionSpec as P


TALL = 4
WIDE = 8
EPSILON = 1e-06
LATE = False
LANES = 128
VMEM = pl.BlockSpec(memory_space=pltpu.VMEM)
HBM = pl.BlockSpec(memory_space=pltpu.HBM)


def strip_of(device, group):
    if group % 4:
        return device
    column, side, core = device // 4, (device // 2) % 2, device % 2
    return side * (group // 2) + 2 * (column + side * (group // 4 - 1 - 2 * column)) + core


def device_at(group):
    places = [strip_of(d, group) for d in range(group)]
    return [places.index(s) for s in range(group)]


def bulk_kernel(*refs, span):
    words, (cells_ref, out_ref, *bufs, in_buf, out_buf, tag_buf, word_sem, in_sem, out_sem) = refs[:3], refs[3:]
    parts, each = in_buf.shape[:2]
    group, _, rows, side = out_buf.shape
    planes = in_buf.shape[3]
    held = parts * each
    many = each * span * planes
    fetches = [
        pltpu.make_async_copy(cells_ref.at[pl.ds(j * each, each), pl.ds(0, span)], in_buf.at[j], in_sem.at[j])
        for j in range(parts)
    ]
    small = [pltpu.make_async_copy(word, buf, word_sem.at[n]) for n, (word, buf) in enumerate(zip(words, bufs))]
    for fetch in small + fetches:
        fetch.start()
    for fetch in small:
        fetch.wait()
    owner_ref, down_ref, across_ref = bufs
    tag_buf[...] = jnp.zeros(tag_buf.shape, jnp.float32)
    tag_buf[0:1, :held] = (owner_ref[...] * TALL + down_ref[...]).astype(jnp.float32)
    tag_buf[1:2, :held] = across_ref[...].astype(jnp.float32)
    tag = tag_buf[...].astype(out_buf.dtype)
    stores = []
    for j, fetch in enumerate(fetches):
        fetch.wait()
        more = j == parts - 1
        for g in range(group):
            strip = strip_of(g, group)
            out_buf[g, j * many : (j + 1) * many] = in_buf[j, :, :, :, strip].reshape(many, rows, side)
            if more:
                out_buf[g, held * span * planes] = tag
            piece = pl.ds(j * many, many + more)
            stores.append(pltpu.make_async_copy(out_buf.at[g, piece], out_ref.at[g, piece], out_sem.at[j, g]))
            stores[-1].start()
    for store in stores:
        store.wait()


def bulk_cut(owner, down, across, cells, span):
    held, _, planes, group, rows, side = cells.shape
    parts = next(p for p in (4, 3, 2, 1) if held % p == 0)
    out = jax.ShapeDtypeStruct((group, held * span * planes + 1, rows, side), cells.dtype)
    return pl.pallas_call(
        functools.partial(bulk_kernel, span=span),
        out_shape=pltpu.HBM(out.shape, out.dtype),
        in_specs=[HBM] * 4,
        out_specs=HBM,
        scratch_shapes=[
            *[pltpu.VMEM((1, held), jnp.int32)] * 3,
            pltpu.VMEM((parts, held // parts, span, planes, group, rows, side), cells.dtype),
            pltpu.VMEM(out.shape, out.dtype),
            pltpu.VMEM((rows, side), jnp.float32),
            pltpu.SemaphoreType.DMA((3,)),
            pltpu.SemaphoreType.DMA((parts,)),
            pltpu.SemaphoreType.DMA((parts, group)),
        ],
        compiler_params=pltpu.CompilerParams(vmem_limit_bytes=24 << 20),
        name="bulk_cut",
    )(owner, down, across, cells)


def cut_kernel(strip_ref, cells_ref, *outs):
    held, _, planes, _, rows, side = cells_ref.shape
    for m, out in enumerate(outs):
        out[...] = cells_ref[:, 0, :, strip_ref[m]].reshape(held * planes, rows, side)


def cut(strips, cells, date):
    held, _, planes, group, rows, side = cells.shape
    piece = (held * planes, rows, side)
    return pl.pallas_call(
        cut_kernel,
        out_shape=[jax.ShapeDtypeStruct(piece, cells.dtype)] * group,
        grid_spec=pltpu.PrefetchScalarGridSpec(
            num_scalar_prefetch=1,
            grid=(1,),
            in_specs=[pl.BlockSpec((held, 1, planes, group, rows, side), lambda i, strips: (0, date, 0, 0, 0, 0))],
            out_specs=[pl.BlockSpec(piece, lambda i, strips: (0, 0, 0))] * group,
        ),
        compiler_params=pltpu.CompilerParams(vmem_limit_bytes=16 << 20),
        name="cut",
    )(strips, cells)


def gather(place_ref, share_ref, pieces, comps, base, held):
    span, planes = len(comps), comps[0].shape[1]
    for m, piece in enumerate(pieces):

        def add(k, carry, m=m, piece=piece):
            place = place_ref[(base + m) * held + k]
            share = share_ref[(base + m) * held + k]
            for d, comp in enumerate(comps):
                for q in range(planes):
                    comp[place, q] += piece[(k * span + d) * planes + q].astype(jnp.float32) * share
            return carry

        lax.fori_loop(0, held, add, 0, unroll=4)


def box_sums(strip, comps, window_ref, sums_ref, own_ref, up_ref, down_ref, group, skip):
    slots, _, rows, side = comps[0].shape
    lines = slots // WIDE
    step = min(lines, 16)
    window = window_ref[...]

    def row_of(comp, q, at):
        parts = [comp[pl.ds(c * lines + at, step), q].reshape(step * rows, side) for c in range(WIDE)]
        return jnp.concatenate(parts, axis=1)

    def emit(index, field, at):
        high = field.astype(jnp.bfloat16)
        low = (field - high.astype(jnp.float32)).astype(jnp.bfloat16)
        total = jnp.dot(high, window, preferred_element_type=jnp.float32)
        total += jnp.dot(low, window, preferred_element_type=jnp.float32)
        for half in range(sums_ref.shape[1]):
            sums_ref[index, half, pl.ds(at * rows, step * rows), :] = total[:, half * LANES : (half + 1) * LANES]

    for number in range(lines // step):
        at = number * step
        index = 0
        re_old = im_old = None
        for d, comp in enumerate(comps):
            re, im = row_of(comp, 0, at), row_of(comp, 1, at)
            if d >= skip:
                emit(index, re * re + im * im, at)
                index += 1
            if d:
                emit(index, re_old * re + im_old * im, at)
                emit(index + 1, im_old * re - re_old * im, at)
                index += 2
            re_old, im_old = re, im
    for f in range(sums_ref.shape[0]):
        level = [
            jnp.concatenate(
                [sums_ref[f, half, pl.ds(y, lines, stride=rows), :] for half in range(sums_ref.shape[1])], axis=1
            )
            for y in range(rows)
        ]
        for i in range(rows // 4):
            begin, end = max(0, 4 * i - 1), min(rows, 4 * i + 6)
            own_ref[f, i] = sum(level[begin + 1 : end], level[begin])
        up, down = level[0] + level[1], level[rows - 1]
        line = lax.broadcasted_iota(jnp.int32, up.shape, 0)
        up_next = jnp.where(line == lines - 1, 0.0, pltpu.roll(up, lines - 1, 0))
        down_next = jnp.where(line == 0, 0.0, pltpu.roll(down, 1, 0))
        up_ref[f] = jnp.where(strip == 0, up_next, up)
        down_ref[f] = jnp.where(strip == group - 1, down_next, down)


def bulk_step_kernel(strip_ref, place_ref, share_ref, got_ref, window_ref, kept_ref, own_ref, up_ref, down_ref, sums_ref, *fresh, group, held):
    comps = [*fresh, kept_ref]
    for comp in comps:
        comp[...] = jnp.zeros(comp.shape, jnp.float32)
    gather(place_ref, share_ref, [got_ref.at[m] for m in range(group)], comps, 0, held)
    box_sums(strip_ref[0], comps, window_ref, sums_ref, own_ref, up_ref, down_ref, group, 0)


def step_kernel(strip_ref, place_ref, share_ref, *refs, group, held):
    pieces, (window_ref, before_ref, comp, own_ref, up_ref, down_ref, sums_ref) = refs[:-7], refs[-7:]
    comp[...] = jnp.zeros(comp.shape, jnp.float32)
    gather(place_ref, share_ref, pieces, [comp], 0, held)
    box_sums(strip_ref[0], [before_ref, comp], window_ref, sums_ref, own_ref, up_ref, down_ref, group, 1)


def part_kernel(place_ref, share_ref, *refs, base, held):
    pieces, comp = refs[:-1], refs[-1]
    comp[...] = jnp.zeros(comp.shape, jnp.float32)
    gather(place_ref, share_ref, pieces, [comp], base, held)


def last_step_kernel(strip_ref, place_ref, share_ref, *refs, group, base, held):
    pieces, (window_ref, before_ref, part_ref, comp, own_ref, up_ref, down_ref, sums_ref) = refs[:-8], refs[-8:]
    del part_ref
    gather(place_ref, share_ref, pieces, [comp], base, held)
    box_sums(strip_ref[0], [before_ref, comp], window_ref, sums_ref, own_ref, up_ref, down_ref, group, 1)


def sums_of(fields, rows, lines, cols):
    outs = [(fields, rows // 4, lines, cols), (fields, lines, cols), (fields, lines, cols)]
    return [jax.ShapeDtypeStruct(s, jnp.float32) for s in outs], pltpu.VMEM((fields, cols // LANES, lines * rows, LANES), jnp.float32)


def call(kernel, prefetch, args, outs, scratch=(), aliases=None, mib=16):
    return pl.pallas_call(
        kernel,
        out_shape=outs,
        grid_spec=pltpu.PrefetchScalarGridSpec(
            num_scalar_prefetch=len(prefetch),
            grid=(),
            in_specs=[VMEM] * len(args),
            out_specs=[VMEM] * len(outs),
            scratch_shapes=list(scratch),
        ),
        input_output_aliases=aliases or {},
        compiler_params=pltpu.CompilerParams(vmem_limit_bytes=mib << 20),
    )(*prefetch, *args)


def whole_sum(own_ref, above_ref, below_ref, f, i):
    total = own_ref[f, i]
    if i == 0:
        total = total + above_ref[f]
    if i == own_ref.shape[1] - 1:
        total = total + below_ref[f]
    return total


def coherence(re, im, first, second):
    return jnp.sqrt(re * re + im * im) / jnp.sqrt(first * second + EPSILON)


def deal(out_ref, at, value):
    for g in range(out_ref.shape[0]):
        out_ref[g, at : at + TALL] = value[g * TALL : (g + 1) * TALL]


def bulk_finish_kernel(own_ref, above_ref, below_ref, next_ref, next_above_ref, next_below_ref, out_ref, power_ref, *, span):
    tall = own_ref.shape[1]
    for i in range(tall):
        powers = []
        for d in range(span):
            at = 0 if d == 0 else 3 * d - 2
            powers.append(whole_sum(own_ref, above_ref, below_ref, at, i))
            if d:
                re, im = (whole_sum(own_ref, above_ref, below_ref, at + n, i) for n in (1, 2))
                deal(out_ref, ((d - 1) * tall + i) * TALL, coherence(re, im, powers[-2], powers[-1]))
        power, re, im = (whole_sum(next_ref, next_above_ref, next_below_ref, n, i) for n in range(3))
        deal(out_ref, ((span - 1) * tall + i) * TALL, coherence(re, im, powers[-1], power))
        power_ref[i] = power


def last_finish_kernel(own_ref, above_ref, below_ref, power_ref, out_ref):
    for i in range(own_ref.shape[1]):
        power, re, im = (whole_sum(own_ref, above_ref, below_ref, n, i) for n in range(3))
        deal(out_ref, i * TALL, coherence(re, im, power_ref[i], power))


def settle_kernel(*refs):
    out_ref = refs[-1]
    base = 0
    for got_ref in refs[:-1]:
        group = got_ref.shape[0]
        tall = out_ref.shape[1] // (TALL * group)
        pairs = got_ref.shape[1] // (tall * TALL)
        for device in range(group):
            strip = strip_of(device, group)
            for k in range(pairs):
                for i in range(tall):
                    for r in range(TALL):
                        at = (k * tall + i) * TALL + r
                        row = (r * group + strip) * tall + i
                        out_ref[base + k, row : row + 1] = got_ref[device, at : at + 1]
        base += pairs


def local(radar_subimages, owning_sector, sector_down_start, sector_across_start):
    group = lax.axis_size("grid")
    held, dates, planes, side, _ = radar_subimages.shape
    rows = side // group
    lines = group * TALL
    cols = WIDE * side
    span = dates - 2
    me = lax.axis_index("grid").astype(jnp.int32)
    devices = jnp.arange(group, dtype=jnp.int32)
    at = device_at(group)
    cells = radar_subimages.reshape(held, dates, planes, group, rows, side)
    cells = pltpu.with_memory_space_constraint(cells, pltpu.HBM)

    words = [
        pltpu.with_memory_space_constraint(word.reshape(1, held), pltpu.HBM)
        for word in (owning_sector, sector_down_start, sector_across_start)
    ]
    bulk = bulk_cut(*words, cells, span)
    got = lax.all_to_all(bulk, "grid", split_axis=0, concat_axis=0, tiled=True)
    strips = strip_of(me ^ devices, group)

    def scatter(date, after=None):
        sends = cut(strips, cells, date)
        if after is not None:
            sends, _ = lax.optimization_barrier((sends, after))
        pieces = [sends[0]] + [None] * (group - 1)
        for m in range(1, group):
            pieces[m] = lax.ppermute(sends[m], "grid", [(i, i ^ m) for i in range(group)])
        return pieces

    pieces_b = scatter(dates - 2)
    pieces = scatter(dates - 1, got if LATE else None)

    col = jnp.arange(cols)[:, None]
    out_col = jnp.arange(cols // 4)[None, :]
    window = ((col >= 4 * out_col - 12) & (col <= 4 * out_col + 15)).astype(jnp.bfloat16)
    tags = got[:, -1, :2, :held].astype(jnp.int32)
    places = tags[:, 1] * lines + tags[:, 0]
    flat = places.reshape(group * held)
    counts = jnp.sum((flat[:, None] == flat[None, :]).astype(jnp.int32), axis=1)
    shares = 1.0 / jnp.maximum(counts, 1).astype(jnp.float32)
    tables = (flat, shares)
    swapped = tuple(t.reshape(group, held)[me ^ devices].reshape(group * held) for t in tables)

    def exchange(up, down):
        below = lax.ppermute(up, "grid", [(at[s], at[s - 1]) for s in range(group)])
        above = lax.ppermute(down, "grid", [(at[s - 1], at[s]) for s in range(group)])
        return above, below

    comp = pltpu.VMEM((lines * WIDE, planes, rows, side), jnp.float32)
    out_cols = cols // 4
    tall = rows // 4
    outs, sums = sums_of(3 * span - 2, rows, lines, out_cols)
    kept, own, up, down = call(
        functools.partial(bulk_step_kernel, group=group, held=held),
        (strips, *tables), (got, window), [comp, *outs], [sums] + [comp] * (span - 1),
        mib=32,
    )
    above, below = exchange(up, down)
    outs, sums = sums_of(3, rows, lines, out_cols)
    kept, *next_sums = call(
        functools.partial(step_kernel, group=group, held=held),
        (strips, *swapped), (*pieces_b, window, kept), [comp, *outs], [sums],
    )
    next_own, up, down = next_sums
    next_above, next_below = exchange(up, down)
    dealt, power = call(
        functools.partial(bulk_finish_kernel, span=span), (),
        (own, above, below, next_own, next_above, next_below),
        [
            jax.ShapeDtypeStruct((group, span * tall * TALL, out_cols), jnp.float32),
            jax.ShapeDtypeStruct((tall, lines, out_cols), jnp.float32),
        ],
    )
    if LATE:
        first = lax.all_to_all(dealt, "grid", split_axis=0, concat_axis=0, tiled=True)

    near = group // 2
    (part,) = call(functools.partial(part_kernel, base=0, held=held), swapped, pieces[:near], [comp])
    far = pieces[near:]
    _, own, up, down = call(
        functools.partial(last_step_kernel, group=group, base=near, held=held),
        (strips, *swapped), (*far, window, kept, part), [comp, *outs], [sums], aliases={3 + len(far) + 2: 0},
    )
    above, below = exchange(up, down)
    (last,) = call(
        last_finish_kernel, (), (own, above, below, power),
        [jax.ShapeDtypeStruct((group, tall * TALL, out_cols), jnp.float32)],
    )
    if LATE:
        second = lax.all_to_all(last, "grid", split_axis=0, concat_axis=0, tiled=True)
        got = (first, second)
    else:
        last = jnp.concatenate([dealt, last], axis=1)
        got = (lax.all_to_all(last, "grid", split_axis=0, concat_axis=0, tiled=True),)
    (out,) = call(
        settle_kernel, (), got,
        [jax.ShapeDtypeStruct((dates - 1, TALL * side // 4, out_cols), jnp.float32)],
    )
    return out


def solution(mesh):
    in_specs = (
        P(("region", "grid"), None, None, None, None),
        P(("region", "grid"), None),
        P(("region", "grid")),
        P(("region", "grid")),
    )
    out_specs = P(None, ("region", "grid"), None)

    return jax.shard_map(local, mesh=mesh, in_specs=in_specs, out_specs=out_specs, check_vma=False)
```

time: 225 us -> 215 us (0.956)
  starting transfers between devices: 78.7 us -> 48 us
  local copies, waits for them, and re-layouts: 5.85 us -> 32.8 us
  Pallas kernels: 37.4 us -> 30.4 us
  waiting for transfers between devices: 76.9 us -> 83.4 us
  blocking collectives: 18.4 us -> 14.5 us
  other arithmetic: 4.43 us -> 2.05 us
    ppermute x51 -> x36, starting transfers between devices: 78.7 us -> 41.4 us  [the longest x30 36.6 us: scatter(): lax.ppermute(sends[m], 'grid', [(i, i ^ m) for i in range(group)])]
    unnamed x97 -> x116, local copies, waits for them, and re-layouts: 2.14 us -> 30.7 us
    pallas_call x6 -> x10, Pallas kernels: 37.4 us -> 30.4 us  [the longest x7 21.2 us: call(): pl.pallas_call(kernel, out_shape=outs, grid_spec=pltpu.PrefetchScalarGrid...]
    all_to_all x0 -> x1, starting transfers between devices: none -> 6.53 us  [local(): got = lax.all_to_all(bulk, 'grid', split_axis=0, concat_axis=0, tiled=True)]
    ppermute x51 -> x36, waiting for transfers between devices: 76.9 us -> 83.4 us  [the longest x30 78.5 us: scatter(): lax.ppermute(sends[m], 'grid', [(i, i ^ m) for i in range(group)])]
    all_to_all x1, blocking collectives: 18.4 us -> 14.5 us  [local(): lax.all_to_all(last, 'grid', split_axis=0, concat_axis=0, tiled=True)]
  transfers between devices with their start and end apart: 51 -> 37, of which waited for: 18 -> 9; matrix products, arithmetic and copies ran while one was open for 2% -> 2% of each run, Pallas kernels for 15% -> 12%
where the time goes in v2:
time: 215 us; the launch traced here: 211 us
  waiting for transfers between devices  83.4 us (39%)
  starting transfers between devices  48 us (22%)
  local copies, waits for them, and re-layouts  32.8 us (15%)
  Pallas kernels  30.4 us (14%)
  blocking collectives  14.5 us (7%)
    ppermute x30, waiting for transfers between devices, scatter(): lax.ppermute(sends[m], 'grid', [(i, i ^ m) for i in range(group)])  78.5 us
    ppermute x30, starting transfers between devices, scatter(): lax.ppermute(sends[m], 'grid', [(i, i ^ m) for i in range(group)])  36.6 us
    unnamed x116, local copies, waits for them, and re-layouts  30.7 us
    pallas_call x7, Pallas kernels, call(): pl.pallas_call(kernel, out_shape=outs, grid_spec=pltpu.PrefetchScalarGrid...  21.2 us
    all_to_all x1, blocking collectives, local(): lax.all_to_all(last, 'grid', split_axis=0, concat_axis=0, tiled=True)  14.5 us
    all_to_all x1, starting transfers between devices, local(): got = lax.all_to_all(bulk, 'grid', split_axis=0, concat_axis=0, tiled=True)  6.53 us
    pallas_call x2, Pallas kernels, cut(): pl.pallas_call(cut_kernel, out_shape=[jax.ShapeDtypeStruct(piece, cells.d...  5.47 us
  transfers between devices with their start and end apart: 37, of which 9 were waited for; matrix products, arithmetic and copies ran while one was open for 2% of the time, Pallas kernels for 12%

profile of v2, /device:TPU:13, one launch (start us, length us, event | category | flops | bytes accessed | tf_op | source)
XLA Modules:
  0.0 211.5 jit_solution(1183285411013097583)
XLA Ops:
  0.0 3.7 %bulk_cut.1 = bf16[16,97,8,128]{3,2,1,0:T(8,128)(2,1)} custom-call(s32[1,24]{1,0:T(1,128)} %bitcast.16, s32[1,24]{1,0:T(1,128)} %bitcast.17, s32[1,24]{1,0:T(1,128)} %bitcast.18, bf16[24,4,2,16,8,128]{5,4,3,2,1,0:T(8,128)(2,1)} %bitcast.12), custom_call_target="tpu_custom_call" | custom-call | tf_op jit(solution)/shard_map/bulk_cut/pallas_call | solution.py:73
  3.8 6.5 %all-to-all-start = ((bf16[16,97,8,128]{3,2,1,0:T(8,128)(2,1)}), bf16[16,97,8,128]{3,2,1,0:T(8,128)(2,1)S(1)}, u32[]{:S(2)}, u32[]{:S(2)}) async-start(bf16[16,97,8,128]{3,2,1,0:T(8,128)(2,1)} %bulk_cut.1), calls=%async_computation | async-start | bytes 6356992 | tf_op jit(solution)/shard_map/all_to_all | solution.py:304
  10.3 3.1 %cut.2 = (bf16[48,8,128]{2,1,0:T(8,128)(2,1)S(1)}, bf16[48,8,128]{2,1,0:T(8,128)(2,1)}, bf16[48,8,128]{2,1,0:T(8,128)(2,1)}, bf16[48,8,128]{2,1,0:T(8,128)(2,1)S...) custom-call(s32[16]{0:T(128)S(1)} %fusion.5.strip_ref, ...), custom_call_target="tpu_custom_call" | custom-call | tf_op jit(solution)/shard_map/cut/pallas_call | solution.py:101
  17.9 2.4 %collective-permute-start.10 = (bf16[48,8,128]{2,1,0:T(8,128)(2,1)S(1)}, bf16[48,8,128]{2,1,0:T(8,128)(2,1)S(1)}, u32[]{:S(2)}, u32[]{:S(2)}) collective-permute-start(bf16[48,8,128]{2,1,0:T(8,128)(2,1)S(1)} %get-tuple-element.62), channel_id=1, source_target_pairs={{0,9},{1,8},{2,11},{3,10},{4,13},{5,12},{6,15},{7,14},{8,1},{9,0},... | collective-permute-start | bytes 294920 | tf_op jit(solution)/shard_map/ppermute | solution.py:313
  20.6 3.3 %collective-permute-start.12 = (bf16[48,8,128]{2,1,0:T(8,128)(2,1)S(1)}, bf16[48,8,128]{2,1,0:T(8,128)(2,1)S(1)}, u32[]{:S(2)}, u32[]{:S(2)}) collective-permute-start(bf16[48,8,128]{2,1,0:T(8,128)(2,1)S(1)} %get-tuple-element.64), channel_id=1, source_target_pairs={{0,11},{1,10},{2,9},{3,8},{4,15},{5,14},{6,13},{7,12},{8,3},{9,2},... | collective-permute-start | bytes 294920 | tf_op jit(solution)/shard_map/ppermute | solution.py:313
  23.8 1.7 collective-permute-start.14
  25.6 2.4 %cut.3 = (bf16[48,8,128]{2,1,0:T(8,128)(2,1)S(1)}, bf16[48,8,128]{2,1,0:T(8,128)(2,1)S(1)}, bf16[48,8,128]{2,1,0:T(8,128)(2,1)S(1)}, bf16[48,8,128]{2,1,0:T(8,12...) custom-call(s32[16]{0:T(128)S(1)} %fusion.5.strip_ref, ...), custom_call_target="tpu_custom_call" | custom-call | tf_op jit(solution)/shard_map/cut/pallas_call | solution.py:101
  36.1 55.1 %collective-permute-done.10.refs_9_ = bf16[48,8,128]{2,1,0:T(8,128)(2,1)S(1)} collective-permute-done((bf16[48,8,128]{2,1,0:T(8,128)(2,1)S(1)}, bf16[48,8,128]{2,1,0:T(8,128)(2,1)S(1)}, u32[]{:S(2)}, u32[]{:S(2)}) %collective-permute-start.10) | collective-permute-done | bytes 98336 | tf_op jit(solution)/shard_map/ppermute | solution.py:313
  94.0 2.7 %collective-permute-start.16 = (bf16[48,8,128]{2,1,0:T(8,128)(2,1)}, bf16[48,8,128]{2,1,0:T(8,128)(2,1)S(1)}, u32[]{:S(2)}, u32[]{:S(2)}) collective-permute-start(bf16[48,8,128]{2,1,0:T(8,128)(2,1)} %get-tuple-element.68), channel_id=1, source_target_pairs={{0,15},{1,14},{2,13},{3,12},{4,11},{5,10},{6,9},{7,8},{8,7},{9,6},... | collective-permute-start | bytes 294920 | tf_op jit(solution)/shard_map/ppermute | solution.py:313
  97.6 4.0 %collective-permute-done.13.refs_12_ = bf16[48,8,128]{2,1,0:T(8,128)(2,1)S(1)} collective-permute-done((bf16[48,8,128]{2,1,0:T(8,128)(2,1)S(1)}, bf16[48,8,128]{2,1,0:T(8,128)(2,1)S(1)}, u32[]{:S(2)}, u32[]{:S(2)}) %collective-permute-start.13) | collective-permute-done | bytes 98336 | tf_op jit(solution)/shard_map/ppermute | solution.py:313
  102.4 4.3 %collective-permute-done.14.refs_13_ = bf16[48,8,128]{2,1,0:T(8,128)(2,1)S(1)} collective-permute-done((bf16[48,8,128]{2,1,0:T(8,128)(2,1)}, bf16[48,8,128]{2,1,0:T(8,128)(2,1)S(1)}, u32[]{:S(2)}, u32[]{:S(2)}) %collective-permute-start.14) | collective-permute-done | bytes 98336 | tf_op jit(solution)/shard_map/ppermute | solution.py:313
  109.0 1.5 collective-permute-done.16.refs_15_
  115.3 1.4 collective-permute-start.9
  117.5 1.6 collective-permute-start.28
  119.1 1.9 collective-permute-start.29
  121.0 1.7 collective-permute-done.8.refs_7_
  123.6 2.3 %collective-permute-start.31 = (bf16[48,8,128]{2,1,0:T(8,128)(2,1)}, bf16[48,8,128]{2,1,0:T(8,128)(2,1)}, u32[]{:S(2)}, u32[]{:S(2)}) collective-permute-start(bf16[48,8,128]{2,1,0:T(8,128)(2,1)} %copy-done.47), channel_id=1, source_target_pairs={{0,5},{1,4},{2,7},{3,6},{4,1},{5,0},{6,3},{7,2},{8,13},{9,12},{10,... | collective-permute-start | bytes 294920 | tf_op jit(solution)/shard_map/ppermute | solution.py:313
  127.5 2.3 %collective-permute-start.33 = (bf16[48,8,128]{2,1,0:T(8,128)(2,1)}, bf16[48,8,128]{2,1,0:T(8,128)(2,1)}, u32[]{:S(2)}, u32[]{:S(2)}) collective-permute-start(bf16[48,8,128]{2,1,0:T(8,128)(2,1)} %copy-done.45), channel_id=1, source_target_pairs={{0,7},{1,6},{2,5},{3,4},{4,3},{5,2},{6,1},{7,0},{8,15},{9,14},{10,... | collective-permute-start | bytes 294920 | tf_op jit(solution)/shard_map/ppermute | solution.py:313
  131.2 2.6 %collective-permute-start.20 = (bf16[48,8,128]{2,1,0:T(8,128)(2,1)}, bf16[48,8,128]{2,1,0:T(8,128)(2,1)S(1)}, u32[]{:S(2)}, u32[]{:S(2)}) collective-permute-start(bf16[48,8,128]{2,1,0:T(8,128)(2,1)} %copy-done.43), channel_id=1, source_target_pairs={{0,9},{1,8},{2,11},{3,10},{4,13},{5,12},{6,15},{7,14},{8,1},{9,0},... | collective-permute-start | bytes 294920 | tf_op jit(solution)/shard_map/ppermute | solution.py:313
  136.3 2.4 %collective-permute-start.22 = (bf16[48,8,128]{2,1,0:T(8,128)(2,1)}, bf16[48,8,128]{2,1,0:T(8,128)(2,1)}, u32[]{:S(2)}, u32[]{:S(2)}) collective-permute-start(bf16[48,8,128]{2,1,0:T(8,128)(2,1)} %copy-done.41), channel_id=1, source_target_pairs={{0,11},{1,10},{2,9},{3,8},{4,15},{5,14},{6,13},{7,12},{8,3},{9,2},... | collective-permute-start | bytes 294920 | tf_op jit(solution)/shard_map/ppermute | solution.py:313
  139.9 6.5 %shard_map.46 = (f32[512,2,8,128]{3,2,1,0:T(8,128)S(1)}, f32[4,2,64,256]{3,2,1,0:T(8,128)S(1)}, f32[4,64,256]{2,1,0:T(8,128)S(1)}, f32[4,64,256]{2,1,0:T(8,128)S(1)}) custom-call(s32[16]{0:T(128)S(1)} %fusion.5.strip_ref, s32[384]{0:T(512)S(1)} %add.77.place_ref, f32[384]{0:T(512)S(1)} %convert_divide_fusion.share_ref, ...), custom_call_target="tpu_custom_call" | custom-call | tf_op jit(solution)/shard_map/pallas_call | solution.py:214
  156.3 6.0 %shard_map.47 = (f32[512,2,8,128]{3,2,1,0:T(8,128)S(1)}, f32[3,2,64,256]{3,2,1,0:T(8,128)S(1)}, f32[3,64,256]{2,1,0:T(8,128)S(1)}, f32[3,64,256]{2,1,0:T(8,128)S(1)}) custom-call(s32[16]{0:T(128)S(1)} %fusion.5.strip_ref, s32[384]{0:T(512)S(1)} %reshape.86.place_ref, f32[384]{0:T(512)S(1)} %reshape.87.share_ref, bf16[48,8,128]{2,1,0:T(8,128)(2,1)S(1)} %copy-done.4, ...), custom_call_target="tpu_custom_call" | custom-call | tf_op jit(solution)/shard_map/pallas_call | solution.py:214
  162.4 1.4 collective-permute-start.23
  164.9 2.0 collective-permute-start.26
  166.9 11.7 %collective-permute-done.23.refs_4_ = bf16[48,8,128]{2,1,0:T(8,128)(2,1)S(1)} collective-permute-done((bf16[48,8,128]{2,1,0:T(8,128)(2,1)S(1)}, bf16[48,8,128]{2,1,0:T(8,128)(2,1)S(1)}, u32[]{:S(2)}, u32[]{:S(2)}) %collective-permute-start.23) | collective-permute-done | bytes 98336 | tf_op jit(solution)/shard_map/ppermute | solution.py:313
  178.5 2.8 %collective-permute-start.1 = (f32[4,64,256]{2,1,0:T(8,128)S(1)}, f32[4,64,256]{2,1,0:T(8,128)S(1)}, u32[]{:S(2)}, u32[]{:S(2)}) collective-permute-start(f32[4,64,256]{2,1,0:T(8,128)S(1)} %get-tuple-element.52), channel_id=1, source_target_pairs={{0,3},{1,0},{4,1},{5,4},{8,5},{9,8},{12,9},{13,12},{14,13},{15,14}... | collective-permute-start | bytes 786440 | tf_op jit(solution)/shard_map/ppermute | solution.py:331
  181.3 2.6 %shard_map.49.refs_10_ = f32[512,2,8,128]{3,2,1,0:T(8,128)S(1)} custom-call(s32[384]{0:T(512)S(1)} %reshape.86.place_ref, f32[384]{0:T(512)S(1)} %reshape.87.share_ref, bf16[48,8,128]{2,1,0:T(8,128)(2,1)S(1)} %copy-done.2, bf16[48,8,128]{2,1,0:T(8,128)(2,1)S(1)} %copy-done.20, bf16[48,8,128]{2,1,0:T(8,128)(2,1)S(1)} %copy-done.22, ...), custom_call_target="tpu_custom_call" | custom-call | tf_op jit(solution)/shard_map/pallas_call | solution.py:214
  184.2 4.8 %shard_map.50 = (f32[512,2,8,128]{3,2,1,0:T(8,128)S(1)}, f32[3,2,64,256]{3,2,1,0:T(8,128)S(1)}, f32[3,64,256]{2,1,0:T(8,128)S(1)}, f32[3,64,256]{2,1,0:T(8,128)S(1)}) custom-call(s32[16]{0:T(128)S(1)} %fusion.5.strip_ref, s32[384]{0:T(512)S(1)} %reshape.86.place_ref, f32[384]{0:T(512)S(1)} %reshape.87.share_ref, ...), custom_call_target="tpu_custom_call", output_to_operand_aliasing={{0}: (13, {})} | custom-call | tf_op jit(solution)/shard_map/pallas_call | solution.py:214
  189.0 1.8 collective-permute-start.34
  191.0 2.3 %collective-permute-done.34.above_ref = f32[3,64,256]{2,1,0:T(8,128)S(1)} collective-permute-done((f32[3,64,256]{2,1,0:T(8,128)S(1)}, f32[3,64,256]{2,1,0:T(8,128)S(1)}, u32[]{:S(2)}, u32[]{:S(2)}) %collective-permute-start.34) | collective-permute-done | bytes 196640 | tf_op jit(solution)/shard_map/ppermute | solution.py:332
  193.4 2.5 %collective-permute-done.35.below_ref = f32[3,64,256]{2,1,0:T(8,128)S(1)} collective-permute-done((f32[3,64,256]{2,1,0:T(8,128)S(1)}, f32[3,64,256]{2,1,0:T(8,128)S(1)}, u32[]{:S(2)}, u32[]{:S(2)}) %collective-permute-start.35) | collective-permute-done | bytes 196640 | tf_op jit(solution)/shard_map/ppermute | solution.py:331
  196.0 14.5 %all_to_all.10.refs_0_ = f32[16,24,256]{2,1,0:T(8,128)S(1)} all-to-all(f32[16,24,256]{2,1,0:T(8,128)S(1)} %pad_maximum_fusion), channel_id=1, replica_groups=mesh['region'=2,'grid'=16] {'grid'}, dimensions={0} | all-to-all | bytes 786432 | tf_op jit(solution)/shard_map/all_to_all | solution.py:380
  (186 shorter events, 45.1 us)
Async XLA Ops:
  3.8 98.7 %all-to-all-start = ((bf16[16,97,8,128]{3,2,1,0:T(8,128)(2,1)}), bf16[16,97,8,128]{3,2,1,0:T(8,128)(2,1)S(1)}, u32[]{:S(2)}, u32[]{:S(2)}) async-start(bf16[16,97,8,128]{3,2,1,0:T(8,128)(2,1)} %bulk_cut.1), calls=%async_computation | async-start | bytes 6356992 | tf_op jit(solution)/shard_map/all_to_all | solution.py:304
  17.9 73.3 %collective-permute-start.10 = (bf16[48,8,128]{2,1,0:T(8,128)(2,1)S(1)}, bf16[48,8,128]{2,1,0:T(8,128)(2,1)S(1)}, u32[]{:S(2)}, u32[]{:S(2)}) collective-permute-start(bf16[48,8,128]{2,1,0:T(8,128)(2,1)S(1)} %get-tuple-element.62), channel_id=1, source_target_pairs={{0,9},{1,8},{2,11},{3,10},{4,13},{5,12},{6,15},{7,14},{8,1},{9,0},... | collective-permute-start | bytes 294920 | tf_op jit(solution)/shard_map/ppermute | solution.py:313
  20.3 73.0 %collective-permute-start.11 = (bf16[48,8,128]{2,1,0:T(8,128)(2,1)S(1)}, bf16[48,8,128]{2,1,0:T(8,128)(2,1)S(1)}, u32[]{:S(2)}, u32[]{:S(2)}) collective-permute-start(bf16[48,8,128]{2,1,0:T(8,128)(2,1)S(1)} %get-tuple-element.63), channel_id=1, source_target_pairs={{0,10},{1,11},{2,8},{3,9},{4,14},{5,15},{6,12},{7,13},{8,2},{9,3},... | collective-permute-start | bytes 294920 | tf_op jit(solution)/shard_map/ppermute | solution.py:313
  20.6 76.1 %collective-permute-start.12 = (bf16[48,8,128]{2,1,0:T(8,128)(2,1)S(1)}, bf16[48,8,128]{2,1,0:T(8,128)(2,1)S(1)}, u32[]{:S(2)}, u32[]{:S(2)}) collective-permute-start(bf16[48,8,128]{2,1,0:T(8,128)(2,1)S(1)} %get-tuple-element.64), channel_id=1, source_target_pairs={{0,11},{1,10},{2,9},{3,8},{4,15},{5,14},{6,13},{7,12},{8,3},{9,2},... | collective-permute-start | bytes 294920 | tf_op jit(solution)/shard_map/ppermute | solution.py:313
  23.8 77.8 %collective-permute-start.13 = (bf16[48,8,128]{2,1,0:T(8,128)(2,1)S(1)}, bf16[48,8,128]{2,1,0:T(8,128)(2,1)S(1)}, u32[]{:S(2)}, u32[]{:S(2)}) collective-permute-start(bf16[48,8,128]{2,1,0:T(8,128)(2,1)S(1)} %get-tuple-element.65), channel_id=1, source_target_pairs={{0,12},{1,13},{2,14},{3,15},{4,8},{5,9},{6,10},{7,11},{8,4},{9,5},... | collective-permute-start | bytes 294920 | tf_op jit(solution)/shard_map/ppermute | solution.py:313
  23.8 82.9 %collective-permute-start.14 = (bf16[48,8,128]{2,1,0:T(8,128)(2,1)}, bf16[48,8,128]{2,1,0:T(8,128)(2,1)S(1)}, u32[]{:S(2)}, u32[]{:S(2)}) collective-permute-start(bf16[48,8,128]{2,1,0:T(8,128)(2,1)} %get-tuple-element.66), channel_id=1, source_target_pairs={{0,13},{1,12},{2,15},{3,14},{4,9},{5,8},{6,11},{7,10},{8,5},{9,4},... | collective-permute-start | bytes 294920 | tf_op jit(solution)/shard_map/ppermute | solution.py:313
  91.9 16.5 %collective-permute-start.15 = (bf16[48,8,128]{2,1,0:T(8,128)(2,1)}, bf16[48,8,128]{2,1,0:T(8,128)(2,1)S(1)}, u32[]{:S(2)}, u32[]{:S(2)}) collective-permute-start(bf16[48,8,128]{2,1,0:T(8,128)(2,1)} %get-tuple-element.67), channel_id=1, source_target_pairs={{0,14},{1,15},{2,12},{3,13},{4,10},{5,11},{6,8},{7,9},{8,6},{9,7},... | collective-permute-start | bytes 294920 | tf_op jit(solution)/shard_map/ppermute | solution.py:313
  94.0 16.5 %collective-permute-start.16 = (bf16[48,8,128]{2,1,0:T(8,128)(2,1)}, bf16[48,8,128]{2,1,0:T(8,128)(2,1)S(1)}, u32[]{:S(2)}, u32[]{:S(2)}) collective-permute-start(bf16[48,8,128]{2,1,0:T(8,128)(2,1)} %get-tuple-element.68), channel_id=1, source_target_pairs={{0,15},{1,14},{2,13},{3,12},{4,11},{5,10},{6,9},{7,8},{8,7},{9,6},... | collective-permute-start | bytes 294920 | tf_op jit(solution)/shard_map/ppermute | solution.py:313
  97.3 14.5 %collective-permute-start.2 = (bf16[48,8,128]{2,1,0:T(8,128)(2,1)}, bf16[48,8,128]{2,1,0:T(8,128)(2,1)}, u32[]{:S(2)}, u32[]{:S(2)}) collective-permute-start(bf16[48,8,128]{2,1,0:T(8,128)(2,1)} %get-tuple-element.54), channel_id=1, source_target_pairs={{0,1},{1,0},{2,3},{3,2},{4,5},{5,4},{6,7},{7,6},{8,9},{9,8},{10,11... | collective-permute-start | bytes 294920 | tf_op jit(solution)/shard_map/ppermute | solution.py:313
  102.3 10.5 %collective-permute-start.3 = (bf16[48,8,128]{2,1,0:T(8,128)(2,1)}, bf16[48,8,128]{2,1,0:T(8,128)(2,1)}, u32[]{:S(2)}, u32[]{:S(2)}) collective-permute-start(bf16[48,8,128]{2,1,0:T(8,128)(2,1)} %get-tuple-element.55), channel_id=1, source_target_pairs={{0,2},{1,3},{2,0},{3,1},{4,6},{5,7},{6,4},{7,5},{8,10},{9,11},{10,... | collective-permute-start | bytes 294920 | tf_op jit(solution)/shard_map/ppermute | solution.py:313
  107.4 7.3 %collective-permute-start.4 = (bf16[48,8,128]{2,1,0:T(8,128)(2,1)}, bf16[48,8,128]{2,1,0:T(8,128)(2,1)S(1)}, u32[]{:S(2)}, u32[]{:S(2)}) collective-permute-start(bf16[48,8,128]{2,1,0:T(8,128)(2,1)} %copy-done.57), channel_id=1, source_target_pairs={{0,3},{1,2},{2,1},{3,0},{4,7},{5,6},{6,5},{7,4},{8,11},{9,10},{10,... | collective-permute-start | bytes 294920 | tf_op jit(solution)/shard_map/ppermute | solution.py:313
  109.0 7.8 %collective-permute-start.5 = (bf16[48,8,128]{2,1,0:T(8,128)(2,1)}, bf16[48,8,128]{2,1,0:T(8,128)(2,1)S(1)}, u32[]{:S(2)}, u32[]{:S(2)}) collective-permute-start(bf16[48,8,128]{2,1,0:T(8,128)(2,1)} %copy-done.56), channel_id=1, source_target_pairs={{0,4},{1,5},{2,6},{3,7},{4,0},{5,1},{6,2},{7,3},{8,12},{9,13},{10,... | collective-permute-start | bytes 294920 | tf_op jit(solution)/shard_map/ppermute | solution.py:313
  112.8 9.9 %collective-permute-start.8 = (bf16[48,8,128]{2,1,0:T(8,128)(2,1)}, bf16[48,8,128]{2,1,0:T(8,128)(2,1)}, u32[]{:S(2)}, u32[]{:S(2)}) collective-permute-start(bf16[48,8,128]{2,1,0:T(8,128)(2,1)} %copy-done.51), channel_id=1, source_target_pairs={{0,7},{1,6},{2,5},{3,4},{4,3},{5,2},{6,1},{7,0},{8,15},{9,14},{10,... | collective-permute-start | bytes 294920 | tf_op jit(solution)/shard_map/ppermute | solution.py:313
  115.3 7.6 %collective-permute-start.9 = (bf16[48,8,128]{2,1,0:T(8,128)(2,1)}, bf16[48,8,128]{2,1,0:T(8,128)(2,1)S(1)}, u32[]{:S(2)}, u32[]{:S(2)}) collective-permute-start(bf16[48,8,128]{2,1,0:T(8,128)(2,1)} %copy-done.49), channel_id=1, source_target_pairs={{0,8},{1,9},{2,10},{3,11},{4,12},{5,13},{6,14},{7,15},{8,0},{9,1},... | collective-permute-start | bytes 294920 | tf_op jit(solution)/shard_map/ppermute | solution.py:313
  117.4 8.5 %collective-permute-start.27 = (bf16[48,8,128]{2,1,0:T(8,128)(2,1)}, bf16[48,8,128]{2,1,0:T(8,128)(2,1)S(1)}, u32[]{:S(2)}, u32[]{:S(2)}) collective-permute-start(bf16[48,8,128]{2,1,0:T(8,128)(2,1)} %copy-done.54), channel_id=1, source_target_pairs={{0,1},{1,0},{2,3},{3,2},{4,5},{5,4},{6,7},{7,6},{8,9},{9,8},{10,11... | collective-permute-start | bytes 294920 | tf_op jit(solution)/shard_map/ppermute | solution.py:313
  117.5 9.3 %collective-permute-start.28 = (bf16[48,8,128]{2,1,0:T(8,128)(2,1)}, bf16[48,8,128]{2,1,0:T(8,128)(2,1)S(1)}, u32[]{:S(2)}, u32[]{:S(2)}) collective-permute-start(bf16[48,8,128]{2,1,0:T(8,128)(2,1)} %copy-done.52), channel_id=1, source_target_pairs={{0,2},{1,3},{2,0},{3,1},{4,6},{5,7},{6,4},{7,5},{8,10},{9,11},{10,... | collective-permute-start | bytes 294920 | tf_op jit(solution)/shard_map/ppermute | solution.py:313
  119.1 10.8 %collective-permute-start.29 = (bf16[48,8,128]{2,1,0:T(8,128)(2,1)}, bf16[48,8,128]{2,1,0:T(8,128)(2,1)S(1)}, u32[]{:S(2)}, u32[]{:S(2)}) collective-permute-start(bf16[48,8,128]{2,1,0:T(8,128)(2,1)} %copy-done.50), channel_id=1, source_target_pairs={{0,3},{1,2},{2,1},{3,0},{4,7},{5,6},{6,5},{7,4},{8,11},{9,10},{10,... | collective-permute-start | bytes 294920 | tf_op jit(solution)/shard_map/ppermute | solution.py:313
  122.7 7.8 %collective-permute-start.30 = (bf16[48,8,128]{2,1,0:T(8,128)(2,1)}, bf16[48,8,128]{2,1,0:T(8,128)(2,1)S(1)}, u32[]{:S(2)}, u32[]{:S(2)}) collective-permute-start(bf16[48,8,128]{2,1,0:T(8,128)(2,1)} %copy-done.48), channel_id=1, source_target_pairs={{0,4},{1,5},{2,6},{3,7},{4,0},{5,1},{6,2},{7,3},{8,12},{9,13},{10,... | collective-permute-start | bytes 294920 | tf_op jit(solution)/shard_map/ppermute | solution.py:313
  123.6 11.5 %collective-permute-start.31 = (bf16[48,8,128]{2,1,0:T(8,128)(2,1)}, bf16[48,8,128]{2,1,0:T(8,128)(2,1)}, u32[]{:S(2)}, u32[]{:S(2)}) collective-permute-start(bf16[48,8,128]{2,1,0:T(8,128)(2,1)} %copy-done.47), channel_id=1, source_target_pairs={{0,5},{1,4},{2,7},{3,6},{4,1},{5,0},{6,3},{7,2},{8,13},{9,12},{10,... | collective-permute-start | bytes 294920 | tf_op jit(solution)/shard_map/ppermute | solution.py:313
  126.6 9.8 %collective-permute-start.32 = (bf16[48,8,128]{2,1,0:T(8,128)(2,1)}, bf16[48,8,128]{2,1,0:T(8,128)(2,1)}, u32[]{:S(2)}, u32[]{:S(2)}) collective-permute-start(bf16[48,8,128]{2,1,0:T(8,128)(2,1)} %copy-done.46), channel_id=1, source_target_pairs={{0,6},{1,7},{2,4},{3,5},{4,2},{5,3},{6,0},{7,1},{8,14},{9,15},{10,... | collective-permute-start | bytes 294920 | tf_op jit(solution)/shard_map/ppermute | solution.py:313
  127.5 34.8 %collective-permute-start.33 = (bf16[48,8,128]{2,1,0:T(8,128)(2,1)}, bf16[48,8,128]{2,1,0:T(8,128)(2,1)}, u32[]{:S(2)}, u32[]{:S(2)}) collective-permute-start(bf16[48,8,128]{2,1,0:T(8,128)(2,1)} %copy-done.45), channel_id=1, source_target_pairs={{0,7},{1,6},{2,5},{3,4},{4,3},{5,2},{6,1},{7,0},{8,15},{9,14},{10,... | collective-permute-start | bytes 294920 | tf_op jit(solution)/shard_map/ppermute | solution.py:313
  130.5 31.9 %collective-permute-start.19 = (bf16[48,8,128]{2,1,0:T(8,128)(2,1)}, bf16[48,8,128]{2,1,0:T(8,128)(2,1)S(1)}, u32[]{:S(2)}, u32[]{:S(2)}) collective-permute-start(bf16[48,8,128]{2,1,0:T(8,128)(2,1)} %copy-done.44), channel_id=1, source_target_pairs={{0,8},{1,9},{2,10},{3,11},{4,12},{5,13},{6,14},{7,15},{8,0},{9,1},... | collective-permute-start | bytes 294920 | tf_op jit(solution)/shard_map/ppermute | solution.py:313
  131.2 32.7 %collective-permute-start.20 = (bf16[48,8,128]{2,1,0:T(8,128)(2,1)}, bf16[48,8,128]{2,1,0:T(8,128)(2,1)S(1)}, u32[]{:S(2)}, u32[]{:S(2)}) collective-permute-start(bf16[48,8,128]{2,1,0:T(8,128)(2,1)} %copy-done.43), channel_id=1, source_target_pairs={{0,9},{1,8},{2,11},{3,10},{4,13},{5,12},{6,15},{7,14},{8,1},{9,0},... | collective-permute-start | bytes 294920 | tf_op jit(solution)/shard_map/ppermute | solution.py:313
  135.1 29.4 %collective-permute-start.21 = (bf16[48,8,128]{2,1,0:T(8,128)(2,1)}, bf16[48,8,128]{2,1,0:T(8,128)(2,1)S(1)}, u32[]{:S(2)}, u32[]{:S(2)}) collective-permute-start(bf16[48,8,128]{2,1,0:T(8,128)(2,1)} %copy-done.42), channel_id=1, source_target_pairs={{0,10},{1,11},{2,8},{3,9},{4,14},{5,15},{6,12},{7,13},{8,2},{9,3},... | collective-permute-start | bytes 294920 | tf_op jit(solution)/shard_map/ppermute | solution.py:313
  136.3 28.5 %collective-permute-start.22 = (bf16[48,8,128]{2,1,0:T(8,128)(2,1)}, bf16[48,8,128]{2,1,0:T(8,128)(2,1)}, u32[]{:S(2)}, u32[]{:S(2)}) collective-permute-start(bf16[48,8,128]{2,1,0:T(8,128)(2,1)} %copy-done.41), channel_id=1, source_target_pairs={{0,11},{1,10},{2,9},{3,8},{4,15},{5,14},{6,13},{7,12},{8,3},{9,2},... | collective-permute-start | bytes 294920 | tf_op jit(solution)/shard_map/ppermute | solution.py:313
  162.3 28.5 %collective-permute-start.17 = (f32[3,64,256]{2,1,0:T(8,128)S(1)}, f32[3,64,256]{2,1,0:T(8,128)S(1)}, u32[]{:S(2)}, u32[]{:S(2)}) collective-permute-start(f32[3,64,256]{2,1,0:T(8,128)S(1)} %get-tuple-element.71), channel_id=1, source_target_pairs={{3,0},{0,1},{1,4},{4,5},{5,8},{8,9},{9,12},{12,13},{13,14},{14,15}... | collective-permute-start | bytes 589832 | tf_op jit(solution)/shard_map/ppermute | solution.py:332
  162.4 16.1 %collective-permute-start.23 = (bf16[48,8,128]{2,1,0:T(8,128)(2,1)S(1)}, bf16[48,8,128]{2,1,0:T(8,128)(2,1)S(1)}, u32[]{:S(2)}, u32[]{:S(2)}) collective-permute-start(bf16[48,8,128]{2,1,0:T(8,128)(2,1)S(1)} %copy-done.40), channel_id=1, source_target_pairs={{0,12},{1,13},{2,14},{3,15},{4,8},{5,9},{6,10},{7,11},{8,4},{9,5},... | collective-permute-start | bytes 294920 | tf_op jit(solution)/shard_map/ppermute | solution.py:313
  163.8 14.7 %collective-permute-start.24 = (bf16[48,8,128]{2,1,0:T(8,128)(2,1)S(1)}, bf16[48,8,128]{2,1,0:T(8,128)(2,1)S(1)}, u32[]{:S(2)}, u32[]{:S(2)}) collective-permute-start(bf16[48,8,128]{2,1,0:T(8,128)(2,1)S(1)} %copy-done.38), channel_id=1, source_target_pairs={{0,13},{1,12},{2,15},{3,14},{4,9},{5,8},{6,11},{7,10},{8,5},{9,4},... | collective-permute-start | bytes 294920 | tf_op jit(solution)/shard_map/ppermute | solution.py:313
  164.5 19.4 %collective-permute-start.25 = (bf16[48,8,128]{2,1,0:T(8,128)(2,1)S(1)}, bf16[48,8,128]{2,1,0:T(8,128)(2,1)S(1)}, u32[]{:S(2)}, u32[]{:S(2)}) collective-permute-start(bf16[48,8,128]{2,1,0:T(8,128)(2,1)S(1)} %copy-done.36), channel_id=1, source_target_pairs={{0,14},{1,15},{2,12},{3,13},{4,10},{5,11},{6,8},{7,9},{8,6},{9,7},... | collective-permute-start | bytes 294920 | tf_op jit(solution)/shard_map/ppermute | solution.py:313
  164.9 19.3 %collective-permute-start.26 = (bf16[48,8,128]{2,1,0:T(8,128)(2,1)S(1)}, bf16[48,8,128]{2,1,0:T(8,128)(2,1)S(1)}, u32[]{:S(2)}, u32[]{:S(2)}) collective-permute-start(bf16[48,8,128]{2,1,0:T(8,128)(2,1)S(1)} %copy-done.34), channel_id=1, source_target_pairs={{0,15},{1,14},{2,13},{3,12},{4,11},{5,10},{6,9},{7,8},{8,7},{9,6},... | collective-permute-start | bytes 294920 | tf_op jit(solution)/shard_map/ppermute | solution.py:313
  178.5 12.3 %collective-permute-start = (f32[4,64,256]{2,1,0:T(8,128)S(1)}, f32[4,64,256]{2,1,0:T(8,128)S(1)}, u32[]{:S(2)}, u32[]{:S(2)}) collective-permute-start(f32[4,64,256]{2,1,0:T(8,128)S(1)} %get-tuple-element.51), channel_id=1, source_target_pairs={{3,0},{0,1},{1,4},{4,5},{5,8},{8,9},{9,12},{12,13},{13,14},{14,15}... | collective-permute-start | bytes 786440 | tf_op jit(solution)/shard_map/ppermute | solution.py:332
  178.5 12.3 %collective-permute-start.1 = (f32[4,64,256]{2,1,0:T(8,128)S(1)}, f32[4,64,256]{2,1,0:T(8,128)S(1)}, u32[]{:S(2)}, u32[]{:S(2)}) collective-permute-start(f32[4,64,256]{2,1,0:T(8,128)S(1)} %get-tuple-element.52), channel_id=1, source_target_pairs={{0,3},{1,0},{4,1},{5,4},{8,5},{9,8},{12,9},{13,12},{14,13},{15,14}... | collective-permute-start | bytes 786440 | tf_op jit(solution)/shard_map/ppermute | solution.py:331
  (63 other events, 725.7 us)

commit v3 on v2

--- a/solution.py
+++ b/solution.py
@@ -22,6 +22,22 @@
         return device
     column, side, core = device // 4, (device // 2) % 2, device % 2
     return side * (group // 2) + 2 * (column + side * (group // 4 - 1 - 2 * column)) + core
+
+
+def shifted(device, m, group, sign=1):
+    if group % 4:
+        return (device + sign * m) % group
+    return ((device // 4 + sign * (m // 4)) % (group // 4)) * 4 + ((device % 4) ^ (m % 4))
+
+
+def started(group):
+    steps = group // 4 if group % 4 == 0 else group
+    width = group // steps
+    half = steps // 2
+    order = [c for n in range(1, half) for c in (steps - n, n)]
+    order += [c for c in range(1, steps) if c not in order]
+    ahead = [m for c in order[:-1] for m in range(c * width, (c + 1) * width)]
+    return ahead, list(range(1, width)), list(range(order[-1] * width, (order[-1] + 1) * width))
 
 
 def device_at(group):
@@ -84,7 +100,7 @@
             pltpu.SemaphoreType.DMA((parts,)),
             pltpu.SemaphoreType.DMA((parts, group)),
         ],
-        compiler_params=pltpu.CompilerParams(vmem_limit_bytes=24 << 20),
+        compiler_params=pltpu.CompilerParams(vmem_limit_bytes=12 << 20),
         name="bulk_cut",
     )(owner, down, across, cells)
 
@@ -100,25 +116,26 @@
     piece = (held * planes, rows, side)
     return pl.pallas_call(
         cut_kernel,
-        out_shape=[jax.ShapeDtypeStruct(piece, cells.dtype)] * group,
+        out_shape=[pltpu.HBM(piece, cells.dtype)] * group,
         grid_spec=pltpu.PrefetchScalarGridSpec(
             num_scalar_prefetch=1,
             grid=(1,),
             in_specs=[pl.BlockSpec((held, 1, planes, group, rows, side), lambda i, strips: (0, date, 0, 0, 0, 0))],
             out_specs=[pl.BlockSpec(piece, lambda i, strips: (0, 0, 0))] * group,
         ),
-        compiler_params=pltpu.CompilerParams(vmem_limit_bytes=16 << 20),
+        compiler_params=pltpu.CompilerParams(vmem_limit_bytes=10 << 20),
         name="cut",
     )(strips, cells)
 
 
-def gather(place_ref, share_ref, pieces, comps, base, held):
+def gather(place_ref, share_ref, pieces, fetches, comps, names, held):
     span, planes = len(comps), comps[0].shape[1]
-    for m, piece in enumerate(pieces):
-
-        def add(k, carry, m=m, piece=piece):
-            place = place_ref[(base + m) * held + k]
-            share = share_ref[(base + m) * held + k]
+    for name, piece, fetch in zip(names, pieces, fetches):
+        fetch.wait()
+
+        def add(k, carry, name=name, piece=piece):
+            place = place_ref[name * held + k]
+            share = share_ref[name * held + k]
             for d, comp in enumerate(comps):
                 for q in range(planes):
                     comp[place, q] += piece[(k * span + d) * planes + q].astype(jnp.float32) * share
@@ -127,10 +144,18 @@
         lax.fori_loop(0, held, add, 0, unroll=4)
 
 
-def box_sums(strip, comps, window_ref, sums_ref, own_ref, up_ref, down_ref, group, skip):
+def start_all(sources, buf_ref, sems):
+    fetches = [pltpu.make_async_copy(source, buf_ref.at[m], sems.at[m]) for m, source in enumerate(sources)]
+    for fetch in fetches:
+        fetch.start()
+    return [buf_ref.at[m] for m in range(len(sources))], fetches
+
+
+def box_sums(strip, comps, window_ref, window_copy, sums_ref, own_ref, up_ref, down_ref, group, skip):
     slots, _, rows, side = comps[0].shape
     lines = slots // WIDE
     step = min(lines, 16)
+    window_copy.wait()
     window = window_ref[...]
 
     def row_of(comp, q, at):
@@ -177,32 +202,47 @@
         down_ref[f] = jnp.where(strip == group - 1, down_next, down)
 
 
-def bulk_step_kernel(strip_ref, place_ref, share_ref, got_ref, window_ref, kept_ref, own_ref, up_ref, down_ref, sums_ref, *fresh, group, held):
-    comps = [*fresh, kept_ref]
+def begin(window_hbm, window_ref, window_sem, sources, buf_ref, sems, comps):
+    views, fetches = start_all(sources, buf_ref, sems)
+    window_copy = pltpu.make_async_copy(window_hbm, window_ref, window_sem)
+    window_copy.start()
     for comp in comps:
         comp[...] = jnp.zeros(comp.shape, jnp.float32)
-    gather(place_ref, share_ref, [got_ref.at[m] for m in range(group)], comps, 0, held)
-    box_sums(strip_ref[0], comps, window_ref, sums_ref, own_ref, up_ref, down_ref, group, 0)
+    return views, fetches, window_copy
+
+
+def bulk_step_kernel(strip_ref, place_ref, share_ref, got_ref, window_hbm, kept_ref, own_ref, up_ref, down_ref, *scratch, group, held):
+    window_ref, window_sem, buf_ref, sems, sums_ref, *fresh = scratch
+    comps = [*fresh, kept_ref]
+    sources = [got_ref.at[m] for m in range(group)]
+    views, fetches, window_copy = begin(window_hbm, window_ref, window_sem, sources, buf_ref, sems, comps)
+    gather(place_ref, share_ref, views, fetches, comps, range(group), held)
+    box_sums(strip_ref[0], comps, window_ref, window_copy, sums_ref, own_ref, up_ref, down_ref, group, 0)
 
 
 def step_kernel(strip_ref, place_ref, share_ref, *refs, group, held):
-    pieces, (window_ref, before_ref, comp, own_ref, up_ref, down_ref, sums_ref) = refs[:-7], refs[-7:]
-    comp[...] = jnp.zeros(comp.shape, jnp.float32)
-    gather(place_ref, share_ref, pieces, [comp], 0, held)
-    box_sums(strip_ref[0], [before_ref, comp], window_ref, sums_ref, own_ref, up_ref, down_ref, group, 1)
-
-
-def part_kernel(place_ref, share_ref, *refs, base, held):
-    pieces, comp = refs[:-1], refs[-1]
-    comp[...] = jnp.zeros(comp.shape, jnp.float32)
-    gather(place_ref, share_ref, pieces, [comp], base, held)
-
-
-def last_step_kernel(strip_ref, place_ref, share_ref, *refs, group, base, held):
-    pieces, (window_ref, before_ref, part_ref, comp, own_ref, up_ref, down_ref, sums_ref) = refs[:-8], refs[-8:]
-    del part_ref
-    gather(place_ref, share_ref, pieces, [comp], base, held)
-    box_sums(strip_ref[0], [before_ref, comp], window_ref, sums_ref, own_ref, up_ref, down_ref, group, 1)
+    pieces, (window_hbm, before_ref, comp, own_ref, up_ref, down_ref) = refs[:group], refs[group : group + 6]
+    window_ref, window_sem, buf_ref, sems, sums_ref = refs[group + 6 :]
+    views, fetches, window_copy = begin(window_hbm, window_ref, window_sem, pieces, buf_ref, sems, [comp])
+    gather(place_ref, share_ref, views, fetches, [comp], range(group), held)
+    box_sums(strip_ref[0], [before_ref, comp], window_ref, window_copy, sums_ref, own_ref, up_ref, down_ref, group, 1)
+
+
+def part_kernel(place_ref, share_ref, *refs, names, held):
+    pieces, (*old, comp, buf_ref, sems) = refs[: len(names)], refs[len(names) :]
+    views, fetches = start_all(pieces, buf_ref, sems)
+    if not old:
+        comp[...] = jnp.zeros(comp.shape, jnp.float32)
+    gather(place_ref, share_ref, views, fetches, [comp], names, held)
+
+
+def last_step_kernel(strip_ref, place_ref, share_ref, *refs, group, names, held):
+    many = len(names)
+    pieces, (window_hbm, before_ref, _, comp, own_ref, up_ref, down_ref) = refs[:many], refs[many : many + 7]
+    window_ref, window_sem, buf_ref, sems, sums_ref = refs[many + 7 :]
+    views, fetches, window_copy = begin(window_hbm, window_ref, window_sem, pieces, buf_ref, sems, [])
+    gather(place_ref, share_ref, views, fetches, [comp], names, held)
+    box_sums(strip_ref[0], [before_ref, comp], window_ref, window_copy, sums_ref, own_ref, up_ref, down_ref, group, 1)
 
 
 def sums_of(fields, rows, lines, cols):
@@ -210,14 +250,14 @@
     return [jax.ShapeDtypeStruct(s, jnp.float32) for s in outs], pltpu.VMEM((fields, cols // LANES, lines * rows, LANES), jnp.float32)
 
 
-def call(kernel, prefetch, args, outs, scratch=(), aliases=None, mib=16):
+def call(kernel, prefetch, args, outs, scratch=(), aliases=None, mib=12, remote=0):
     return pl.pallas_call(
         kernel,
         out_shape=outs,
         grid_spec=pltpu.PrefetchScalarGridSpec(
             num_scalar_prefetch=len(prefetch),
             grid=(),
-            in_specs=[VMEM] * len(args),
+            in_specs=[HBM] * remote + [VMEM] * (len(args) - remote),
             out_specs=[VMEM] * len(outs),
             scratch_shapes=list(scratch),
         ),
@@ -302,7 +342,7 @@
     ]
     bulk = bulk_cut(*words, cells, span)
     got = lax.all_to_all(bulk, "grid", split_axis=0, concat_axis=0, tiled=True)
-    strips = strip_of(me ^ devices, group)
+    strips = strip_of(shifted(me, devices, group), group)
 
     def scatter(date, after=None):
         sends = cut(strips, cells, date)
@@ -310,7 +350,7 @@
             sends, _ = lax.optimization_barrier((sends, after))
         pieces = [sends[0]] + [None] * (group - 1)
         for m in range(1, group):
-            pieces[m] = lax.ppermute(sends[m], "grid", [(i, i ^ m) for i in range(group)])
+            pieces[m] = lax.ppermute(sends[m], "grid", [(i, shifted(i, m, group)) for i in range(group)])
         return pieces
 
     pieces_b = scatter(dates - 2)
@@ -325,12 +365,18 @@
     counts = jnp.sum((flat[:, None] == flat[None, :]).astype(jnp.int32), axis=1)
     shares = 1.0 / jnp.maximum(counts, 1).astype(jnp.float32)
     tables = (flat, shares)
-    swapped = tuple(t.reshape(group, held)[me ^ devices].reshape(group * held) for t in tables)
+    swapped = tuple(t.reshape(group, held)[shifted(me, devices, group, -1)].reshape(group * held) for t in tables)
+    tables, swapped = lax.optimization_barrier((tables, swapped))
 
     def exchange(up, down):
         below = lax.ppermute(up, "grid", [(at[s], at[s - 1]) for s in range(group)])
         above = lax.ppermute(down, "grid", [(at[s - 1], at[s]) for s in range(group)])
         return above, below
+
+    window_bufs = [pltpu.VMEM(window.shape, window.dtype), pltpu.SemaphoreType.DMA(())]
+
+    def piece_bufs(many):
+        return [pltpu.VMEM((many, *pieces[0].shape), pieces[0].dtype), pltpu.SemaphoreType.DMA((many,))]
 
     comp = pltpu.VMEM((lines * WIDE, planes, rows, side), jnp.float32)
     out_cols = cols // 4
@@ -338,14 +384,16 @@
     outs, sums = sums_of(3 * span - 2, rows, lines, out_cols)
     kept, own, up, down = call(
         functools.partial(bulk_step_kernel, group=group, held=held),
-        (strips, *tables), (got, window), [comp, *outs], [sums] + [comp] * (span - 1),
-        mib=32,
+        (strips, *tables), (got, window), [comp, *outs],
+        [*window_bufs, pltpu.VMEM(got.shape, got.dtype), pltpu.SemaphoreType.DMA((group,)), sums] + [comp] * (span - 1),
+        mib=16, remote=2,
     )
     above, below = exchange(up, down)
     outs, sums = sums_of(3, rows, lines, out_cols)
     kept, *next_sums = call(
         functools.partial(step_kernel, group=group, held=held),
-        (strips, *swapped), (*pieces_b, window, kept), [comp, *outs], [sums],
+        (strips, *swapped), (*pieces_b, window, kept), [comp, *outs],
+        [*window_bufs, *piece_bufs(group), sums], remote=group + 1,
     )
     next_own, up, down = next_sums
     next_above, next_below = exchange(up, down)
@@ -360,12 +408,22 @@
     if LATE:
         first = lax.all_to_all(dealt, "grid", split_axis=0, concat_axis=0, tiled=True)
 
-    near = group // 2
-    (part,) = call(functools.partial(part_kernel, base=0, held=held), swapped, pieces[:near], [comp])
-    far = pieces[near:]
+    ahead, level, late = started(group)
+    near, middle, far = [0, *level, *ahead[: len(ahead) // 2]], ahead[len(ahead) // 2 :], late
+    (part,) = call(
+        functools.partial(part_kernel, names=near, held=held), swapped, [pieces[m] for m in near], [comp],
+        piece_bufs(len(near)), remote=len(near),
+    )
+    (part,) = call(
+        functools.partial(part_kernel, names=middle, held=held), swapped, (*[pieces[m] for m in middle], part), [comp],
+        piece_bufs(len(middle)), aliases={2 + len(middle): 0}, remote=len(middle),
+    )
+    far_pieces = [pieces[m] for m in far]
     _, own, up, down = call(
-        functools.partial(last_step_kernel, group=group, base=near, held=held),
-        (strips, *swapped), (*far, window, kept, part), [comp, *outs], [sums], aliases={3 + len(far) + 2: 0},
+        functools.partial(last_step_kernel, group=group, names=far, held=held),
+        (strips, *swapped), (*far_pieces, window, kept, part), [comp, *outs],
+        [*window_bufs, *piece_bufs(len(far)), sums], aliases={3 + len(far) + 2: 0},
+        remote=len(far) + 1,
     )
     above, below = exchange(up, down)
     (last,) = call(

time: 215 us -> 211 us (0.981)
  local copies, waits for them, and re-layouts: 32.8 us -> 15.2 us
  starting transfers between devices: 48 us -> 57.8 us
  Pallas kernels: 30.4 us -> 36.8 us
  waiting for transfers between devices: 83.4 us -> 80.5 us
    unnamed x116 -> x58, local copies, waits for them, and re-layouts: 30.7 us -> 13.2 us
    ppermute x30, starting transfers between devices: 36.6 us -> 43.5 us  [scatter(): lax.ppermute(sends[m], 'grid', [(i, shifted(i, m, group)) for i in range(...]
    pallas_call x7 -> x8, Pallas kernels: 21.2 us -> 26 us  [call(): pl.pallas_call(kernel, out_shape=outs, grid_spec=pltpu.PrefetchScalarGrid...]
    ppermute x3, starting transfers between devices: 1.83 us -> 4.75 us  [exchange(): lax.ppermute(down, 'grid', [(at[s - 1], at[s]) for s in range(group)])]
    ppermute x30, waiting for transfers between devices: 78.5 us -> 75.6 us  [scatter(): lax.ppermute(sends[m], 'grid', [(i, shifted(i, m, group)) for i in range(...]
  transfers between devices with their start and end apart: 37 -> 37, of which waited for: 9 -> 8; matrix products, arithmetic and copies ran while one was open for 2% -> 2% of each run, Pallas kernels for 12% -> 15%
where the time goes in v3:
time: 211 us; the launch traced here: 208 us
  waiting for transfers between devices  80.5 us (38%)
  starting transfers between devices  57.8 us (27%)
  Pallas kernels  36.8 us (17%)
  local copies, waits for them, and re-layouts  15.2 us (7%)
  blocking collectives  15.1 us (7%)
    ppermute x30, waiting for transfers between devices, scatter(): lax.ppermute(sends[m], 'grid', [(i, shifted(i, m, group)) for i in range(...  75.6 us
    ppermute x30, starting transfers between devices, scatter(): lax.ppermute(sends[m], 'grid', [(i, shifted(i, m, group)) for i in range(...  43.5 us
    pallas_call x8, Pallas kernels, call(): pl.pallas_call(kernel, out_shape=outs, grid_spec=pltpu.PrefetchScalarGrid...  26 us
    all_to_all x1, blocking collectives, local(): lax.all_to_all(last, 'grid', split_axis=0, concat_axis=0, tiled=True)  15.1 us
    unnamed x58, local copies, waits for them, and re-layouts  13.2 us
    pallas_call x2, Pallas kernels, cut(): pl.pallas_call(cut_kernel, out_shape=[pltpu.HBM(piece, cells.dtype)] * gr...  7.06 us
    all_to_all x1, starting transfers between devices, local(): got = lax.all_to_all(bulk, 'grid', split_axis=0, concat_axis=0, tiled=True)  6.53 us
    ppermute x3, starting transfers between devices, exchange(): lax.ppermute(down, 'grid', [(at[s - 1], at[s]) for s in range(group)])  4.75 us
  transfers between devices with their start and end apart: 37, of which 8 were waited for; matrix products, arithmetic and copies ran while one was open for 2% of the time, Pallas kernels for 15%

profile of v3, /device:TPU:13, one launch (start us, length us, event | category | flops | bytes accessed | tf_op | source)
XLA Modules:
  0.0 207.6 jit_solution(6420886426647826564)
XLA Ops:
  0.0 3.8 %bulk_cut.1 = bf16[16,97,8,128]{3,2,1,0:T(8,128)(2,1)} custom-call(s32[1,24]{1,0:T(1,128)} %bitcast.16, s32[1,24]{1,0:T(1,128)} %bitcast.17, s32[1,24]{1,0:T(1,128)} %bitcast.18, bf16[24,4,2,16,8,128]{5,4,3,2,1,0:T(8,128)(2,1)} %bitcast.12), custom_call_target="tpu_custom_call" | custom-call | tf_op jit(solution)/shard_map/bulk_cut/pallas_call | solution.py:89
  3.8 6.5 %all-to-all-start = ((bf16[16,97,8,128]{3,2,1,0:T(8,128)(2,1)}), bf16[16,97,8,128]{3,2,1,0:T(8,128)(2,1)S(1)}, u32[]{:S(2)}, u32[]{:S(2)}) async-start(bf16[16,97,8,128]{3,2,1,0:T(8,128)(2,1)} %bulk_cut.1), calls=%async_computation | async-start | bytes 6356992 | tf_op jit(solution)/shard_map/all_to_all | solution.py:344
  10.3 3.6 %cut.2 = (bf16[48,8,128]{2,1,0:T(8,128)(2,1)}, bf16[48,8,128]{2,1,0:T(8,128)(2,1)}, bf16[48,8,128]{2,1,0:T(8,128)(2,1)}, bf16[48,8,128]{2,1,0:T(8,128)(2,1)}, bf...) custom-call(s32[16]{0:T(128)S(1)} %fusion.7.strip_ref, ...), custom_call_target="tpu_custom_call" | custom-call | tf_op jit(solution)/shard_map/cut/pallas_call | solution.py:117
  13.9 2.4 %collective-permute-start.10 = (bf16[48,8,128]{2,1,0:T(8,128)(2,1)}, bf16[48,8,128]{2,1,0:T(8,128)(2,1)S(1)}, u32[]{:S(2)}, u32[]{:S(2)}) collective-permute-start(bf16[48,8,128]{2,1,0:T(8,128)(2,1)} %get-tuple-element.70), channel_id=1, source_target_pairs={{0,9},{1,8},{2,11},{3,10},{4,13},{5,12},{6,15},{7,14},{8,1},{9,0},... | collective-permute-start | bytes 294920 | tf_op jit(solution)/shard_map/ppermute | solution.py:353
  16.6 3.3 %collective-permute-start.12 = (bf16[48,8,128]{2,1,0:T(8,128)(2,1)}, bf16[48,8,128]{2,1,0:T(8,128)(2,1)S(1)}, u32[]{:S(2)}, u32[]{:S(2)}) collective-permute-start(bf16[48,8,128]{2,1,0:T(8,128)(2,1)} %get-tuple-element.72), channel_id=1, source_target_pairs={{0,11},{1,10},{2,9},{3,8},{4,15},{5,14},{6,13},{7,12},{8,3},{9,2},... | collective-permute-start | bytes 294920 | tf_op jit(solution)/shard_map/ppermute | solution.py:353
  20.1 1.5 collective-permute-start.14
  21.6 3.5 %cut.3 = (bf16[48,8,128]{2,1,0:T(8,128)(2,1)}, bf16[48,8,128]{2,1,0:T(8,128)(2,1)}, bf16[48,8,128]{2,1,0:T(8,128)(2,1)}, bf16[48,8,128]{2,1,0:T(8,128)(2,1)}, bf...) custom-call(s32[16]{0:T(128)S(1)} %fusion.7.strip_ref, ...), custom_call_target="tpu_custom_call" | custom-call | tf_op jit(solution)/shard_map/cut/pallas_call | solution.py:117
  26.1 65.2 %collective-permute-done.10.refs_9_ = bf16[48,8,128]{2,1,0:T(8,128)(2,1)S(1)} collective-permute-done((bf16[48,8,128]{2,1,0:T(8,128)(2,1)}, bf16[48,8,128]{2,1,0:T(8,128)(2,1)S(1)}, u32[]{:S(2)}, u32[]{:S(2)}) %collective-permute-start.10) | collective-permute-done | bytes 98336 | tf_op jit(solution)/shard_map/ppermute | solution.py:353
  91.3 2.1 %collective-permute-done.11.refs_10_ = bf16[48,8,128]{2,1,0:T(8,128)(2,1)S(1)} collective-permute-done((bf16[48,8,128]{2,1,0:T(8,128)(2,1)}, bf16[48,8,128]{2,1,0:T(8,128)(2,1)S(1)}, u32[]{:S(2)}, u32[]{:S(2)}) %collective-permute-start.11) | collective-permute-done | bytes 98336 | tf_op jit(solution)/shard_map/ppermute | solution.py:353
  94.1 3.5 %collective-permute-start.16 = (bf16[48,8,128]{2,1,0:T(8,128)(2,1)}, bf16[48,8,128]{2,1,0:T(8,128)(2,1)S(1)}, u32[]{:S(2)}, u32[]{:S(2)}) collective-permute-start(bf16[48,8,128]{2,1,0:T(8,128)(2,1)} %get-tuple-element.76), channel_id=1, source_target_pairs={{0,15},{1,14},{2,13},{3,12},{4,3},{5,2},{6,1},{7,0},{8,7},{9,6},{1... | collective-permute-start | bytes 294920 | tf_op jit(solution)/shard_map/ppermute | solution.py:353
  102.6 1.9 collective-permute-start.6
  104.5 3.1 %collective-permute-start.7 = (bf16[48,8,128]{2,1,0:T(8,128)(2,1)}, bf16[48,8,128]{2,1,0:T(8,128)(2,1)}, u32[]{:S(2)}, u32[]{:S(2)}) collective-permute-start(bf16[48,8,128]{2,1,0:T(8,128)(2,1)} %get-tuple-element.67), channel_id=1, source_target_pairs={{0,6},{1,7},{2,4},{3,5},{4,10},{5,11},{6,8},{7,9},{8,14},{9,15},{1... | collective-permute-start | bytes 294920 | tf_op jit(solution)/shard_map/ppermute | solution.py:353
  110.9 1.9 collective-permute-start.28
  114.1 3.4 %collective-permute-start.30 = (bf16[48,8,128]{2,1,0:T(8,128)(2,1)}, bf16[48,8,128]{2,1,0:T(8,128)(2,1)S(1)}, u32[]{:S(2)}, u32[]{:S(2)}) collective-permute-start(bf16[48,8,128]{2,1,0:T(8,128)(2,1)} %get-tuple-element.95), channel_id=1, source_target_pairs={{0,12},{1,13},{2,14},{3,15},{4,0},{5,1},{6,2},{7,3},{8,4},{9,5},{1... | collective-permute-start | bytes 294920 | tf_op jit(solution)/shard_map/ppermute | solution.py:353
  118.7 3.8 %collective-permute-start.31 = (bf16[48,8,128]{2,1,0:T(8,128)(2,1)}, bf16[48,8,128]{2,1,0:T(8,128)(2,1)}, u32[]{:S(2)}, u32[]{:S(2)}) collective-permute-start(bf16[48,8,128]{2,1,0:T(8,128)(2,1)} %get-tuple-element.96), channel_id=1, source_target_pairs={{0,13},{1,12},{2,15},{3,14},{4,1},{5,0},{6,3},{7,2},{8,5},{9,4},{1... | collective-permute-start | bytes 294920 | tf_op jit(solution)/shard_map/ppermute | solution.py:353
  123.7 1.6 collective-permute-start.33
  127.7 1.7 collective-permute-start.24
  131.9 10.6 %shard_map.46 = (f32[512,2,8,128]{3,2,1,0:T(8,128)S(1)}, f32[4,2,64,256]{3,2,1,0:T(8,128)S(1)}, f32[4,64,256]{2,1,0:T(8,128)S(1)}, f32[4,64,256]{2,1,0:T(8,128)S(1)}) custom-call(s32[16]{0:T(128)S(1)} %fusion.7.strip_ref, s32[384]{0:T(512)S(1)} %add.167.place_ref, f32[384]{0:T(512)S(1)} %convert_divide_fusion.share_ref, ...), custom_call_target="tpu_custom_call" | custom-call | tf_op jit(solution)/shard_map/pallas_call | solution.py:254
  143.0 2.1 %collective-permute-start.26 = (bf16[48,8,128]{2,1,0:T(8,128)(2,1)}, bf16[48,8,128]{2,1,0:T(8,128)(2,1)S(1)}, u32[]{:S(2)}, u32[]{:S(2)}) collective-permute-start(bf16[48,8,128]{2,1,0:T(8,128)(2,1)} %get-tuple-element.90), channel_id=1, source_target_pairs={{0,7},{1,6},{2,5},{3,4},{4,11},{5,10},{6,9},{7,8},{8,15},{9,14},{1... | collective-permute-start | bytes 294920 | tf_op jit(solution)/shard_map/ppermute | solution.py:353
  151.5 6.1 %shard_map.47 = (f32[512,2,8,128]{3,2,1,0:T(8,128)S(1)}, f32[3,2,64,256]{3,2,1,0:T(8,128)S(1)}, f32[3,64,256]{2,1,0:T(8,128)S(1)}, f32[3,64,256]{2,1,0:T(8,128)S(1)}) custom-call(s32[16]{0:T(128)S(1)} %fusion.7.strip_ref, s32[384]{0:T(512)S(1)} %reshape.176.place_ref, f32[384]{0:T(512)S(1)} %reshape.177.share_ref, bf16[48,8,128]{2,1,0:T(8,128)(2,1)S(1)} %copy-done.4, ...), custom_call_target="tpu_custom_call" | custom-call | tf_op jit(solution)/shard_map/pallas_call | solution.py:254
  157.8 2.1 %collective-permute-start.19 = (bf16[48,8,128]{2,1,0:T(8,128)(2,1)S(1)}, bf16[48,8,128]{2,1,0:T(8,128)(2,1)S(1)}, u32[]{:S(2)}, u32[]{:S(2)}) collective-permute-start(bf16[48,8,128]{2,1,0:T(8,128)(2,1)S(1)} %copy-done.28), channel_id=1, source_target_pairs={{0,8},{1,9},{2,10},{3,11},{4,12},{5,13},{6,14},{7,15},{8,0},{9,1},... | collective-permute-start | bytes 294920 | tf_op jit(solution)/shard_map/ppermute | solution.py:353
  160.7 2.1 %collective-permute-start.21 = (bf16[48,8,128]{2,1,0:T(8,128)(2,1)S(1)}, bf16[48,8,128]{2,1,0:T(8,128)(2,1)S(1)}, u32[]{:S(2)}, u32[]{:S(2)}) collective-permute-start(bf16[48,8,128]{2,1,0:T(8,128)(2,1)S(1)} %copy-done.26), channel_id=1, source_target_pairs={{0,10},{1,11},{2,8},{3,9},{4,14},{5,15},{6,12},{7,13},{8,2},{9,3},... | collective-permute-start | bytes 294920 | tf_op jit(solution)/shard_map/ppermute | solution.py:353
  164.1 6.5 %collective-permute-done.19.refs_0_ = bf16[48,8,128]{2,1,0:T(8,128)(2,1)S(1)} collective-permute-done((bf16[48,8,128]{2,1,0:T(8,128)(2,1)S(1)}, bf16[48,8,128]{2,1,0:T(8,128)(2,1)S(1)}, u32[]{:S(2)}, u32[]{:S(2)}) %collective-permute-start.19) | collective-permute-done | bytes 98336 | tf_op jit(solution)/shard_map/ppermute | solution.py:353
  170.6 2.6 %collective-permute-start = (f32[4,64,256]{2,1,0:T(8,128)S(1)}, f32[4,64,256]{2,1,0:T(8,128)S(1)}, u32[]{:S(2)}, u32[]{:S(2)}) collective-permute-start(f32[4,64,256]{2,1,0:T(8,128)S(1)} %get-tuple-element.57), channel_id=1, source_target_pairs={{3,0},{0,1},{1,4},{4,5},{5,8},{8,9},{9,12},{12,13},{13,14},{14,15}... | collective-permute-start | bytes 786440 | tf_op jit(solution)/shard_map/ppermute | solution.py:373
  173.7 2.5 %shard_map.49.refs_4_ = f32[512,2,8,128]{3,2,1,0:T(8,128)S(1)} custom-call(s32[384]{0:T(512)S(1)} %reshape.176.place_ref, f32[384]{0:T(512)S(1)} %reshape.177.share_ref, bf16[48,8,128]{2,1,0:T(8,128)(2,1)S(1)} %copy-done.3, bf16[48,8,128]{2,1,0:T(8,128)(2,1)S(1)} %copy-done.16, bf16[48,8,128]{2,1,0:T(8,128)(2,1)S(1)} %copy-done.18, ...), custom_call_target="tpu_custom_call" | custom-call | tf_op jit(solution)/shard_map/pallas_call | solution.py:254
  176.2 1.5 shard_map.50.refs_6_
  177.7 2.5 %collective-permute-start.18 = (f32[3,64,256]{2,1,0:T(8,128)S(1)}, f32[3,64,256]{2,1,0:T(8,128)S(1)}, u32[]{:S(2)}, u32[]{:S(2)}) collective-permute-start(f32[3,64,256]{2,1,0:T(8,128)S(1)} %get-tuple-element.80), channel_id=1, source_target_pairs={{0,3},{1,0},{4,1},{5,4},{8,5},{9,8},{12,9},{13,12},{14,13},{15,14}... | collective-permute-start | bytes 589832 | tf_op jit(solution)/shard_map/ppermute | solution.py:372
  180.2 4.1 %shard_map.51 = (f32[512,2,8,128]{3,2,1,0:T(8,128)S(1)}, f32[3,2,64,256]{3,2,1,0:T(8,128)S(1)}, f32[3,64,256]{2,1,0:T(8,128)S(1)}, f32[3,64,256]{2,1,0:T(8,128)S(1)}) custom-call(s32[16]{0:T(128)S(1)} %fusion.7.strip_ref, s32[384]{0:T(512)S(1)} %reshape.176.place_ref, f32[384]{0:T(512)S(1)} %reshape.177.share_ref, ...), custom_call_target="tpu_custom_call", output_to_operand_aliasing={{0}: (9, {})} | custom-call | tf_op jit(solution)/shard_map/pallas_call | solution.py:254
  184.3 2.0 collective-permute-start.34
  186.6 2.3 %collective-permute-done.34.above_ref = f32[3,64,256]{2,1,0:T(8,128)S(1)} collective-permute-done((f32[3,64,256]{2,1,0:T(8,128)S(1)}, f32[3,64,256]{2,1,0:T(8,128)S(1)}, u32[]{:S(2)}, u32[]{:S(2)}) %collective-permute-start.34) | collective-permute-done | bytes 196640 | tf_op jit(solution)/shard_map/ppermute | solution.py:373
  188.9 2.5 %collective-permute-done.35.below_ref = f32[3,64,256]{2,1,0:T(8,128)S(1)} collective-permute-done((f32[3,64,256]{2,1,0:T(8,128)S(1)}, f32[3,64,256]{2,1,0:T(8,128)S(1)}, u32[]{:S(2)}, u32[]{:S(2)}) %collective-permute-start.35) | collective-permute-done | bytes 196640 | tf_op jit(solution)/shard_map/ppermute | solution.py:372
  191.6 15.1 %all_to_all.10.refs_0_ = f32[16,24,256]{2,1,0:T(8,128)S(1)} all-to-all(f32[16,24,256]{2,1,0:T(8,128)S(1)} %pad_maximum_fusion), channel_id=1, replica_groups=mesh['region'=2,'grid'=16] {'grid'}, dimensions={0} | all-to-all | bytes 786432 | tf_op jit(solution)/shard_map/all_to_all | solution.py:438
  (129 shorter events, 30.0 us)
Async XLA Ops:
  3.8 96.1 %all-to-all-start = ((bf16[16,97,8,128]{3,2,1,0:T(8,128)(2,1)}), bf16[16,97,8,128]{3,2,1,0:T(8,128)(2,1)S(1)}, u32[]{:S(2)}, u32[]{:S(2)}) async-start(bf16[16,97,8,128]{3,2,1,0:T(8,128)(2,1)} %bulk_cut.1), calls=%async_computation | async-start | bytes 6356992 | tf_op jit(solution)/shard_map/all_to_all | solution.py:344
  13.9 77.4 %collective-permute-start.10 = (bf16[48,8,128]{2,1,0:T(8,128)(2,1)}, bf16[48,8,128]{2,1,0:T(8,128)(2,1)S(1)}, u32[]{:S(2)}, u32[]{:S(2)}) collective-permute-start(bf16[48,8,128]{2,1,0:T(8,128)(2,1)} %get-tuple-element.70), channel_id=1, source_target_pairs={{0,9},{1,8},{2,11},{3,10},{4,13},{5,12},{6,15},{7,14},{8,1},{9,0},... | collective-permute-start | bytes 294920 | tf_op jit(solution)/shard_map/ppermute | solution.py:353
  16.3 77.2 %collective-permute-start.11 = (bf16[48,8,128]{2,1,0:T(8,128)(2,1)}, bf16[48,8,128]{2,1,0:T(8,128)(2,1)S(1)}, u32[]{:S(2)}, u32[]{:S(2)}) collective-permute-start(bf16[48,8,128]{2,1,0:T(8,128)(2,1)} %get-tuple-element.71), channel_id=1, source_target_pairs={{0,10},{1,11},{2,8},{3,9},{4,14},{5,15},{6,12},{7,13},{8,2},{9,3},... | collective-permute-start | bytes 294920 | tf_op jit(solution)/shard_map/ppermute | solution.py:353
  16.6 81.1 %collective-permute-start.12 = (bf16[48,8,128]{2,1,0:T(8,128)(2,1)}, bf16[48,8,128]{2,1,0:T(8,128)(2,1)S(1)}, u32[]{:S(2)}, u32[]{:S(2)}) collective-permute-start(bf16[48,8,128]{2,1,0:T(8,128)(2,1)} %get-tuple-element.72), channel_id=1, source_target_pairs={{0,11},{1,10},{2,9},{3,8},{4,15},{5,14},{6,13},{7,12},{8,3},{9,2},... | collective-permute-start | bytes 294920 | tf_op jit(solution)/shard_map/ppermute | solution.py:353
  19.8 79.1 %collective-permute-start.13 = (bf16[48,8,128]{2,1,0:T(8,128)(2,1)}, bf16[48,8,128]{2,1,0:T(8,128)(2,1)S(1)}, u32[]{:S(2)}, u32[]{:S(2)}) collective-permute-start(bf16[48,8,128]{2,1,0:T(8,128)(2,1)} %get-tuple-element.73), channel_id=1, source_target_pairs={{0,12},{1,13},{2,14},{3,15},{4,0},{5,1},{6,2},{7,3},{8,4},{9,5},{1... | collective-permute-start | bytes 294920 | tf_op jit(solution)/shard_map/ppermute | solution.py:353
  20.1 79.8 %collective-permute-start.14 = (bf16[48,8,128]{2,1,0:T(8,128)(2,1)}, bf16[48,8,128]{2,1,0:T(8,128)(2,1)}, u32[]{:S(2)}, u32[]{:S(2)}) collective-permute-start(bf16[48,8,128]{2,1,0:T(8,128)(2,1)} %get-tuple-element.74), channel_id=1, source_target_pairs={{0,13},{1,12},{2,15},{3,14},{4,1},{5,0},{6,3},{7,2},{8,5},{9,4},{1... | collective-permute-start | bytes 294920 | tf_op jit(solution)/shard_map/ppermute | solution.py:353
  91.3 10.0 %collective-permute-start.15 = (bf16[48,8,128]{2,1,0:T(8,128)(2,1)}, bf16[48,8,128]{2,1,0:T(8,128)(2,1)}, u32[]{:S(2)}, u32[]{:S(2)}) collective-permute-start(bf16[48,8,128]{2,1,0:T(8,128)(2,1)} %get-tuple-element.75), channel_id=1, source_target_pairs={{0,14},{1,15},{2,12},{3,13},{4,2},{5,3},{6,0},{7,1},{8,6},{9,7},{1... | collective-permute-start | bytes 294920 | tf_op jit(solution)/shard_map/ppermute | solution.py:353
  99.6 8.0 %collective-permute-start.3 = (bf16[48,8,128]{2,1,0:T(8,128)(2,1)}, bf16[48,8,128]{2,1,0:T(8,128)(2,1)}, u32[]{:S(2)}, u32[]{:S(2)}) collective-permute-start(bf16[48,8,128]{2,1,0:T(8,128)(2,1)} %get-tuple-element.63), channel_id=1, source_target_pairs={{0,2},{1,3},{2,0},{3,1},{4,6},{5,7},{6,4},{7,5},{8,10},{9,11},{10,... | collective-permute-start | bytes 294920 | tf_op jit(solution)/shard_map/ppermute | solution.py:353
  99.9 9.8 %collective-permute-start.4 = (bf16[48,8,128]{2,1,0:T(8,128)(2,1)}, bf16[48,8,128]{2,1,0:T(8,128)(2,1)}, u32[]{:S(2)}, u32[]{:S(2)}) collective-permute-start(bf16[48,8,128]{2,1,0:T(8,128)(2,1)} %get-tuple-element.64), channel_id=1, source_target_pairs={{0,3},{1,2},{2,1},{3,0},{4,7},{5,6},{6,5},{7,4},{8,11},{9,10},{10,... | collective-permute-start | bytes 294920 | tf_op jit(solution)/shard_map/ppermute | solution.py:353
  101.3 9.6 %collective-permute-start.5 = (bf16[48,8,128]{2,1,0:T(8,128)(2,1)}, bf16[48,8,128]{2,1,0:T(8,128)(2,1)}, u32[]{:S(2)}, u32[]{:S(2)}) collective-permute-start(bf16[48,8,128]{2,1,0:T(8,128)(2,1)} %get-tuple-element.65), channel_id=1, source_target_pairs={{0,4},{1,5},{2,6},{3,7},{4,8},{5,9},{6,10},{7,11},{8,12},{9,13},{1... | collective-permute-start | bytes 294920 | tf_op jit(solution)/shard_map/ppermute | solution.py:353
  102.6 8.3 %collective-permute-start.6 = (bf16[48,8,128]{2,1,0:T(8,128)(2,1)}, bf16[48,8,128]{2,1,0:T(8,128)(2,1)}, u32[]{:S(2)}, u32[]{:S(2)}) collective-permute-start(bf16[48,8,128]{2,1,0:T(8,128)(2,1)} %get-tuple-element.66), channel_id=1, source_target_pairs={{0,5},{1,4},{2,7},{3,6},{4,9},{5,8},{6,11},{7,10},{8,13},{9,12},{1... | collective-permute-start | bytes 294920 | tf_op jit(solution)/shard_map/ppermute | solution.py:353
  104.5 8.3 %collective-permute-start.7 = (bf16[48,8,128]{2,1,0:T(8,128)(2,1)}, bf16[48,8,128]{2,1,0:T(8,128)(2,1)}, u32[]{:S(2)}, u32[]{:S(2)}) collective-permute-start(bf16[48,8,128]{2,1,0:T(8,128)(2,1)} %get-tuple-element.67), channel_id=1, source_target_pairs={{0,6},{1,7},{2,4},{3,5},{4,10},{5,11},{6,8},{7,9},{8,14},{9,15},{1... | collective-permute-start | bytes 294920 | tf_op jit(solution)/shard_map/ppermute | solution.py:353
  109.8 8.2 %collective-permute-start.9 = (bf16[48,8,128]{2,1,0:T(8,128)(2,1)}, bf16[48,8,128]{2,1,0:T(8,128)(2,1)S(1)}, u32[]{:S(2)}, u32[]{:S(2)}) collective-permute-start(bf16[48,8,128]{2,1,0:T(8,128)(2,1)} %get-tuple-element.69), channel_id=1, source_target_pairs={{0,8},{1,9},{2,10},{3,11},{4,12},{5,13},{6,14},{7,15},{8,0},{9,1},... | collective-permute-start | bytes 294920 | tf_op jit(solution)/shard_map/ppermute | solution.py:353
  110.9 11.6 %collective-permute-start.27 = (bf16[48,8,128]{2,1,0:T(8,128)(2,1)}, bf16[48,8,128]{2,1,0:T(8,128)(2,1)S(1)}, u32[]{:S(2)}, u32[]{:S(2)}) collective-permute-start(bf16[48,8,128]{2,1,0:T(8,128)(2,1)} %get-tuple-element.92), channel_id=1, source_target_pairs={{0,1},{1,0},{2,3},{3,2},{4,5},{5,4},{6,7},{7,6},{8,9},{9,8},{10,11... | collective-permute-start | bytes 294920 | tf_op jit(solution)/shard_map/ppermute | solution.py:353
  110.9 12.2 %collective-permute-start.28 = (bf16[48,8,128]{2,1,0:T(8,128)(2,1)}, bf16[48,8,128]{2,1,0:T(8,128)(2,1)S(1)}, u32[]{:S(2)}, u32[]{:S(2)}) collective-permute-start(bf16[48,8,128]{2,1,0:T(8,128)(2,1)} %get-tuple-element.93), channel_id=1, source_target_pairs={{0,2},{1,3},{2,0},{3,1},{4,6},{5,7},{6,4},{7,5},{8,10},{9,11},{10,... | collective-permute-start | bytes 294920 | tf_op jit(solution)/shard_map/ppermute | solution.py:353
  112.8 12.5 %collective-permute-start.29 = (bf16[48,8,128]{2,1,0:T(8,128)(2,1)}, bf16[48,8,128]{2,1,0:T(8,128)(2,1)S(1)}, u32[]{:S(2)}, u32[]{:S(2)}) collective-permute-start(bf16[48,8,128]{2,1,0:T(8,128)(2,1)} %get-tuple-element.94), channel_id=1, source_target_pairs={{0,3},{1,2},{2,1},{3,0},{4,7},{5,6},{6,5},{7,4},{8,11},{9,10},{10,... | collective-permute-start | bytes 294920 | tf_op jit(solution)/shard_map/ppermute | solution.py:353
  114.1 13.0 %collective-permute-start.30 = (bf16[48,8,128]{2,1,0:T(8,128)(2,1)}, bf16[48,8,128]{2,1,0:T(8,128)(2,1)S(1)}, u32[]{:S(2)}, u32[]{:S(2)}) collective-permute-start(bf16[48,8,128]{2,1,0:T(8,128)(2,1)} %get-tuple-element.95), channel_id=1, source_target_pairs={{0,12},{1,13},{2,14},{3,15},{4,0},{5,1},{6,2},{7,3},{8,4},{9,5},{1... | collective-permute-start | bytes 294920 | tf_op jit(solution)/shard_map/ppermute | solution.py:353
  118.7 23.9 %collective-permute-start.31 = (bf16[48,8,128]{2,1,0:T(8,128)(2,1)}, bf16[48,8,128]{2,1,0:T(8,128)(2,1)}, u32[]{:S(2)}, u32[]{:S(2)}) collective-permute-start(bf16[48,8,128]{2,1,0:T(8,128)(2,1)} %get-tuple-element.96), channel_id=1, source_target_pairs={{0,13},{1,12},{2,15},{3,14},{4,1},{5,0},{6,3},{7,2},{8,5},{9,4},{1... | collective-permute-start | bytes 294920 | tf_op jit(solution)/shard_map/ppermute | solution.py:353
  123.1 19.9 %collective-permute-start.32 = (bf16[48,8,128]{2,1,0:T(8,128)(2,1)}, bf16[48,8,128]{2,1,0:T(8,128)(2,1)}, u32[]{:S(2)}, u32[]{:S(2)}) collective-permute-start(bf16[48,8,128]{2,1,0:T(8,128)(2,1)} %get-tuple-element.97), channel_id=1, source_target_pairs={{0,14},{1,15},{2,12},{3,13},{4,2},{5,3},{6,0},{7,1},{8,6},{9,7},{1... | collective-permute-start | bytes 294920 | tf_op jit(solution)/shard_map/ppermute | solution.py:353
  123.7 33.8 %collective-permute-start.33 = (bf16[48,8,128]{2,1,0:T(8,128)(2,1)}, bf16[48,8,128]{2,1,0:T(8,128)(2,1)}, u32[]{:S(2)}, u32[]{:S(2)}) collective-permute-start(bf16[48,8,128]{2,1,0:T(8,128)(2,1)} %get-tuple-element.98), channel_id=1, source_target_pairs={{0,15},{1,14},{2,13},{3,12},{4,3},{5,2},{6,1},{7,0},{8,7},{9,6},{1... | collective-permute-start | bytes 294920 | tf_op jit(solution)/shard_map/ppermute | solution.py:353
  126.0 31.8 %collective-permute-start.23 = (bf16[48,8,128]{2,1,0:T(8,128)(2,1)}, bf16[48,8,128]{2,1,0:T(8,128)(2,1)S(1)}, u32[]{:S(2)}, u32[]{:S(2)}) collective-permute-start(bf16[48,8,128]{2,1,0:T(8,128)(2,1)} %get-tuple-element.87), channel_id=1, source_target_pairs={{0,4},{1,5},{2,6},{3,7},{4,8},{5,9},{6,10},{7,11},{8,12},{9,13},{1... | collective-permute-start | bytes 294920 | tf_op jit(solution)/shard_map/ppermute | solution.py:353
  127.7 32.2 %collective-permute-start.24 = (bf16[48,8,128]{2,1,0:T(8,128)(2,1)}, bf16[48,8,128]{2,1,0:T(8,128)(2,1)S(1)}, u32[]{:S(2)}, u32[]{:S(2)}) collective-permute-start(bf16[48,8,128]{2,1,0:T(8,128)(2,1)} %get-tuple-element.88), channel_id=1, source_target_pairs={{0,5},{1,4},{2,7},{3,6},{4,9},{5,8},{6,11},{7,10},{8,13},{9,12},{1... | collective-permute-start | bytes 294920 | tf_op jit(solution)/shard_map/ppermute | solution.py:353
  142.5 18.2 %collective-permute-start.25 = (bf16[48,8,128]{2,1,0:T(8,128)(2,1)}, bf16[48,8,128]{2,1,0:T(8,128)(2,1)S(1)}, u32[]{:S(2)}, u32[]{:S(2)}) collective-permute-start(bf16[48,8,128]{2,1,0:T(8,128)(2,1)} %get-tuple-element.89), channel_id=1, source_target_pairs={{0,6},{1,7},{2,4},{3,5},{4,10},{5,11},{6,8},{7,9},{8,14},{9,15},{1... | collective-permute-start | bytes 294920 | tf_op jit(solution)/shard_map/ppermute | solution.py:353
  143.0 19.8 %collective-permute-start.26 = (bf16[48,8,128]{2,1,0:T(8,128)(2,1)}, bf16[48,8,128]{2,1,0:T(8,128)(2,1)S(1)}, u32[]{:S(2)}, u32[]{:S(2)}) collective-permute-start(bf16[48,8,128]{2,1,0:T(8,128)(2,1)} %get-tuple-element.90), channel_id=1, source_target_pairs={{0,7},{1,6},{2,5},{3,4},{4,11},{5,10},{6,9},{7,8},{8,15},{9,14},{1... | collective-permute-start | bytes 294920 | tf_op jit(solution)/shard_map/ppermute | solution.py:353
  157.6 28.7 %collective-permute-start.17 = (f32[3,64,256]{2,1,0:T(8,128)S(1)}, f32[3,64,256]{2,1,0:T(8,128)S(1)}, u32[]{:S(2)}, u32[]{:S(2)}) collective-permute-start(f32[3,64,256]{2,1,0:T(8,128)S(1)} %get-tuple-element.79), channel_id=1, source_target_pairs={{3,0},{0,1},{1,4},{4,5},{5,8},{8,9},{9,12},{12,13},{13,14},{14,15}... | collective-permute-start | bytes 589832 | tf_op jit(solution)/shard_map/ppermute | solution.py:373
  157.8 12.8 %collective-permute-start.19 = (bf16[48,8,128]{2,1,0:T(8,128)(2,1)S(1)}, bf16[48,8,128]{2,1,0:T(8,128)(2,1)S(1)}, u32[]{:S(2)}, u32[]{:S(2)}) collective-permute-start(bf16[48,8,128]{2,1,0:T(8,128)(2,1)S(1)} %copy-done.28), channel_id=1, source_target_pairs={{0,8},{1,9},{2,10},{3,11},{4,12},{5,13},{6,14},{7,15},{8,0},{9,1},... | collective-permute-start | bytes 294920 | tf_op jit(solution)/shard_map/ppermute | solution.py:353
  159.9 13.3 %collective-permute-start.20 = (bf16[48,8,128]{2,1,0:T(8,128)(2,1)S(1)}, bf16[48,8,128]{2,1,0:T(8,128)(2,1)S(1)}, u32[]{:S(2)}, u32[]{:S(2)}) collective-permute-start(bf16[48,8,128]{2,1,0:T(8,128)(2,1)S(1)} %copy-done.27), channel_id=1, source_target_pairs={{0,9},{1,8},{2,11},{3,10},{4,13},{5,12},{6,15},{7,14},{8,1},{9,0},... | collective-permute-start | bytes 294920 | tf_op jit(solution)/shard_map/ppermute | solution.py:353
  160.7 17.0 %collective-permute-start.21 = (bf16[48,8,128]{2,1,0:T(8,128)(2,1)S(1)}, bf16[48,8,128]{2,1,0:T(8,128)(2,1)S(1)}, u32[]{:S(2)}, u32[]{:S(2)}) collective-permute-start(bf16[48,8,128]{2,1,0:T(8,128)(2,1)S(1)} %copy-done.26), channel_id=1, source_target_pairs={{0,10},{1,11},{2,8},{3,9},{4,14},{5,15},{6,12},{7,13},{8,2},{9,3},... | collective-permute-start | bytes 294920 | tf_op jit(solution)/shard_map/ppermute | solution.py:353
  162.8 17.4 %collective-permute-start.22 = (bf16[48,8,128]{2,1,0:T(8,128)(2,1)S(1)}, bf16[48,8,128]{2,1,0:T(8,128)(2,1)S(1)}, u32[]{:S(2)}, u32[]{:S(2)}) collective-permute-start(bf16[48,8,128]{2,1,0:T(8,128)(2,1)S(1)} %copy-done.25), channel_id=1, source_target_pairs={{0,11},{1,10},{2,9},{3,8},{4,15},{5,14},{6,13},{7,12},{8,3},{9,2},... | collective-permute-start | bytes 294920 | tf_op jit(solution)/shard_map/ppermute | solution.py:353
  170.6 15.7 %collective-permute-start = (f32[4,64,256]{2,1,0:T(8,128)S(1)}, f32[4,64,256]{2,1,0:T(8,128)S(1)}, u32[]{:S(2)}, u32[]{:S(2)}) collective-permute-start(f32[4,64,256]{2,1,0:T(8,128)S(1)} %get-tuple-element.57), channel_id=1, source_target_pairs={{3,0},{0,1},{1,4},{4,5},{5,8},{8,9},{9,12},{12,13},{13,14},{14,15}... | collective-permute-start | bytes 786440 | tf_op jit(solution)/shard_map/ppermute | solution.py:373
  173.2 13.1 %collective-permute-start.1 = (f32[4,64,256]{2,1,0:T(8,128)S(1)}, f32[4,64,256]{2,1,0:T(8,128)S(1)}, u32[]{:S(2)}, u32[]{:S(2)}) collective-permute-start(f32[4,64,256]{2,1,0:T(8,128)S(1)} %get-tuple-element.58), channel_id=1, source_target_pairs={{0,3},{1,0},{4,1},{5,4},{8,5},{9,8},{12,9},{13,12},{14,13},{15,14}... | collective-permute-start | bytes 786440 | tf_op jit(solution)/shard_map/ppermute | solution.py:372
  177.7 8.6 %collective-permute-start.18 = (f32[3,64,256]{2,1,0:T(8,128)S(1)}, f32[3,64,256]{2,1,0:T(8,128)S(1)}, u32[]{:S(2)}, u32[]{:S(2)}) collective-permute-start(f32[3,64,256]{2,1,0:T(8,128)S(1)} %get-tuple-element.80), channel_id=1, source_target_pairs={{0,3},{1,0},{4,1},{5,4},{8,5},{9,8},{12,9},{13,12},{14,13},{15,14}... | collective-permute-start | bytes 589832 | tf_op jit(solution)/shard_map/ppermute | solution.py:372
  (34 other events, 529.1 us)

commit v4 on v3

--- a/solution.py
+++ b/solution.py
@@ -11,7 +11,6 @@
 TALL = 4
 WIDE = 8
 EPSILON = 1e-06
-LATE = False
 LANES = 128
 VMEM = pl.BlockSpec(memory_space=pltpu.VMEM)
 HBM = pl.BlockSpec(memory_space=pltpu.HBM)
@@ -59,17 +58,18 @@
     small = [pltpu.make_async_copy(word, buf, word_sem.at[n]) for n, (word, buf) in enumerate(zip(words, bufs))]
     for fetch in small + fetches:
         fetch.start()
-    for fetch in small:
-        fetch.wait()
-    owner_ref, down_ref, across_ref = bufs
-    tag_buf[...] = jnp.zeros(tag_buf.shape, jnp.float32)
-    tag_buf[0:1, :held] = (owner_ref[...] * TALL + down_ref[...]).astype(jnp.float32)
-    tag_buf[1:2, :held] = across_ref[...].astype(jnp.float32)
-    tag = tag_buf[...].astype(out_buf.dtype)
     stores = []
     for j, fetch in enumerate(fetches):
         fetch.wait()
         more = j == parts - 1
+        if more:
+            for copy in small:
+                copy.wait()
+            owner_ref, down_ref, across_ref = bufs
+            tag_buf[...] = jnp.zeros(tag_buf.shape, jnp.float32)
+            tag_buf[0:1, :held] = (owner_ref[...] * TALL + down_ref[...]).astype(jnp.float32)
+            tag_buf[1:2, :held] = across_ref[...].astype(jnp.float32)
+            tag = tag_buf[...].astype(out_buf.dtype)
         for g in range(group):
             strip = strip_of(g, group)
             out_buf[g, j * many : (j + 1) * many] = in_buf[j, :, :, :, strip].reshape(many, rows, side)
@@ -84,7 +84,7 @@
 
 def bulk_cut(owner, down, across, cells, span):
     held, _, planes, group, rows, side = cells.shape
-    parts = next(p for p in (4, 3, 2, 1) if held % p == 0)
+    parts = next(p for p in (6, 4, 3, 2, 1) if held % p == 0)
     out = jax.ShapeDtypeStruct((group, held * span * planes + 1, rows, side), cells.dtype)
     return pl.pallas_call(
         functools.partial(bulk_kernel, span=span),
@@ -305,22 +305,17 @@
         deal(out_ref, i * TALL, coherence(re, im, power_ref[i], power))
 
 
-def settle_kernel(*refs):
-    out_ref = refs[-1]
-    base = 0
-    for got_ref in refs[:-1]:
-        group = got_ref.shape[0]
-        tall = out_ref.shape[1] // (TALL * group)
-        pairs = got_ref.shape[1] // (tall * TALL)
-        for device in range(group):
-            strip = strip_of(device, group)
-            for k in range(pairs):
-                for i in range(tall):
-                    for r in range(TALL):
-                        at = (k * tall + i) * TALL + r
-                        row = (r * group + strip) * tall + i
-                        out_ref[base + k, row : row + 1] = got_ref[device, at : at + 1]
-        base += pairs
+def settle_kernel(got_ref, out_ref):
+    group = got_ref.shape[0]
+    pairs, tall = out_ref.shape[0], out_ref.shape[1] // (TALL * group)
+    for device in range(group):
+        strip = strip_of(device, group)
+        for k in range(pairs):
+            for i in range(tall):
+                for r in range(TALL):
+                    at = (k * tall + i) * TALL + r
+                    row = (r * group + strip) * tall + i
+                    out_ref[k, row : row + 1] = got_ref[device, at : at + 1]
 
 
 def local(radar_subimages, owning_sector, sector_down_start, sector_across_start):
@@ -344,21 +339,20 @@
     got = lax.all_to_all(bulk, "grid", split_axis=0, concat_axis=0, tiled=True)
     strips = strip_of(shifted(me, devices, group), group)
 
-    def scatter(date, after=None):
+    def scatter(date):
         sends = cut(strips, cells, date)
-        if after is not None:
-            sends, _ = lax.optimization_barrier((sends, after))
-        pieces = [sends[0]] + [None] * (group - 1)
+        pieces = [pltpu.with_memory_space_constraint(sends[0], pltpu.HBM)] + [None] * (group - 1)
         for m in range(1, group):
             pieces[m] = lax.ppermute(sends[m], "grid", [(i, shifted(i, m, group)) for i in range(group)])
         return pieces
 
     pieces_b = scatter(dates - 2)
-    pieces = scatter(dates - 1, got if LATE else None)
+    pieces = scatter(dates - 1)
 
     col = jnp.arange(cols)[:, None]
     out_col = jnp.arange(cols // 4)[None, :]
     window = ((col >= 4 * out_col - 12) & (col <= 4 * out_col + 15)).astype(jnp.bfloat16)
+    window = pltpu.with_memory_space_constraint(window, pltpu.HBM)
     tags = got[:, -1, :2, :held].astype(jnp.int32)
     places = tags[:, 1] * lines + tags[:, 0]
     flat = places.reshape(group * held)
@@ -405,8 +399,6 @@
             jax.ShapeDtypeStruct((tall, lines, out_cols), jnp.float32),
         ],
     )
-    if LATE:
-        first = lax.all_to_all(dealt, "grid", split_axis=0, concat_axis=0, tiled=True)
 
     ahead, level, late = started(group)
     near, middle, far = [0, *level, *ahead[: len(ahead) // 2]], ahead[len(ahead) // 2 :], late
@@ -430,14 +422,10 @@
         last_finish_kernel, (), (own, above, below, power),
         [jax.ShapeDtypeStruct((group, tall * TALL, out_cols), jnp.float32)],
     )
-    if LATE:
-        second = lax.all_to_all(last, "grid", split_axis=0, concat_axis=0, tiled=True)
-        got = (first, second)
-    else:
-        last = jnp.concatenate([dealt, last], axis=1)
-        got = (lax.all_to_all(last, "grid", split_axis=0, concat_axis=0, tiled=True),)
+    dealt = jnp.concatenate([dealt, last], axis=1)
+    got = lax.all_to_all(dealt, "grid", split_axis=0, concat_axis=0, tiled=True)
     (out,) = call(
-        settle_kernel, (), got,
+        settle_kernel, (), (got,),
         [jax.ShapeDtypeStruct((dates - 1, TALL * side // 4, out_cols), jnp.float32)],
     )
     return out

time: 211 us -> 207 us (0.981)
  local copies, waits for them, and re-layouts: 15.2 us -> 11.7 us
    unnamed x58 -> x44, local copies, waits for them, and re-layouts: 13.2 us -> 9.63 us
  transfers between devices with their start and end apart: 37 -> 37, of which waited for: 8 -> 8; matrix products, arithmetic and copies ran while one was open for 2% -> 2% of each run, Pallas kernels for 15% -> 16%
where the time goes in v4:
time: 207 us; the launch traced here: 204 us
  waiting for transfers between devices  81 us (39%)
  starting transfers between devices  57 us (28%)
  Pallas kernels  37.1 us (18%)
  blocking collectives  15.1 us (7%)
  local copies, waits for them, and re-layouts  11.7 us (6%)
  other arithmetic  2.09 us (1%)
    ppermute x30, waiting for transfers between devices, scatter(): lax.ppermute(sends[m], 'grid', [(i, shifted(i, m, group)) for i in range(...  76.2 us
    ppermute x30, starting transfers between devices, scatter(): lax.ppermute(sends[m], 'grid', [(i, shifted(i, m, group)) for i in range(...  42.6 us
    pallas_call x8, Pallas kernels, call(): pl.pallas_call(kernel, out_shape=outs, grid_spec=pltpu.PrefetchScalarGrid...  26.3 us
    all_to_all x1, blocking collectives, local(): got = lax.all_to_all(dealt, 'grid', split_axis=0, concat_axis=0, tiled=True)  15.1 us
    unnamed x44, local copies, waits for them, and re-layouts  9.63 us
    pallas_call x2, Pallas kernels, cut(): pl.pallas_call(cut_kernel, out_shape=[pltpu.HBM(piece, cells.dtype)] * gr...  7.07 us
    all_to_all x1, starting transfers between devices, local(): got = lax.all_to_all(bulk, 'grid', split_axis=0, concat_axis=0, tiled=True)  6.53 us
    ppermute x3, starting transfers between devices, exchange(): lax.ppermute(down, 'grid', [(at[s - 1], at[s]) for s in range(group)])  4.86 us
  transfers between devices with their start and end apart: 37, of which 8 were waited for; matrix products, arithmetic and copies ran while one was open for 2% of the time, Pallas kernels for 16%

profile of v4, /device:TPU:13, one launch (start us, length us, event | category | flops | bytes accessed | tf_op | source)
XLA Modules:
  0.0 204.3 jit_solution(9834659172784952317)
XLA Ops:
  0.0 3.7 %bulk_cut.1 = bf16[16,97,8,128]{3,2,1,0:T(8,128)(2,1)} custom-call(s32[1,24]{1,0:T(1,128)} %bitcast.16, s32[1,24]{1,0:T(1,128)} %bitcast.17, s32[1,24]{1,0:T(1,128)} %bitcast.18, bf16[24,4,2,16,8,128]{5,4,3,2,1,0:T(8,128)(2,1)} %bitcast.12), custom_call_target="tpu_custom_call" | custom-call | tf_op jit(solution)/shard_map/bulk_cut/pallas_call | solution.py:89
  3.7 6.5 %all-to-all-start = ((bf16[16,97,8,128]{3,2,1,0:T(8,128)(2,1)}), bf16[16,97,8,128]{3,2,1,0:T(8,128)(2,1)S(1)}, u32[]{:S(2)}, u32[]{:S(2)}) async-start(bf16[16,97,8,128]{3,2,1,0:T(8,128)(2,1)} %bulk_cut.1), calls=%async_computation | async-start | bytes 6356992 | tf_op jit(solution)/shard_map/all_to_all | solution.py:339
  10.3 3.6 %cut.2 = (bf16[48,8,128]{2,1,0:T(8,128)(2,1)}, bf16[48,8,128]{2,1,0:T(8,128)(2,1)}, bf16[48,8,128]{2,1,0:T(8,128)(2,1)}, bf16[48,8,128]{2,1,0:T(8,128)(2,1)}, bf...) custom-call(s32[16]{0:T(128)S(1)} %fusion.7.strip_ref, ...), custom_call_target="tpu_custom_call" | custom-call | tf_op jit(solution)/shard_map/cut/pallas_call | solution.py:117
  13.8 2.4 %collective-permute-start.10 = (bf16[48,8,128]{2,1,0:T(8,128)(2,1)}, bf16[48,8,128]{2,1,0:T(8,128)(2,1)S(1)}, u32[]{:S(2)}, u32[]{:S(2)}) collective-permute-start(bf16[48,8,128]{2,1,0:T(8,128)(2,1)} %get-tuple-element.70), channel_id=1, source_target_pairs={{0,9},{1,8},{2,11},{3,10},{4,13},{5,12},{6,15},{7,14},{8,1},{9,0},... | collective-permute-start | bytes 294920 | tf_op jit(solution)/shard_map/ppermute | solution.py:346
  16.5 3.3 %collective-permute-start.12 = (bf16[48,8,128]{2,1,0:T(8,128)(2,1)}, bf16[48,8,128]{2,1,0:T(8,128)(2,1)S(1)}, u32[]{:S(2)}, u32[]{:S(2)}) collective-permute-start(bf16[48,8,128]{2,1,0:T(8,128)(2,1)} %get-tuple-element.72), channel_id=1, source_target_pairs={{0,11},{1,10},{2,9},{3,8},{4,15},{5,14},{6,13},{7,12},{8,3},{9,2},... | collective-permute-start | bytes 294920 | tf_op jit(solution)/shard_map/ppermute | solution.py:346
  20.0 1.5 collective-permute-start.14
  21.5 3.5 %cut.3 = (bf16[48,8,128]{2,1,0:T(8,128)(2,1)}, bf16[48,8,128]{2,1,0:T(8,128)(2,1)}, bf16[48,8,128]{2,1,0:T(8,128)(2,1)}, bf16[48,8,128]{2,1,0:T(8,128)(2,1)}, bf...) custom-call(s32[16]{0:T(128)S(1)} %fusion.7.strip_ref, ...), custom_call_target="tpu_custom_call" | custom-call | tf_op jit(solution)/shard_map/cut/pallas_call | solution.py:117
  26.1 65.2 %collective-permute-done.10.refs_9_ = bf16[48,8,128]{2,1,0:T(8,128)(2,1)S(1)} collective-permute-done((bf16[48,8,128]{2,1,0:T(8,128)(2,1)}, bf16[48,8,128]{2,1,0:T(8,128)(2,1)S(1)}, u32[]{:S(2)}, u32[]{:S(2)}) %collective-permute-start.10) | collective-permute-done | bytes 98336 | tf_op jit(solution)/shard_map/ppermute | solution.py:346
  91.3 2.1 %collective-permute-done.11.refs_10_ = bf16[48,8,128]{2,1,0:T(8,128)(2,1)S(1)} collective-permute-done((bf16[48,8,128]{2,1,0:T(8,128)(2,1)}, bf16[48,8,128]{2,1,0:T(8,128)(2,1)S(1)}, u32[]{:S(2)}, u32[]{:S(2)}) %collective-permute-start.11) | collective-permute-done | bytes 98336 | tf_op jit(solution)/shard_map/ppermute | solution.py:346
  93.4 3.5 %collective-permute-start.16 = (bf16[48,8,128]{2,1,0:T(8,128)(2,1)}, bf16[48,8,128]{2,1,0:T(8,128)(2,1)}, u32[]{:S(2)}, u32[]{:S(2)}) collective-permute-start(bf16[48,8,128]{2,1,0:T(8,128)(2,1)} %get-tuple-element.76), channel_id=1, source_target_pairs={{0,15},{1,14},{2,13},{3,12},{4,3},{5,2},{6,1},{7,0},{8,7},{9,6},{1... | collective-permute-start | bytes 294920 | tf_op jit(solution)/shard_map/ppermute | solution.py:346
  100.6 1.4 collective-permute-done.16.refs_15_
  102.0 1.8 collective-permute-start.6
  104.5 2.5 %collective-permute-start.7 = (bf16[48,8,128]{2,1,0:T(8,128)(2,1)}, bf16[48,8,128]{2,1,0:T(8,128)(2,1)}, u32[]{:S(2)}, u32[]{:S(2)}) collective-permute-start(bf16[48,8,128]{2,1,0:T(8,128)(2,1)} %get-tuple-element.67), channel_id=1, source_target_pairs={{0,6},{1,7},{2,4},{3,5},{4,10},{5,11},{6,8},{7,9},{8,14},{9,15},{1... | collective-permute-start | bytes 294920 | tf_op jit(solution)/shard_map/ppermute | solution.py:346
  113.5 3.4 %collective-permute-start.30 = (bf16[48,8,128]{2,1,0:T(8,128)(2,1)}, bf16[48,8,128]{2,1,0:T(8,128)(2,1)S(1)}, u32[]{:S(2)}, u32[]{:S(2)}) collective-permute-start(bf16[48,8,128]{2,1,0:T(8,128)(2,1)} %get-tuple-element.95), channel_id=1, source_target_pairs={{0,12},{1,13},{2,14},{3,15},{4,0},{5,1},{6,2},{7,3},{8,4},{9,5},{1... | collective-permute-start | bytes 294920 | tf_op jit(solution)/shard_map/ppermute | solution.py:346
  118.0 3.8 %collective-permute-start.31 = (bf16[48,8,128]{2,1,0:T(8,128)(2,1)}, bf16[48,8,128]{2,1,0:T(8,128)(2,1)}, u32[]{:S(2)}, u32[]{:S(2)}) collective-permute-start(bf16[48,8,128]{2,1,0:T(8,128)(2,1)} %get-tuple-element.96), channel_id=1, source_target_pairs={{0,13},{1,12},{2,15},{3,14},{4,1},{5,0},{6,3},{7,2},{8,5},{9,4},{1... | collective-permute-start | bytes 294920 | tf_op jit(solution)/shard_map/ppermute | solution.py:346
  123.1 1.6 collective-permute-start.33
  127.0 1.7 collective-permute-start.24
  130.3 10.5 %shard_map.46 = (f32[512,2,8,128]{3,2,1,0:T(8,128)S(1)}, f32[4,2,64,256]{3,2,1,0:T(8,128)S(1)}, f32[4,64,256]{2,1,0:T(8,128)S(1)}, f32[4,64,256]{2,1,0:T(8,128)S(1)}) custom-call(s32[16]{0:T(128)S(1)} %fusion.7.strip_ref, s32[384]{0:T(512)S(1)} %add.167.place_ref, f32[384]{0:T(512)S(1)} %convert_divide_fusion.share_ref, ...), custom_call_target="tpu_custom_call" | custom-call | tf_op jit(solution)/shard_map/pallas_call | solution.py:254
  141.3 2.1 %collective-permute-start.26 = (bf16[48,8,128]{2,1,0:T(8,128)(2,1)}, bf16[48,8,128]{2,1,0:T(8,128)(2,1)S(1)}, u32[]{:S(2)}, u32[]{:S(2)}) collective-permute-start(bf16[48,8,128]{2,1,0:T(8,128)(2,1)} %get-tuple-element.90), channel_id=1, source_target_pairs={{0,7},{1,6},{2,5},{3,4},{4,11},{5,10},{6,9},{7,8},{8,15},{9,14},{1... | collective-permute-start | bytes 294920 | tf_op jit(solution)/shard_map/ppermute | solution.py:346
  147.9 5.9 %shard_map.47 = (f32[512,2,8,128]{3,2,1,0:T(8,128)S(1)}, f32[3,2,64,256]{3,2,1,0:T(8,128)S(1)}, f32[3,64,256]{2,1,0:T(8,128)S(1)}, f32[3,64,256]{2,1,0:T(8,128)S(1)}) custom-call(s32[16]{0:T(128)S(1)} %fusion.7.strip_ref, s32[384]{0:T(512)S(1)} %reshape.176.place_ref, f32[384]{0:T(512)S(1)} %reshape.177.share_ref, ...), custom_call_target="tpu_custom_call" | custom-call | tf_op jit(solution)/shard_map/pallas_call | solution.py:254
  154.1 1.9 collective-permute-start.19
  156.9 2.1 %collective-permute-start.21 = (bf16[48,8,128]{2,1,0:T(8,128)(2,1)S(1)}, bf16[48,8,128]{2,1,0:T(8,128)(2,1)S(1)}, u32[]{:S(2)}, u32[]{:S(2)}) collective-permute-start(bf16[48,8,128]{2,1,0:T(8,128)(2,1)S(1)} %copy-done.19), channel_id=1, source_target_pairs={{0,10},{1,11},{2,8},{3,9},{4,14},{5,15},{6,12},{7,13},{8,2},{9,3},... | collective-permute-start | bytes 294920 | tf_op jit(solution)/shard_map/ppermute | solution.py:346
  160.3 6.5 %collective-permute-done.19.refs_0_ = bf16[48,8,128]{2,1,0:T(8,128)(2,1)S(1)} collective-permute-done((bf16[48,8,128]{2,1,0:T(8,128)(2,1)S(1)}, bf16[48,8,128]{2,1,0:T(8,128)(2,1)S(1)}, u32[]{:S(2)}, u32[]{:S(2)}) %collective-permute-start.19) | collective-permute-done | bytes 98336 | tf_op jit(solution)/shard_map/ppermute | solution.py:346
  166.7 2.6 %collective-permute-start = (f32[4,64,256]{2,1,0:T(8,128)S(1)}, f32[4,64,256]{2,1,0:T(8,128)S(1)}, u32[]{:S(2)}, u32[]{:S(2)}) collective-permute-start(f32[4,64,256]{2,1,0:T(8,128)S(1)} %get-tuple-element.57), channel_id=1, source_target_pairs={{3,0},{0,1},{1,4},{4,5},{5,8},{8,9},{9,12},{12,13},{13,14},{14,15}... | collective-permute-start | bytes 786440 | tf_op jit(solution)/shard_map/ppermute | solution.py:367
  169.9 2.3 %shard_map.49.refs_4_ = f32[512,2,8,128]{3,2,1,0:T(8,128)S(1)} custom-call(s32[384]{0:T(512)S(1)} %reshape.176.place_ref, f32[384]{0:T(512)S(1)} %reshape.177.share_ref, bf16[48,8,128]{2,1,0:T(8,128)(2,1)} %get-tuple-element.91.refs_0_, bf16[48,8,128]{2,1,0:T(8,128)(2,1)S(1)} %copy-done.9, bf16[48,8,128]{2,1,0:T(8,128)(2,1)S(1)} %copy-done.11, ...), custom_call_target="tpu_custom_call" | custom-call | tf_op jit(solution)/shard_map/pallas_call | solution.py:254
  172.2 1.5 shard_map.50.refs_6_
  173.8 2.5 %collective-permute-start.18 = (f32[3,64,256]{2,1,0:T(8,128)S(1)}, f32[3,64,256]{2,1,0:T(8,128)S(1)}, u32[]{:S(2)}, u32[]{:S(2)}) collective-permute-start(f32[3,64,256]{2,1,0:T(8,128)S(1)} %get-tuple-element.80), channel_id=1, source_target_pairs={{0,3},{1,0},{4,1},{5,4},{8,5},{9,8},{12,9},{13,12},{14,13},{15,14}... | collective-permute-start | bytes 589832 | tf_op jit(solution)/shard_map/ppermute | solution.py:366
  176.3 4.7 %shard_map.51 = (f32[512,2,8,128]{3,2,1,0:T(8,128)S(1)}, f32[3,2,64,256]{3,2,1,0:T(8,128)S(1)}, f32[3,64,256]{2,1,0:T(8,128)S(1)}, f32[3,64,256]{2,1,0:T(8,128)S(1)}) custom-call(s32[16]{0:T(128)S(1)} %fusion.7.strip_ref, s32[384]{0:T(512)S(1)} %reshape.176.place_ref, f32[384]{0:T(512)S(1)} %reshape.177.share_ref, ...), custom_call_target="tpu_custom_call", output_to_operand_aliasing={{0}: (9, {})} | custom-call | tf_op jit(solution)/shard_map/pallas_call | solution.py:254
  181.0 2.0 collective-permute-start.34
  183.3 2.3 %collective-permute-done.34.above_ref = f32[3,64,256]{2,1,0:T(8,128)S(1)} collective-permute-done((f32[3,64,256]{2,1,0:T(8,128)S(1)}, f32[3,64,256]{2,1,0:T(8,128)S(1)}, u32[]{:S(2)}, u32[]{:S(2)}) %collective-permute-start.34) | collective-permute-done | bytes 196640 | tf_op jit(solution)/shard_map/ppermute | solution.py:367
  185.6 2.5 %collective-permute-done.35.below_ref = f32[3,64,256]{2,1,0:T(8,128)S(1)} collective-permute-done((f32[3,64,256]{2,1,0:T(8,128)S(1)}, f32[3,64,256]{2,1,0:T(8,128)S(1)}, u32[]{:S(2)}, u32[]{:S(2)}) %collective-permute-start.35) | collective-permute-done | bytes 196640 | tf_op jit(solution)/shard_map/ppermute | solution.py:366
  188.2 15.1 %all_to_all.10.got_ref = f32[16,24,256]{2,1,0:T(8,128)S(1)} all-to-all(f32[16,24,256]{2,1,0:T(8,128)S(1)} %pad_maximum_fusion), channel_id=1, replica_groups=mesh['region'=2,'grid'=16] {'grid'}, dimensions={0} | all-to-all | bytes 786432 | tf_op jit(solution)/shard_map/all_to_all | solution.py:426
  (115 shorter events, 27.9 us)
Async XLA Ops:
  3.7 95.5 %all-to-all-start = ((bf16[16,97,8,128]{3,2,1,0:T(8,128)(2,1)}), bf16[16,97,8,128]{3,2,1,0:T(8,128)(2,1)S(1)}, u32[]{:S(2)}, u32[]{:S(2)}) async-start(bf16[16,97,8,128]{3,2,1,0:T(8,128)(2,1)} %bulk_cut.1), calls=%async_computation | async-start | bytes 6356992 | tf_op jit(solution)/shard_map/all_to_all | solution.py:339
  13.8 77.4 %collective-permute-start.10 = (bf16[48,8,128]{2,1,0:T(8,128)(2,1)}, bf16[48,8,128]{2,1,0:T(8,128)(2,1)S(1)}, u32[]{:S(2)}, u32[]{:S(2)}) collective-permute-start(bf16[48,8,128]{2,1,0:T(8,128)(2,1)} %get-tuple-element.70), channel_id=1, source_target_pairs={{0,9},{1,8},{2,11},{3,10},{4,13},{5,12},{6,15},{7,14},{8,1},{9,0},... | collective-permute-start | bytes 294920 | tf_op jit(solution)/shard_map/ppermute | solution.py:346
  16.2 77.2 %collective-permute-start.11 = (bf16[48,8,128]{2,1,0:T(8,128)(2,1)}, bf16[48,8,128]{2,1,0:T(8,128)(2,1)S(1)}, u32[]{:S(2)}, u32[]{:S(2)}) collective-permute-start(bf16[48,8,128]{2,1,0:T(8,128)(2,1)} %get-tuple-element.71), channel_id=1, source_target_pairs={{0,10},{1,11},{2,8},{3,9},{4,14},{5,15},{6,12},{7,13},{8,2},{9,3},... | collective-permute-start | bytes 294920 | tf_op jit(solution)/shard_map/ppermute | solution.py:346
  16.5 80.4 %collective-permute-start.12 = (bf16[48,8,128]{2,1,0:T(8,128)(2,1)}, bf16[48,8,128]{2,1,0:T(8,128)(2,1)S(1)}, u32[]{:S(2)}, u32[]{:S(2)}) collective-permute-start(bf16[48,8,128]{2,1,0:T(8,128)(2,1)} %get-tuple-element.72), channel_id=1, source_target_pairs={{0,11},{1,10},{2,9},{3,8},{4,15},{5,14},{6,13},{7,12},{8,3},{9,2},... | collective-permute-start | bytes 294920 | tf_op jit(solution)/shard_map/ppermute | solution.py:346
  19.7 78.5 %collective-permute-start.13 = (bf16[48,8,128]{2,1,0:T(8,128)(2,1)}, bf16[48,8,128]{2,1,0:T(8,128)(2,1)S(1)}, u32[]{:S(2)}, u32[]{:S(2)}) collective-permute-start(bf16[48,8,128]{2,1,0:T(8,128)(2,1)} %get-tuple-element.73), channel_id=1, source_target_pairs={{0,12},{1,13},{2,14},{3,15},{4,0},{5,1},{6,2},{7,3},{8,4},{9,5},{1... | collective-permute-start | bytes 294920 | tf_op jit(solution)/shard_map/ppermute | solution.py:346
  20.0 79.2 %collective-permute-start.14 = (bf16[48,8,128]{2,1,0:T(8,128)(2,1)}, bf16[48,8,128]{2,1,0:T(8,128)(2,1)}, u32[]{:S(2)}, u32[]{:S(2)}) collective-permute-start(bf16[48,8,128]{2,1,0:T(8,128)(2,1)} %get-tuple-element.74), channel_id=1, source_target_pairs={{0,13},{1,12},{2,15},{3,14},{4,1},{5,0},{6,3},{7,2},{8,5},{9,4},{1... | collective-permute-start | bytes 294920 | tf_op jit(solution)/shard_map/ppermute | solution.py:346
  91.3 9.3 %collective-permute-start.15 = (bf16[48,8,128]{2,1,0:T(8,128)(2,1)}, bf16[48,8,128]{2,1,0:T(8,128)(2,1)}, u32[]{:S(2)}, u32[]{:S(2)}) collective-permute-start(bf16[48,8,128]{2,1,0:T(8,128)(2,1)} %get-tuple-element.75), channel_id=1, source_target_pairs={{0,14},{1,15},{2,12},{3,13},{4,2},{5,3},{6,0},{7,1},{8,6},{9,7},{1... | collective-permute-start | bytes 294920 | tf_op jit(solution)/shard_map/ppermute | solution.py:346
  93.4 8.7 %collective-permute-start.16 = (bf16[48,8,128]{2,1,0:T(8,128)(2,1)}, bf16[48,8,128]{2,1,0:T(8,128)(2,1)}, u32[]{:S(2)}, u32[]{:S(2)}) collective-permute-start(bf16[48,8,128]{2,1,0:T(8,128)(2,1)} %get-tuple-element.76), channel_id=1, source_target_pairs={{0,15},{1,14},{2,13},{3,12},{4,3},{5,2},{6,1},{7,0},{8,7},{9,6},{1... | collective-permute-start | bytes 294920 | tf_op jit(solution)/shard_map/ppermute | solution.py:346
  98.9 8.1 %collective-permute-start.3 = (bf16[48,8,128]{2,1,0:T(8,128)(2,1)}, bf16[48,8,128]{2,1,0:T(8,128)(2,1)}, u32[]{:S(2)}, u32[]{:S(2)}) collective-permute-start(bf16[48,8,128]{2,1,0:T(8,128)(2,1)} %get-tuple-element.63), channel_id=1, source_target_pairs={{0,2},{1,3},{2,0},{3,1},{4,6},{5,7},{6,4},{7,5},{8,10},{9,11},{10,... | collective-permute-start | bytes 294920 | tf_op jit(solution)/shard_map/ppermute | solution.py:346
  99.3 10.1 %collective-permute-start.4 = (bf16[48,8,128]{2,1,0:T(8,128)(2,1)}, bf16[48,8,128]{2,1,0:T(8,128)(2,1)}, u32[]{:S(2)}, u32[]{:S(2)}) collective-permute-start(bf16[48,8,128]{2,1,0:T(8,128)(2,1)} %get-tuple-element.64), channel_id=1, source_target_pairs={{0,3},{1,2},{2,1},{3,0},{4,7},{5,6},{6,5},{7,4},{8,11},{9,10},{10,... | collective-permute-start | bytes 294920 | tf_op jit(solution)/shard_map/ppermute | solution.py:346
  100.6 9.7 %collective-permute-start.5 = (bf16[48,8,128]{2,1,0:T(8,128)(2,1)}, bf16[48,8,128]{2,1,0:T(8,128)(2,1)}, u32[]{:S(2)}, u32[]{:S(2)}) collective-permute-start(bf16[48,8,128]{2,1,0:T(8,128)(2,1)} %get-tuple-element.65), channel_id=1, source_target_pairs={{0,4},{1,5},{2,6},{3,7},{4,8},{5,9},{6,10},{7,11},{8,12},{9,13},{1... | collective-permute-start | bytes 294920 | tf_op jit(solution)/shard_map/ppermute | solution.py:346
  102.0 9.0 %collective-permute-start.6 = (bf16[48,8,128]{2,1,0:T(8,128)(2,1)}, bf16[48,8,128]{2,1,0:T(8,128)(2,1)}, u32[]{:S(2)}, u32[]{:S(2)}) collective-permute-start(bf16[48,8,128]{2,1,0:T(8,128)(2,1)} %get-tuple-element.66), channel_id=1, source_target_pairs={{0,5},{1,4},{2,7},{3,6},{4,9},{5,8},{6,11},{7,10},{8,13},{9,12},{1... | collective-permute-start | bytes 294920 | tf_op jit(solution)/shard_map/ppermute | solution.py:346
  109.4 8.0 %collective-permute-start.9 = (bf16[48,8,128]{2,1,0:T(8,128)(2,1)}, bf16[48,8,128]{2,1,0:T(8,128)(2,1)S(1)}, u32[]{:S(2)}, u32[]{:S(2)}) collective-permute-start(bf16[48,8,128]{2,1,0:T(8,128)(2,1)} %get-tuple-element.69), channel_id=1, source_target_pairs={{0,8},{1,9},{2,10},{3,11},{4,12},{5,13},{6,14},{7,15},{8,0},{9,1},... | collective-permute-start | bytes 294920 | tf_op jit(solution)/shard_map/ppermute | solution.py:346
  110.4 11.4 %collective-permute-start.27 = (bf16[48,8,128]{2,1,0:T(8,128)(2,1)}, bf16[48,8,128]{2,1,0:T(8,128)(2,1)S(1)}, u32[]{:S(2)}, u32[]{:S(2)}) collective-permute-start(bf16[48,8,128]{2,1,0:T(8,128)(2,1)} %get-tuple-element.92), channel_id=1, source_target_pairs={{0,1},{1,0},{2,3},{3,2},{4,5},{5,4},{6,7},{7,6},{8,9},{9,8},{10,11... | collective-permute-start | bytes 294920 | tf_op jit(solution)/shard_map/ppermute | solution.py:346
  111.1 11.4 %collective-permute-start.28 = (bf16[48,8,128]{2,1,0:T(8,128)(2,1)}, bf16[48,8,128]{2,1,0:T(8,128)(2,1)S(1)}, u32[]{:S(2)}, u32[]{:S(2)}) collective-permute-start(bf16[48,8,128]{2,1,0:T(8,128)(2,1)} %get-tuple-element.93), channel_id=1, source_target_pairs={{0,2},{1,3},{2,0},{3,1},{4,6},{5,7},{6,4},{7,5},{8,10},{9,11},{10,... | collective-permute-start | bytes 294920 | tf_op jit(solution)/shard_map/ppermute | solution.py:346
  112.4 12.3 %collective-permute-start.29 = (bf16[48,8,128]{2,1,0:T(8,128)(2,1)}, bf16[48,8,128]{2,1,0:T(8,128)(2,1)S(1)}, u32[]{:S(2)}, u32[]{:S(2)}) collective-permute-start(bf16[48,8,128]{2,1,0:T(8,128)(2,1)} %get-tuple-element.94), channel_id=1, source_target_pairs={{0,3},{1,2},{2,1},{3,0},{4,7},{5,6},{6,5},{7,4},{8,11},{9,10},{10,... | collective-permute-start | bytes 294920 | tf_op jit(solution)/shard_map/ppermute | solution.py:346
  113.5 12.9 %collective-permute-start.30 = (bf16[48,8,128]{2,1,0:T(8,128)(2,1)}, bf16[48,8,128]{2,1,0:T(8,128)(2,1)S(1)}, u32[]{:S(2)}, u32[]{:S(2)}) collective-permute-start(bf16[48,8,128]{2,1,0:T(8,128)(2,1)} %get-tuple-element.95), channel_id=1, source_target_pairs={{0,12},{1,13},{2,14},{3,15},{4,0},{5,1},{6,2},{7,3},{8,4},{9,5},{1... | collective-permute-start | bytes 294920 | tf_op jit(solution)/shard_map/ppermute | solution.py:346
  118.0 22.8 %collective-permute-start.31 = (bf16[48,8,128]{2,1,0:T(8,128)(2,1)}, bf16[48,8,128]{2,1,0:T(8,128)(2,1)}, u32[]{:S(2)}, u32[]{:S(2)}) collective-permute-start(bf16[48,8,128]{2,1,0:T(8,128)(2,1)} %get-tuple-element.96), channel_id=1, source_target_pairs={{0,13},{1,12},{2,15},{3,14},{4,1},{5,0},{6,3},{7,2},{8,5},{9,4},{1... | collective-permute-start | bytes 294920 | tf_op jit(solution)/shard_map/ppermute | solution.py:346
  122.4 18.8 %collective-permute-start.32 = (bf16[48,8,128]{2,1,0:T(8,128)(2,1)}, bf16[48,8,128]{2,1,0:T(8,128)(2,1)}, u32[]{:S(2)}, u32[]{:S(2)}) collective-permute-start(bf16[48,8,128]{2,1,0:T(8,128)(2,1)} %get-tuple-element.97), channel_id=1, source_target_pairs={{0,14},{1,15},{2,12},{3,13},{4,2},{5,3},{6,0},{7,1},{8,6},{9,7},{1... | collective-permute-start | bytes 294920 | tf_op jit(solution)/shard_map/ppermute | solution.py:346
  123.1 30.7 %collective-permute-start.33 = (bf16[48,8,128]{2,1,0:T(8,128)(2,1)}, bf16[48,8,128]{2,1,0:T(8,128)(2,1)}, u32[]{:S(2)}, u32[]{:S(2)}) collective-permute-start(bf16[48,8,128]{2,1,0:T(8,128)(2,1)} %get-tuple-element.98), channel_id=1, source_target_pairs={{0,15},{1,14},{2,13},{3,12},{4,3},{5,2},{6,1},{7,0},{8,7},{9,6},{1... | collective-permute-start | bytes 294920 | tf_op jit(solution)/shard_map/ppermute | solution.py:346
  125.3 28.7 %collective-permute-start.23 = (bf16[48,8,128]{2,1,0:T(8,128)(2,1)}, bf16[48,8,128]{2,1,0:T(8,128)(2,1)S(1)}, u32[]{:S(2)}, u32[]{:S(2)}) collective-permute-start(bf16[48,8,128]{2,1,0:T(8,128)(2,1)} %get-tuple-element.87), channel_id=1, source_target_pairs={{0,4},{1,5},{2,6},{3,7},{4,8},{5,9},{6,10},{7,11},{8,12},{9,13},{1... | collective-permute-start | bytes 294920 | tf_op jit(solution)/shard_map/ppermute | solution.py:346
  127.0 29.0 %collective-permute-start.24 = (bf16[48,8,128]{2,1,0:T(8,128)(2,1)}, bf16[48,8,128]{2,1,0:T(8,128)(2,1)S(1)}, u32[]{:S(2)}, u32[]{:S(2)}) collective-permute-start(bf16[48,8,128]{2,1,0:T(8,128)(2,1)} %get-tuple-element.88), channel_id=1, source_target_pairs={{0,5},{1,4},{2,7},{3,6},{4,9},{5,8},{6,11},{7,10},{8,13},{9,12},{1... | collective-permute-start | bytes 294920 | tf_op jit(solution)/shard_map/ppermute | solution.py:346
  140.8 16.1 %collective-permute-start.25 = (bf16[48,8,128]{2,1,0:T(8,128)(2,1)}, bf16[48,8,128]{2,1,0:T(8,128)(2,1)S(1)}, u32[]{:S(2)}, u32[]{:S(2)}) collective-permute-start(bf16[48,8,128]{2,1,0:T(8,128)(2,1)} %get-tuple-element.89), channel_id=1, source_target_pairs={{0,6},{1,7},{2,4},{3,5},{4,10},{5,11},{6,8},{7,9},{8,14},{9,15},{1... | collective-permute-start | bytes 294920 | tf_op jit(solution)/shard_map/ppermute | solution.py:346
  141.3 17.7 %collective-permute-start.26 = (bf16[48,8,128]{2,1,0:T(8,128)(2,1)}, bf16[48,8,128]{2,1,0:T(8,128)(2,1)S(1)}, u32[]{:S(2)}, u32[]{:S(2)}) collective-permute-start(bf16[48,8,128]{2,1,0:T(8,128)(2,1)} %get-tuple-element.90), channel_id=1, source_target_pairs={{0,7},{1,6},{2,5},{3,4},{4,11},{5,10},{6,9},{7,8},{8,15},{9,14},{1... | collective-permute-start | bytes 294920 | tf_op jit(solution)/shard_map/ppermute | solution.py:346
  153.8 29.2 %collective-permute-start.17 = (f32[3,64,256]{2,1,0:T(8,128)S(1)}, f32[3,64,256]{2,1,0:T(8,128)S(1)}, u32[]{:S(2)}, u32[]{:S(2)}) collective-permute-start(f32[3,64,256]{2,1,0:T(8,128)S(1)} %get-tuple-element.79), channel_id=1, source_target_pairs={{3,0},{0,1},{1,4},{4,5},{5,8},{8,9},{9,12},{12,13},{13,14},{14,15}... | collective-permute-start | bytes 589832 | tf_op jit(solution)/shard_map/ppermute | solution.py:367
  154.1 12.7 %collective-permute-start.19 = (bf16[48,8,128]{2,1,0:T(8,128)(2,1)S(1)}, bf16[48,8,128]{2,1,0:T(8,128)(2,1)S(1)}, u32[]{:S(2)}, u32[]{:S(2)}) collective-permute-start(bf16[48,8,128]{2,1,0:T(8,128)(2,1)S(1)} %copy-done.21), channel_id=1, source_target_pairs={{0,8},{1,9},{2,10},{3,11},{4,12},{5,13},{6,14},{7,15},{8,0},{9,1},... | collective-permute-start | bytes 294920 | tf_op jit(solution)/shard_map/ppermute | solution.py:346
  156.0 13.3 %collective-permute-start.20 = (bf16[48,8,128]{2,1,0:T(8,128)(2,1)S(1)}, bf16[48,8,128]{2,1,0:T(8,128)(2,1)S(1)}, u32[]{:S(2)}, u32[]{:S(2)}) collective-permute-start(bf16[48,8,128]{2,1,0:T(8,128)(2,1)S(1)} %copy-done.20), channel_id=1, source_target_pairs={{0,9},{1,8},{2,11},{3,10},{4,13},{5,12},{6,15},{7,14},{8,1},{9,0},... | collective-permute-start | bytes 294920 | tf_op jit(solution)/shard_map/ppermute | solution.py:346
  156.9 16.8 %collective-permute-start.21 = (bf16[48,8,128]{2,1,0:T(8,128)(2,1)S(1)}, bf16[48,8,128]{2,1,0:T(8,128)(2,1)S(1)}, u32[]{:S(2)}, u32[]{:S(2)}) collective-permute-start(bf16[48,8,128]{2,1,0:T(8,128)(2,1)S(1)} %copy-done.19), channel_id=1, source_target_pairs={{0,10},{1,11},{2,8},{3,9},{4,14},{5,15},{6,12},{7,13},{8,2},{9,3},... | collective-permute-start | bytes 294920 | tf_op jit(solution)/shard_map/ppermute | solution.py:346
  159.0 17.3 %collective-permute-start.22 = (bf16[48,8,128]{2,1,0:T(8,128)(2,1)S(1)}, bf16[48,8,128]{2,1,0:T(8,128)(2,1)S(1)}, u32[]{:S(2)}, u32[]{:S(2)}) collective-permute-start(bf16[48,8,128]{2,1,0:T(8,128)(2,1)S(1)} %copy-done.18), channel_id=1, source_target_pairs={{0,11},{1,10},{2,9},{3,8},{4,15},{5,14},{6,13},{7,12},{8,3},{9,2},... | collective-permute-start | bytes 294920 | tf_op jit(solution)/shard_map/ppermute | solution.py:346
  166.7 16.2 %collective-permute-start = (f32[4,64,256]{2,1,0:T(8,128)S(1)}, f32[4,64,256]{2,1,0:T(8,128)S(1)}, u32[]{:S(2)}, u32[]{:S(2)}) collective-permute-start(f32[4,64,256]{2,1,0:T(8,128)S(1)} %get-tuple-element.57), channel_id=1, source_target_pairs={{3,0},{0,1},{1,4},{4,5},{5,8},{8,9},{9,12},{12,13},{13,14},{14,15}... | collective-permute-start | bytes 786440 | tf_op jit(solution)/shard_map/ppermute | solution.py:367
  169.4 13.6 %collective-permute-start.1 = (f32[4,64,256]{2,1,0:T(8,128)S(1)}, f32[4,64,256]{2,1,0:T(8,128)S(1)}, u32[]{:S(2)}, u32[]{:S(2)}) collective-permute-start(f32[4,64,256]{2,1,0:T(8,128)S(1)} %get-tuple-element.58), channel_id=1, source_target_pairs={{0,3},{1,0},{4,1},{5,4},{8,5},{9,8},{12,9},{13,12},{14,13},{15,14}... | collective-permute-start | bytes 786440 | tf_op jit(solution)/shard_map/ppermute | solution.py:366
  173.8 9.2 %collective-permute-start.18 = (f32[3,64,256]{2,1,0:T(8,128)S(1)}, f32[3,64,256]{2,1,0:T(8,128)S(1)}, u32[]{:S(2)}, u32[]{:S(2)}) collective-permute-start(f32[3,64,256]{2,1,0:T(8,128)S(1)} %get-tuple-element.80), channel_id=1, source_target_pairs={{0,3},{1,0},{4,1},{5,4},{8,5},{9,8},{12,9},{13,12},{14,13},{15,14}... | collective-permute-start | bytes 589832 | tf_op jit(solution)/shard_map/ppermute | solution.py:366
  (27 other events, 335.0 us)

commit v5 on v4

--- a/solution.py
+++ b/solution.py
@@ -410,6 +410,11 @@
         functools.partial(part_kernel, names=middle, held=held), swapped, (*[pieces[m] for m in middle], part), [comp],
         piece_bufs(len(middle)), aliases={2 + len(middle): 0}, remote=len(middle),
     )
+    middle, far = far[: len(far) // 2], far[len(far) // 2 :]
+    (part,) = call(
+        functools.partial(part_kernel, names=middle, held=held), swapped, (*[pieces[m] for m in middle], part), [comp],
+        piece_bufs(len(middle)), aliases={2 + len(middle): 0}, remote=len(middle),
+    )
     far_pieces = [pieces[m] for m in far]
     _, own, up, down = call(
         functools.partial(last_step_kernel, group=group, names=far, held=held),

time: 207 us -> 208 us (level)
    pallas_call x8 -> x9, Pallas kernels: 26.3 us -> 27.1 us  [call(): pl.pallas_call(kernel, out_shape=outs, grid_spec=pltpu.PrefetchScalarGrid...]
where the time goes in v5:
time: 208 us; the launch traced here: 205 us
  waiting for transfers between devices  81 us (39%)
  starting transfers between devices  57 us (27%)
  Pallas kernels  37.9 us (18%)
  blocking collectives  15.1 us (7%)
  local copies, waits for them, and re-layouts  11.7 us (6%)
  other arithmetic  2.09 us (1%)
    ppermute x30, waiting for transfers between devices, scatter(): lax.ppermute(sends[m], 'grid', [(i, shifted(i, m, group)) for i in range(...  76.2 us
    ppermute x30, starting transfers between devices, scatter(): lax.ppermute(sends[m], 'grid', [(i, shifted(i, m, group)) for i in range(...  42.6 us
    pallas_call x9, Pallas kernels, call(): pl.pallas_call(kernel, out_shape=outs, grid_spec=pltpu.PrefetchScalarGrid...  27.1 us
    all_to_all x1, blocking collectives, local(): got = lax.all_to_all(dealt, 'grid', split_axis=0, concat_axis=0, tiled=True)  15.1 us
    unnamed x44, local copies, waits for them, and re-layouts  9.63 us
    pallas_call x2, Pallas kernels, cut(): pl.pallas_call(cut_kernel, out_shape=[pltpu.HBM(piece, cells.dtype)] * gr...  7.07 us
    all_to_all x1, starting transfers between devices, local(): got = lax.all_to_all(bulk, 'grid', split_axis=0, concat_axis=0, tiled=True)  6.53 us
    ppermute x3, starting transfers between devices, exchange(): lax.ppermute(down, 'grid', [(at[s - 1], at[s]) for s in range(group)])  4.85 us
  transfers between devices with their start and end apart: 37, of which 8 were waited for; matrix products, arithmetic and copies ran while one was open for 2% of the time, Pallas kernels for 16%

profile of v5, /device:TPU:13, one launch (start us, length us, event | category | flops | bytes accessed | tf_op | source)
XLA Modules:
  0.0 205.1 jit_solution(15082448541194442806)
XLA Ops:
  0.0 3.7 %bulk_cut.1 = bf16[16,97,8,128]{3,2,1,0:T(8,128)(2,1)} custom-call(s32[1,24]{1,0:T(1,128)} %bitcast.16, s32[1,24]{1,0:T(1,128)} %bitcast.17, s32[1,24]{1,0:T(1,128)} %bitcast.18, bf16[24,4,2,16,8,128]{5,4,3,2,1,0:T(8,128)(2,1)} %bitcast.12), custom_call_target="tpu_custom_call" | custom-call | tf_op jit(solution)/shard_map/bulk_cut/pallas_call | solution.py:89
  3.7 6.5 %all-to-all-start = ((bf16[16,97,8,128]{3,2,1,0:T(8,128)(2,1)}), bf16[16,97,8,128]{3,2,1,0:T(8,128)(2,1)S(1)}, u32[]{:S(2)}, u32[]{:S(2)}) async-start(bf16[16,97,8,128]{3,2,1,0:T(8,128)(2,1)} %bulk_cut.1), calls=%async_computation | async-start | bytes 6356992 | tf_op jit(solution)/shard_map/all_to_all | solution.py:339
  10.3 3.6 %cut.2 = (bf16[48,8,128]{2,1,0:T(8,128)(2,1)}, bf16[48,8,128]{2,1,0:T(8,128)(2,1)}, bf16[48,8,128]{2,1,0:T(8,128)(2,1)}, bf16[48,8,128]{2,1,0:T(8,128)(2,1)}, bf...) custom-call(s32[16]{0:T(128)S(1)} %fusion.7.strip_ref, ...), custom_call_target="tpu_custom_call" | custom-call | tf_op jit(solution)/shard_map/cut/pallas_call | solution.py:117
  13.8 2.4 %collective-permute-start.10 = (bf16[48,8,128]{2,1,0:T(8,128)(2,1)}, bf16[48,8,128]{2,1,0:T(8,128)(2,1)S(1)}, u32[]{:S(2)}, u32[]{:S(2)}) collective-permute-start(bf16[48,8,128]{2,1,0:T(8,128)(2,1)} %get-tuple-element.70), channel_id=1, source_target_pairs={{0,9},{1,8},{2,11},{3,10},{4,13},{5,12},{6,15},{7,14},{8,1},{9,0},... | collective-permute-start | bytes 294920 | tf_op jit(solution)/shard_map/ppermute | solution.py:346
  16.5 3.3 %collective-permute-start.12 = (bf16[48,8,128]{2,1,0:T(8,128)(2,1)}, bf16[48,8,128]{2,1,0:T(8,128)(2,1)S(1)}, u32[]{:S(2)}, u32[]{:S(2)}) collective-permute-start(bf16[48,8,128]{2,1,0:T(8,128)(2,1)} %get-tuple-element.72), channel_id=1, source_target_pairs={{0,11},{1,10},{2,9},{3,8},{4,15},{5,14},{6,13},{7,12},{8,3},{9,2},... | collective-permute-start | bytes 294920 | tf_op jit(solution)/shard_map/ppermute | solution.py:346
  20.0 1.5 collective-permute-start.14
  21.5 3.5 %cut.3 = (bf16[48,8,128]{2,1,0:T(8,128)(2,1)}, bf16[48,8,128]{2,1,0:T(8,128)(2,1)}, bf16[48,8,128]{2,1,0:T(8,128)(2,1)}, bf16[48,8,128]{2,1,0:T(8,128)(2,1)}, bf...) custom-call(s32[16]{0:T(128)S(1)} %fusion.7.strip_ref, ...), custom_call_target="tpu_custom_call" | custom-call | tf_op jit(solution)/shard_map/cut/pallas_call | solution.py:117
  26.1 65.2 %collective-permute-done.10.refs_9_ = bf16[48,8,128]{2,1,0:T(8,128)(2,1)S(1)} collective-permute-done((bf16[48,8,128]{2,1,0:T(8,128)(2,1)}, bf16[48,8,128]{2,1,0:T(8,128)(2,1)S(1)}, u32[]{:S(2)}, u32[]{:S(2)}) %collective-permute-start.10) | collective-permute-done | bytes 98336 | tf_op jit(solution)/shard_map/ppermute | solution.py:346
  91.3 2.1 %collective-permute-done.11.refs_10_ = bf16[48,8,128]{2,1,0:T(8,128)(2,1)S(1)} collective-permute-done((bf16[48,8,128]{2,1,0:T(8,128)(2,1)}, bf16[48,8,128]{2,1,0:T(8,128)(2,1)S(1)}, u32[]{:S(2)}, u32[]{:S(2)}) %collective-permute-start.11) | collective-permute-done | bytes 98336 | tf_op jit(solution)/shard_map/ppermute | solution.py:346
  93.4 3.5 %collective-permute-start.16 = (bf16[48,8,128]{2,1,0:T(8,128)(2,1)}, bf16[48,8,128]{2,1,0:T(8,128)(2,1)}, u32[]{:S(2)}, u32[]{:S(2)}) collective-permute-start(bf16[48,8,128]{2,1,0:T(8,128)(2,1)} %get-tuple-element.76), channel_id=1, source_target_pairs={{0,15},{1,14},{2,13},{3,12},{4,3},{5,2},{6,1},{7,0},{8,7},{9,6},{1... | collective-permute-start | bytes 294920 | tf_op jit(solution)/shard_map/ppermute | solution.py:346
  100.6 1.4 collective-permute-done.16.refs_15_
  102.0 1.8 collective-permute-start.6
  104.5 2.5 %collective-permute-start.7 = (bf16[48,8,128]{2,1,0:T(8,128)(2,1)}, bf16[48,8,128]{2,1,0:T(8,128)(2,1)}, u32[]{:S(2)}, u32[]{:S(2)}) collective-permute-start(bf16[48,8,128]{2,1,0:T(8,128)(2,1)} %get-tuple-element.67), channel_id=1, source_target_pairs={{0,6},{1,7},{2,4},{3,5},{4,10},{5,11},{6,8},{7,9},{8,14},{9,15},{1... | collective-permute-start | bytes 294920 | tf_op jit(solution)/shard_map/ppermute | solution.py:346
  113.5 3.4 %collective-permute-start.30 = (bf16[48,8,128]{2,1,0:T(8,128)(2,1)}, bf16[48,8,128]{2,1,0:T(8,128)(2,1)S(1)}, u32[]{:S(2)}, u32[]{:S(2)}) collective-permute-start(bf16[48,8,128]{2,1,0:T(8,128)(2,1)} %get-tuple-element.95), channel_id=1, source_target_pairs={{0,12},{1,13},{2,14},{3,15},{4,0},{5,1},{6,2},{7,3},{8,4},{9,5},{1... | collective-permute-start | bytes 294920 | tf_op jit(solution)/shard_map/ppermute | solution.py:346
  118.0 3.8 %collective-permute-start.31 = (bf16[48,8,128]{2,1,0:T(8,128)(2,1)}, bf16[48,8,128]{2,1,0:T(8,128)(2,1)}, u32[]{:S(2)}, u32[]{:S(2)}) collective-permute-start(bf16[48,8,128]{2,1,0:T(8,128)(2,1)} %get-tuple-element.96), channel_id=1, source_target_pairs={{0,13},{1,12},{2,15},{3,14},{4,1},{5,0},{6,3},{7,2},{8,5},{9,4},{1... | collective-permute-start | bytes 294920 | tf_op jit(solution)/shard_map/ppermute | solution.py:346
  123.1 1.6 collective-permute-start.33
  127.0 1.7 collective-permute-start.24
  130.3 10.5 %shard_map.46 = (f32[512,2,8,128]{3,2,1,0:T(8,128)S(1)}, f32[4,2,64,256]{3,2,1,0:T(8,128)S(1)}, f32[4,64,256]{2,1,0:T(8,128)S(1)}, f32[4,64,256]{2,1,0:T(8,128)S(1)}) custom-call(s32[16]{0:T(128)S(1)} %fusion.7.strip_ref, s32[384]{0:T(512)S(1)} %add.167.place_ref, f32[384]{0:T(512)S(1)} %convert_divide_fusion.share_ref, ...), custom_call_target="tpu_custom_call" | custom-call | tf_op jit(solution)/shard_map/pallas_call | solution.py:254
  141.3 2.1 %collective-permute-start.26 = (bf16[48,8,128]{2,1,0:T(8,128)(2,1)}, bf16[48,8,128]{2,1,0:T(8,128)(2,1)S(1)}, u32[]{:S(2)}, u32[]{:S(2)}) collective-permute-start(bf16[48,8,128]{2,1,0:T(8,128)(2,1)} %get-tuple-element.90), channel_id=1, source_target_pairs={{0,7},{1,6},{2,5},{3,4},{4,11},{5,10},{6,9},{7,8},{8,15},{9,14},{1... | collective-permute-start | bytes 294920 | tf_op jit(solution)/shard_map/ppermute | solution.py:346
  147.9 5.9 %shard_map.47 = (f32[512,2,8,128]{3,2,1,0:T(8,128)S(1)}, f32[3,2,64,256]{3,2,1,0:T(8,128)S(1)}, f32[3,64,256]{2,1,0:T(8,128)S(1)}, f32[3,64,256]{2,1,0:T(8,128)S(1)}) custom-call(s32[16]{0:T(128)S(1)} %fusion.7.strip_ref, s32[384]{0:T(512)S(1)} %reshape.176.place_ref, f32[384]{0:T(512)S(1)} %reshape.177.share_ref, ...), custom_call_target="tpu_custom_call" | custom-call | tf_op jit(solution)/shard_map/pallas_call | solution.py:254
  154.1 1.9 collective-permute-start.21
  156.9 2.1 %collective-permute-start.19 = (bf16[48,8,128]{2,1,0:T(8,128)(2,1)S(1)}, bf16[48,8,128]{2,1,0:T(8,128)(2,1)S(1)}, u32[]{:S(2)}, u32[]{:S(2)}) collective-permute-start(bf16[48,8,128]{2,1,0:T(8,128)(2,1)S(1)} %copy-done.19), channel_id=1, source_target_pairs={{0,10},{1,11},{2,8},{3,9},{4,14},{5,15},{6,12},{7,13},{8,2},{9,3},... | collective-permute-start | bytes 294920 | tf_op jit(solution)/shard_map/ppermute | solution.py:346
  160.3 6.5 %collective-permute-done.21.refs_0_ = bf16[48,8,128]{2,1,0:T(8,128)(2,1)S(1)} collective-permute-done((bf16[48,8,128]{2,1,0:T(8,128)(2,1)S(1)}, bf16[48,8,128]{2,1,0:T(8,128)(2,1)S(1)}, u32[]{:S(2)}, u32[]{:S(2)}) %collective-permute-start.21) | collective-permute-done | bytes 98336 | tf_op jit(solution)/shard_map/ppermute | solution.py:346
  166.7 2.6 %collective-permute-start = (f32[4,64,256]{2,1,0:T(8,128)S(1)}, f32[4,64,256]{2,1,0:T(8,128)S(1)}, u32[]{:S(2)}, u32[]{:S(2)}) collective-permute-start(f32[4,64,256]{2,1,0:T(8,128)S(1)} %get-tuple-element.57), channel_id=1, source_target_pairs={{3,0},{0,1},{1,4},{4,5},{5,8},{8,9},{9,12},{12,13},{13,14},{14,15}... | collective-permute-start | bytes 786440 | tf_op jit(solution)/shard_map/ppermute | solution.py:367
  169.9 2.3 %shard_map.49.refs_4_ = f32[512,2,8,128]{3,2,1,0:T(8,128)S(1)} custom-call(s32[384]{0:T(512)S(1)} %reshape.176.place_ref, f32[384]{0:T(512)S(1)} %reshape.177.share_ref, bf16[48,8,128]{2,1,0:T(8,128)(2,1)} %get-tuple-element.91.refs_0_, bf16[48,8,128]{2,1,0:T(8,128)(2,1)S(1)} %copy-done.9, bf16[48,8,128]{2,1,0:T(8,128)(2,1)S(1)} %copy-done.11, ...), custom_call_target="tpu_custom_call" | custom-call | tf_op jit(solution)/shard_map/pallas_call | solution.py:254
  172.2 1.5 shard_map.50.refs_2_
  174.8 2.5 %collective-permute-start.18 = (f32[3,64,256]{2,1,0:T(8,128)S(1)}, f32[3,64,256]{2,1,0:T(8,128)S(1)}, u32[]{:S(2)}, u32[]{:S(2)}) collective-permute-start(f32[3,64,256]{2,1,0:T(8,128)S(1)} %get-tuple-element.80), channel_id=1, source_target_pairs={{0,3},{1,0},{4,1},{5,4},{8,5},{9,8},{12,9},{13,12},{14,13},{15,14}... | collective-permute-start | bytes 589832 | tf_op jit(solution)/shard_map/ppermute | solution.py:366
  177.3 4.5 %shard_map.52 = (f32[512,2,8,128]{3,2,1,0:T(8,128)S(1)}, f32[3,2,64,256]{3,2,1,0:T(8,128)S(1)}, f32[3,64,256]{2,1,0:T(8,128)S(1)}, f32[3,64,256]{2,1,0:T(8,128)S(1)}) custom-call(s32[16]{0:T(128)S(1)} %fusion.7.strip_ref, s32[384]{0:T(512)S(1)} %reshape.176.place_ref, f32[384]{0:T(512)S(1)} %reshape.177.share_ref, ...), custom_call_target="tpu_custom_call", output_to_operand_aliasing={{0}: (7, {})} | custom-call | tf_op jit(solution)/shard_map/pallas_call | solution.py:254
  181.8 2.0 collective-permute-start.34
  184.0 2.3 %collective-permute-done.34.above_ref = f32[3,64,256]{2,1,0:T(8,128)S(1)} collective-permute-done((f32[3,64,256]{2,1,0:T(8,128)S(1)}, f32[3,64,256]{2,1,0:T(8,128)S(1)}, u32[]{:S(2)}, u32[]{:S(2)}) %collective-permute-start.34) | collective-permute-done | bytes 196640 | tf_op jit(solution)/shard_map/ppermute | solution.py:367
  186.4 2.5 %collective-permute-done.35.below_ref = f32[3,64,256]{2,1,0:T(8,128)S(1)} collective-permute-done((f32[3,64,256]{2,1,0:T(8,128)S(1)}, f32[3,64,256]{2,1,0:T(8,128)S(1)}, u32[]{:S(2)}, u32[]{:S(2)}) %collective-permute-start.35) | collective-permute-done | bytes 196640 | tf_op jit(solution)/shard_map/ppermute | solution.py:366
  189.0 15.1 %all_to_all.10.got_ref = f32[16,24,256]{2,1,0:T(8,128)S(1)} all-to-all(f32[16,24,256]{2,1,0:T(8,128)S(1)} %pad_maximum_fusion), channel_id=1, replica_groups=mesh['region'=2,'grid'=16] {'grid'}, dimensions={0} | all-to-all | bytes 786432 | tf_op jit(solution)/shard_map/all_to_all | solution.py:431
  (116 shorter events, 28.9 us)
Async XLA Ops:
  3.7 95.5 %all-to-all-start = ((bf16[16,97,8,128]{3,2,1,0:T(8,128)(2,1)}), bf16[16,97,8,128]{3,2,1,0:T(8,128)(2,1)S(1)}, u32[]{:S(2)}, u32[]{:S(2)}) async-start(bf16[16,97,8,128]{3,2,1,0:T(8,128)(2,1)} %bulk_cut.1), calls=%async_computation | async-start | bytes 6356992 | tf_op jit(solution)/shard_map/all_to_all | solution.py:339
  13.8 77.4 %collective-permute-start.10 = (bf16[48,8,128]{2,1,0:T(8,128)(2,1)}, bf16[48,8,128]{2,1,0:T(8,128)(2,1)S(1)}, u32[]{:S(2)}, u32[]{:S(2)}) collective-permute-start(bf16[48,8,128]{2,1,0:T(8,128)(2,1)} %get-tuple-element.70), channel_id=1, source_target_pairs={{0,9},{1,8},{2,11},{3,10},{4,13},{5,12},{6,15},{7,14},{8,1},{9,0},... | collective-permute-start | bytes 294920 | tf_op jit(solution)/shard_map/ppermute | solution.py:346
  16.2 77.2 %collective-permute-start.11 = (bf16[48,8,128]{2,1,0:T(8,128)(2,1)}, bf16[48,8,128]{2,1,0:T(8,128)(2,1)S(1)}, u32[]{:S(2)}, u32[]{:S(2)}) collective-permute-start(bf16[48,8,128]{2,1,0:T(8,128)(2,1)} %get-tuple-element.71), channel_id=1, source_target_pairs={{0,10},{1,11},{2,8},{3,9},{4,14},{5,15},{6,12},{7,13},{8,2},{9,3},... | collective-permute-start | bytes 294920 | tf_op jit(solution)/shard_map/ppermute | solution.py:346
  16.5 80.4 %collective-permute-start.12 = (bf16[48,8,128]{2,1,0:T(8,128)(2,1)}, bf16[48,8,128]{2,1,0:T(8,128)(2,1)S(1)}, u32[]{:S(2)}, u32[]{:S(2)}) collective-permute-start(bf16[48,8,128]{2,1,0:T(8,128)(2,1)} %get-tuple-element.72), channel_id=1, source_target_pairs={{0,11},{1,10},{2,9},{3,8},{4,15},{5,14},{6,13},{7,12},{8,3},{9,2},... | collective-permute-start | bytes 294920 | tf_op jit(solution)/shard_map/ppermute | solution.py:346
  19.7 78.5 %collective-permute-start.13 = (bf16[48,8,128]{2,1,0:T(8,128)(2,1)}, bf16[48,8,128]{2,1,0:T(8,128)(2,1)S(1)}, u32[]{:S(2)}, u32[]{:S(2)}) collective-permute-start(bf16[48,8,128]{2,1,0:T(8,128)(2,1)} %get-tuple-element.73), channel_id=1, source_target_pairs={{0,12},{1,13},{2,14},{3,15},{4,0},{5,1},{6,2},{7,3},{8,4},{9,5},{1... | collective-permute-start | bytes 294920 | tf_op jit(solution)/shard_map/ppermute | solution.py:346
  20.0 79.2 %collective-permute-start.14 = (bf16[48,8,128]{2,1,0:T(8,128)(2,1)}, bf16[48,8,128]{2,1,0:T(8,128)(2,1)}, u32[]{:S(2)}, u32[]{:S(2)}) collective-permute-start(bf16[48,8,128]{2,1,0:T(8,128)(2,1)} %get-tuple-element.74), channel_id=1, source_target_pairs={{0,13},{1,12},{2,15},{3,14},{4,1},{5,0},{6,3},{7,2},{8,5},{9,4},{1... | collective-permute-start | bytes 294920 | tf_op jit(solution)/shard_map/ppermute | solution.py:346
  91.3 9.3 %collective-permute-start.15 = (bf16[48,8,128]{2,1,0:T(8,128)(2,1)}, bf16[48,8,128]{2,1,0:T(8,128)(2,1)}, u32[]{:S(2)}, u32[]{:S(2)}) collective-permute-start(bf16[48,8,128]{2,1,0:T(8,128)(2,1)} %get-tuple-element.75), channel_id=1, source_target_pairs={{0,14},{1,15},{2,12},{3,13},{4,2},{5,3},{6,0},{7,1},{8,6},{9,7},{1... | collective-permute-start | bytes 294920 | tf_op jit(solution)/shard_map/ppermute | solution.py:346
  93.4 8.7 %collective-permute-start.16 = (bf16[48,8,128]{2,1,0:T(8,128)(2,1)}, bf16[48,8,128]{2,1,0:T(8,128)(2,1)}, u32[]{:S(2)}, u32[]{:S(2)}) collective-permute-start(bf16[48,8,128]{2,1,0:T(8,128)(2,1)} %get-tuple-element.76), channel_id=1, source_target_pairs={{0,15},{1,14},{2,13},{3,12},{4,3},{5,2},{6,1},{7,0},{8,7},{9,6},{1... | collective-permute-start | bytes 294920 | tf_op jit(solution)/shard_map/ppermute | solution.py:346
  98.9 8.1 %collective-permute-start.3 = (bf16[48,8,128]{2,1,0:T(8,128)(2,1)}, bf16[48,8,128]{2,1,0:T(8,128)(2,1)}, u32[]{:S(2)}, u32[]{:S(2)}) collective-permute-start(bf16[48,8,128]{2,1,0:T(8,128)(2,1)} %get-tuple-element.63), channel_id=1, source_target_pairs={{0,2},{1,3},{2,0},{3,1},{4,6},{5,7},{6,4},{7,5},{8,10},{9,11},{10,... | collective-permute-start | bytes 294920 | tf_op jit(solution)/shard_map/ppermute | solution.py:346
  99.3 10.1 %collective-permute-start.4 = (bf16[48,8,128]{2,1,0:T(8,128)(2,1)}, bf16[48,8,128]{2,1,0:T(8,128)(2,1)}, u32[]{:S(2)}, u32[]{:S(2)}) collective-permute-start(bf16[48,8,128]{2,1,0:T(8,128)(2,1)} %get-tuple-element.64), channel_id=1, source_target_pairs={{0,3},{1,2},{2,1},{3,0},{4,7},{5,6},{6,5},{7,4},{8,11},{9,10},{10,... | collective-permute-start | bytes 294920 | tf_op jit(solution)/shard_map/ppermute | solution.py:346
  100.6 9.7 %collective-permute-start.5 = (bf16[48,8,128]{2,1,0:T(8,128)(2,1)}, bf16[48,8,128]{2,1,0:T(8,128)(2,1)}, u32[]{:S(2)}, u32[]{:S(2)}) collective-permute-start(bf16[48,8,128]{2,1,0:T(8,128)(2,1)} %get-tuple-element.65), channel_id=1, source_target_pairs={{0,4},{1,5},{2,6},{3,7},{4,8},{5,9},{6,10},{7,11},{8,12},{9,13},{1... | collective-permute-start | bytes 294920 | tf_op jit(solution)/shard_map/ppermute | solution.py:346
  102.0 9.0 %collective-permute-start.6 = (bf16[48,8,128]{2,1,0:T(8,128)(2,1)}, bf16[48,8,128]{2,1,0:T(8,128)(2,1)}, u32[]{:S(2)}, u32[]{:S(2)}) collective-permute-start(bf16[48,8,128]{2,1,0:T(8,128)(2,1)} %get-tuple-element.66), channel_id=1, source_target_pairs={{0,5},{1,4},{2,7},{3,6},{4,9},{5,8},{6,11},{7,10},{8,13},{9,12},{1... | collective-permute-start | bytes 294920 | tf_op jit(solution)/shard_map/ppermute | solution.py:346
  109.4 8.0 %collective-permute-start.9 = (bf16[48,8,128]{2,1,0:T(8,128)(2,1)}, bf16[48,8,128]{2,1,0:T(8,128)(2,1)S(1)}, u32[]{:S(2)}, u32[]{:S(2)}) collective-permute-start(bf16[48,8,128]{2,1,0:T(8,128)(2,1)} %get-tuple-element.69), channel_id=1, source_target_pairs={{0,8},{1,9},{2,10},{3,11},{4,12},{5,13},{6,14},{7,15},{8,0},{9,1},... | collective-permute-start | bytes 294920 | tf_op jit(solution)/shard_map/ppermute | solution.py:346
  110.4 11.4 %collective-permute-start.27 = (bf16[48,8,128]{2,1,0:T(8,128)(2,1)}, bf16[48,8,128]{2,1,0:T(8,128)(2,1)S(1)}, u32[]{:S(2)}, u32[]{:S(2)}) collective-permute-start(bf16[48,8,128]{2,1,0:T(8,128)(2,1)} %get-tuple-element.92), channel_id=1, source_target_pairs={{0,1},{1,0},{2,3},{3,2},{4,5},{5,4},{6,7},{7,6},{8,9},{9,8},{10,11... | collective-permute-start | bytes 294920 | tf_op jit(solution)/shard_map/ppermute | solution.py:346
  111.1 11.4 %collective-permute-start.28 = (bf16[48,8,128]{2,1,0:T(8,128)(2,1)}, bf16[48,8,128]{2,1,0:T(8,128)(2,1)S(1)}, u32[]{:S(2)}, u32[]{:S(2)}) collective-permute-start(bf16[48,8,128]{2,1,0:T(8,128)(2,1)} %get-tuple-element.93), channel_id=1, source_target_pairs={{0,2},{1,3},{2,0},{3,1},{4,6},{5,7},{6,4},{7,5},{8,10},{9,11},{10,... | collective-permute-start | bytes 294920 | tf_op jit(solution)/shard_map/ppermute | solution.py:346
  112.4 12.3 %collective-permute-start.29 = (bf16[48,8,128]{2,1,0:T(8,128)(2,1)}, bf16[48,8,128]{2,1,0:T(8,128)(2,1)S(1)}, u32[]{:S(2)}, u32[]{:S(2)}) collective-permute-start(bf16[48,8,128]{2,1,0:T(8,128)(2,1)} %get-tuple-element.94), channel_id=1, source_target_pairs={{0,3},{1,2},{2,1},{3,0},{4,7},{5,6},{6,5},{7,4},{8,11},{9,10},{10,... | collective-permute-start | bytes 294920 | tf_op jit(solution)/shard_map/ppermute | solution.py:346
  113.5 12.9 %collective-permute-start.30 = (bf16[48,8,128]{2,1,0:T(8,128)(2,1)}, bf16[48,8,128]{2,1,0:T(8,128)(2,1)S(1)}, u32[]{:S(2)}, u32[]{:S(2)}) collective-permute-start(bf16[48,8,128]{2,1,0:T(8,128)(2,1)} %get-tuple-element.95), channel_id=1, source_target_pairs={{0,12},{1,13},{2,14},{3,15},{4,0},{5,1},{6,2},{7,3},{8,4},{9,5},{1... | collective-permute-start | bytes 294920 | tf_op jit(solution)/shard_map/ppermute | solution.py:346
  118.0 22.8 %collective-permute-start.31 = (bf16[48,8,128]{2,1,0:T(8,128)(2,1)}, bf16[48,8,128]{2,1,0:T(8,128)(2,1)}, u32[]{:S(2)}, u32[]{:S(2)}) collective-permute-start(bf16[48,8,128]{2,1,0:T(8,128)(2,1)} %get-tuple-element.96), channel_id=1, source_target_pairs={{0,13},{1,12},{2,15},{3,14},{4,1},{5,0},{6,3},{7,2},{8,5},{9,4},{1... | collective-permute-start | bytes 294920 | tf_op jit(solution)/shard_map/ppermute | solution.py:346
  122.4 18.8 %collective-permute-start.32 = (bf16[48,8,128]{2,1,0:T(8,128)(2,1)}, bf16[48,8,128]{2,1,0:T(8,128)(2,1)}, u32[]{:S(2)}, u32[]{:S(2)}) collective-permute-start(bf16[48,8,128]{2,1,0:T(8,128)(2,1)} %get-tuple-element.97), channel_id=1, source_target_pairs={{0,14},{1,15},{2,12},{3,13},{4,2},{5,3},{6,0},{7,1},{8,6},{9,7},{1... | collective-permute-start | bytes 294920 | tf_op jit(solution)/shard_map/ppermute | solution.py:346
  123.1 30.7 %collective-permute-start.33 = (bf16[48,8,128]{2,1,0:T(8,128)(2,1)}, bf16[48,8,128]{2,1,0:T(8,128)(2,1)}, u32[]{:S(2)}, u32[]{:S(2)}) collective-permute-start(bf16[48,8,128]{2,1,0:T(8,128)(2,1)} %get-tuple-element.98), channel_id=1, source_target_pairs={{0,15},{1,14},{2,13},{3,12},{4,3},{5,2},{6,1},{7,0},{8,7},{9,6},{1... | collective-permute-start | bytes 294920 | tf_op jit(solution)/shard_map/ppermute | solution.py:346
  125.3 28.7 %collective-permute-start.23 = (bf16[48,8,128]{2,1,0:T(8,128)(2,1)}, bf16[48,8,128]{2,1,0:T(8,128)(2,1)S(1)}, u32[]{:S(2)}, u32[]{:S(2)}) collective-permute-start(bf16[48,8,128]{2,1,0:T(8,128)(2,1)} %get-tuple-element.87), channel_id=1, source_target_pairs={{0,4},{1,5},{2,6},{3,7},{4,8},{5,9},{6,10},{7,11},{8,12},{9,13},{1... | collective-permute-start | bytes 294920 | tf_op jit(solution)/shard_map/ppermute | solution.py:346
  127.0 29.0 %collective-permute-start.24 = (bf16[48,8,128]{2,1,0:T(8,128)(2,1)}, bf16[48,8,128]{2,1,0:T(8,128)(2,1)S(1)}, u32[]{:S(2)}, u32[]{:S(2)}) collective-permute-start(bf16[48,8,128]{2,1,0:T(8,128)(2,1)} %get-tuple-element.88), channel_id=1, source_target_pairs={{0,5},{1,4},{2,7},{3,6},{4,9},{5,8},{6,11},{7,10},{8,13},{9,12},{1... | collective-permute-start | bytes 294920 | tf_op jit(solution)/shard_map/ppermute | solution.py:346
  140.8 16.1 %collective-permute-start.25 = (bf16[48,8,128]{2,1,0:T(8,128)(2,1)}, bf16[48,8,128]{2,1,0:T(8,128)(2,1)S(1)}, u32[]{:S(2)}, u32[]{:S(2)}) collective-permute-start(bf16[48,8,128]{2,1,0:T(8,128)(2,1)} %get-tuple-element.89), channel_id=1, source_target_pairs={{0,6},{1,7},{2,4},{3,5},{4,10},{5,11},{6,8},{7,9},{8,14},{9,15},{1... | collective-permute-start | bytes 294920 | tf_op jit(solution)/shard_map/ppermute | solution.py:346
  141.3 17.7 %collective-permute-start.26 = (bf16[48,8,128]{2,1,0:T(8,128)(2,1)}, bf16[48,8,128]{2,1,0:T(8,128)(2,1)S(1)}, u32[]{:S(2)}, u32[]{:S(2)}) collective-permute-start(bf16[48,8,128]{2,1,0:T(8,128)(2,1)} %get-tuple-element.90), channel_id=1, source_target_pairs={{0,7},{1,6},{2,5},{3,4},{4,11},{5,10},{6,9},{7,8},{8,15},{9,14},{1... | collective-permute-start | bytes 294920 | tf_op jit(solution)/shard_map/ppermute | solution.py:346
  153.8 30.0 %collective-permute-start.17 = (f32[3,64,256]{2,1,0:T(8,128)S(1)}, f32[3,64,256]{2,1,0:T(8,128)S(1)}, u32[]{:S(2)}, u32[]{:S(2)}) collective-permute-start(f32[3,64,256]{2,1,0:T(8,128)S(1)} %get-tuple-element.79), channel_id=1, source_target_pairs={{3,0},{0,1},{1,4},{4,5},{5,8},{8,9},{9,12},{12,13},{13,14},{14,15}... | collective-permute-start | bytes 589832 | tf_op jit(solution)/shard_map/ppermute | solution.py:367
  154.1 12.7 %collective-permute-start.21 = (bf16[48,8,128]{2,1,0:T(8,128)(2,1)S(1)}, bf16[48,8,128]{2,1,0:T(8,128)(2,1)S(1)}, u32[]{:S(2)}, u32[]{:S(2)}) collective-permute-start(bf16[48,8,128]{2,1,0:T(8,128)(2,1)S(1)} %copy-done.21), channel_id=1, source_target_pairs={{0,8},{1,9},{2,10},{3,11},{4,12},{5,13},{6,14},{7,15},{8,0},{9,1},... | collective-permute-start | bytes 294920 | tf_op jit(solution)/shard_map/ppermute | solution.py:346
  156.0 13.3 %collective-permute-start.22 = (bf16[48,8,128]{2,1,0:T(8,128)(2,1)S(1)}, bf16[48,8,128]{2,1,0:T(8,128)(2,1)S(1)}, u32[]{:S(2)}, u32[]{:S(2)}) collective-permute-start(bf16[48,8,128]{2,1,0:T(8,128)(2,1)S(1)} %copy-done.20), channel_id=1, source_target_pairs={{0,9},{1,8},{2,11},{3,10},{4,13},{5,12},{6,15},{7,14},{8,1},{9,0},... | collective-permute-start | bytes 294920 | tf_op jit(solution)/shard_map/ppermute | solution.py:346
  156.9 17.9 %collective-permute-start.19 = (bf16[48,8,128]{2,1,0:T(8,128)(2,1)S(1)}, bf16[48,8,128]{2,1,0:T(8,128)(2,1)S(1)}, u32[]{:S(2)}, u32[]{:S(2)}) collective-permute-start(bf16[48,8,128]{2,1,0:T(8,128)(2,1)S(1)} %copy-done.19), channel_id=1, source_target_pairs={{0,10},{1,11},{2,8},{3,9},{4,14},{5,15},{6,12},{7,13},{8,2},{9,3},... | collective-permute-start | bytes 294920 | tf_op jit(solution)/shard_map/ppermute | solution.py:346
  159.0 18.3 %collective-permute-start.20 = (bf16[48,8,128]{2,1,0:T(8,128)(2,1)S(1)}, bf16[48,8,128]{2,1,0:T(8,128)(2,1)S(1)}, u32[]{:S(2)}, u32[]{:S(2)}) collective-permute-start(bf16[48,8,128]{2,1,0:T(8,128)(2,1)S(1)} %copy-done.18), channel_id=1, source_target_pairs={{0,11},{1,10},{2,9},{3,8},{4,15},{5,14},{6,13},{7,12},{8,3},{9,2},... | collective-permute-start | bytes 294920 | tf_op jit(solution)/shard_map/ppermute | solution.py:346
  166.7 17.0 %collective-permute-start = (f32[4,64,256]{2,1,0:T(8,128)S(1)}, f32[4,64,256]{2,1,0:T(8,128)S(1)}, u32[]{:S(2)}, u32[]{:S(2)}) collective-permute-start(f32[4,64,256]{2,1,0:T(8,128)S(1)} %get-tuple-element.57), channel_id=1, source_target_pairs={{3,0},{0,1},{1,4},{4,5},{5,8},{8,9},{9,12},{12,13},{13,14},{14,15}... | collective-permute-start | bytes 786440 | tf_op jit(solution)/shard_map/ppermute | solution.py:367
  169.4 14.4 %collective-permute-start.1 = (f32[4,64,256]{2,1,0:T(8,128)S(1)}, f32[4,64,256]{2,1,0:T(8,128)S(1)}, u32[]{:S(2)}, u32[]{:S(2)}) collective-permute-start(f32[4,64,256]{2,1,0:T(8,128)S(1)} %get-tuple-element.58), channel_id=1, source_target_pairs={{0,3},{1,0},{4,1},{5,4},{8,5},{9,8},{12,9},{13,12},{14,13},{15,14}... | collective-permute-start | bytes 786440 | tf_op jit(solution)/shard_map/ppermute | solution.py:366
  174.8 9.0 %collective-permute-start.18 = (f32[3,64,256]{2,1,0:T(8,128)S(1)}, f32[3,64,256]{2,1,0:T(8,128)S(1)}, u32[]{:S(2)}, u32[]{:S(2)}) collective-permute-start(f32[3,64,256]{2,1,0:T(8,128)S(1)} %get-tuple-element.80), channel_id=1, source_target_pairs={{0,3},{1,0},{4,1},{5,4},{8,5},{9,8},{12,9},{13,12},{14,13},{15,14}... | collective-permute-start | bytes 589832 | tf_op jit(solution)/shard_map/ppermute | solution.py:366
  (27 other events, 335.0 us)
